TPU v7x, 32 devices: a whole 2x2x4 slice. The times are simulated.
32 devices in a mesh: dp: 8 (over y, x, core), seq: 4 (over z).
Axes of the slice: x: 2, y: 2, z: 4, core: 2. Of those that a mesh axis runs over, the one named last changes fastest.
Arguments:
- layer_input: bfloat16 [8, 512, 768], P('dp', 'seq')
- w_qkv: bfloat16 [768, 2304], P('dp'), may hold values from -0.21875 to 0.21875
- w_out: bfloat16 [768, 768], P('dp'), may hold values from -0.875 to 0.875
- ln1_gain: bfloat16 [768], P('dp'), may hold values from 0.5 to 1.5
- ln1_bias: bfloat16 [768], P('dp'), may hold values from -1 to 1
- w_gate_up: bfloat16 [768, 6144], P('dp'), may hold values from -0.21875 to 0.21875
- w_down: bfloat16 [3072, 768], P('dp'), may hold values from -0.15625 to 0.15625
- ln2_gain: bfloat16 [768], P('dp'), may hold values from 0.5 to 1.5
- ln2_bias: bfloat16 [768], P('dp'), may hold values from -1 to 1
- doc_starts: int32 [8, 8], P('dp'), may hold values from 0 to 511, as said below
- cotangent: bfloat16 [8, 512, 768], P('dp', 'seq'), may hold values from -6 to 6
Outputs:
- output: bfloat16 [8, 512, 768], P('dp', 'seq')
- input_grad: bfloat16 [8, 512, 768], P('dp', 'seq')
- w_qkv_grad: float32 [768, 2304], P('dp')
- w_out_grad: float32 [768, 768], P('dp')
- ln1_gain_grad: float32 [768], P('dp')
- ln1_bias_grad: float32 [768], P('dp')
- w_gate_up_grad: float32 [768, 6144], P('dp')
- w_down_grad: float32 [3072, 768], P('dp')
- ln2_gain_grad: float32 [768], P('dp')
- ln2_bias_grad: float32 [768], P('dp')
- root_means: float32 [8, 4], P('dp')
Inputs may be any that keep to these rules, and one draw needn't show every extreme that they name: `doc_starts`: row b holds the first positions of the 8 documents of window b: 0 first, strictly rising, each below 512; a document runs to the next start or to the window's end. In the last window the last document begins at 511.
All inputs are finite; a program needn't handle non-finite values.
Results may differ from a plain program's by a relative error of at most 0.015.
Values may be sent and summed in bfloat16 or wider, within the bound.
No kernel may reach another device: no remote copies, remote signals or barrier semaphores. Data moves between devices by JAX's collectives and lax.ppermute only.
A program may use at most 128 MiB of HBM per device.

v0:
```python
import math

import jax
import jax.numpy as jnp
import numpy as np
from jax import lax
from jax.experimental import pallas as pl
from jax.experimental.pallas import tpu as pltpu
from jax.sharding import PartitionSpec as P

HEADS = 12
HEAD_DIM = 64
NORM_EPSILON = 1e-05
GELU_C = 0.7978845608028654
GELU_A = 0.044715
INNER = 8
CHIPS = 4
SEQ = 4
PAD = 16

F32 = jnp.float32
BF16 = jnp.bfloat16
SLOPES = (2.0 ** (-8.0 * (np.arange(HEADS) + 1.0) / HEADS)).astype(np.float32)


def dot(left, right):
    return jnp.dot(left, right, preferred_element_type=F32)


def dot_nt(left, right):
    return lax.dot_general(left, right, (((1,), (1,)), ((), ())), preferred_element_type=F32)


def dot_tn(left, right):
    return lax.dot_general(left, right, (((0,), (0,)), ((), ())), preferred_element_type=F32)


def gelu_parts(value):
    square = value * value
    tanh = jnp.tanh(GELU_C * (value + GELU_A * square * value))
    half = 0.5 * (1.0 + tanh)
    slope = half + 0.5 * value * (1.0 - tanh * tanh) * (GELU_C * (1.0 + 3.0 * GELU_A * square))
    return value * half, slope


def gelu(value):
    return 0.5 * value * (1.0 + jnp.tanh(GELU_C * (value + GELU_A * value * value * value)))


def norm_parts(summed):
    centered = summed - jnp.mean(summed, axis=-1, keepdims=True)
    variance = jnp.mean(centered * centered, axis=-1, keepdims=True)
    inv_std = lax.rsqrt(variance + NORM_EPSILON)
    return centered * inv_std, inv_std


def norm_back(grad_in, normalized, inv_std, gain):
    scaled = grad_in * gain
    return inv_std * (
        scaled
        - jnp.mean(scaled, axis=-1, keepdims=True)
        - normalized * jnp.mean(scaled * normalized, axis=-1, keepdims=True)
    )


def column_sum(value):
    return jnp.sum(value, axis=0, keepdims=True)


def total(value):
    return jnp.sum(jnp.sum(value, axis=1, keepdims=True), axis=0, keepdims=True)


def at(start, size, step):
    return pl.ds(pl.multiple_of(start, step), size)


def call(kernel, outs, smem, *vmem, scratch=(), flops=0, mib=8, aliases=None):
    specs = [pl.BlockSpec(memory_space=pltpu.SMEM) for _ in smem]
    specs += [pl.BlockSpec(memory_space=pltpu.VMEM) for _ in vmem]
    out_shape = [jax.ShapeDtypeStruct(shape, dtype) for shape, dtype in outs]
    moved = sum(math.prod(a.shape) * a.dtype.itemsize for a in list(vmem) + out_shape)
    return pl.pallas_call(
        kernel,
        out_shape=out_shape,
        in_specs=specs,
        out_specs=[pl.BlockSpec(memory_space=pltpu.VMEM) for _ in outs],
        scratch_shapes=[pltpu.VMEM(shape, dtype) for shape, dtype in scratch],
        input_output_aliases=aliases or {},
        cost_estimate=pl.CostEstimate(flops=flops, transcendentals=0, bytes_accessed=moved),
        name=kernel.__name__,
        compiler_params=pltpu.CompilerParams(vmem_limit_bytes=mib << 20),
    )(*smem, *vmem)


def select_units(ids, gate_up, down, w_out, params, piece):
    z = ids[8]
    rows = w_out.shape[0]
    window = down.shape[0]
    units = window // SEQ
    model = w_out.shape[1]
    hidden = gate_up.shape[1] // 2
    group = lax.broadcasted_iota(jnp.int32, (rows, window), 1) // units
    for g in range(2):
        for w in range(model // window):
            acc = jnp.zeros((rows, window), F32)
            for i in range(SEQ):
                start = g * hidden + (SEQ * w + i) * window
                shift = lax.rem(units * (i - z) + window, window)
                moved = pltpu.roll(gate_up[:, start : start + window].astype(F32), shift, 1)
                acc = jnp.where(group == i, moved, acc)
            piece[g * rows : (g + 1) * rows, w * window : (w + 1) * window] = acc.astype(BF16)
    piece[2 * rows : 3 * rows, :] = down[at(z * units, units, 32), :]
    piece[3 * rows : 4 * rows, :] = w_out[...]
    piece[4 * rows :, :] = params[...]


def gather_weights(ids, *refs):
    blocks, odd = refs[0:4], refs[4]
    gate_up, down, w_out, vectors = refs[5:9]
    model = w_out.shape[0]
    rows = model // INNER
    size = blocks[0].shape[0]
    gathered = jnp.zeros((8, model), F32)
    for t in range(CHIPS):
        for s in range(2):
            start = ids[2 * t + s] * rows
            place = at(start, rows, 32)
            block = blocks[t] if s == 0 else odd.at[t * size : (t + 1) * size]
            gate_up[0, place, :] = block[0:rows, :]
            gate_up[1, place, :] = block[rows : 2 * rows, :]
            down[place, :] = block[2 * rows : 3 * rows, :]
            w_out[place, :] = block[3 * rows : 4 * rows, :]
            piece = block[4 * rows : 4 * rows + PAD, :].astype(F32)
            gathered = gathered + pltpu.roll(piece, start, 1)[0:8]
    vectors[...] = gathered


def attention_forward(ids, starts, slopes, *refs):
    x_blocks, w_blocks, odd = refs[0:4], refs[4:8], refs[8]
    packed, q_out, k_out, v_out, probs_out, w_qkv = refs[9:15]
    xs, attended = refs[15:17]
    rows = x_blocks[0].shape[0]
    length = SEQ * rows
    model = w_qkv.shape[1]
    width = w_qkv.shape[2]
    shard = model // INNER
    for t in range(CHIPS):
        for s in range(2):
            place = at(ids[2 * t + s] * shard, shard, 32)
            block = w_blocks[t] if s == 0 else odd.at[t * shard : (t + 1) * shard]
            for part in range(3):
                w_qkv[part, place, :] = block[:, part * width : (part + 1) * width]
    for s in range(SEQ):
        xs[s * rows : (s + 1) * rows, :] = x_blocks[s][...]
    joint = xs[...]
    q_out[...] = dot(joint, w_qkv[0]).astype(BF16)
    k_out[...] = dot(joint, w_qkv[1]).astype(BF16)
    v_out[...] = dot(joint, w_qkv[2]).astype(BF16)
    keys = k_out[...]
    values = v_out[...]
    heads = width // HEAD_DIM
    z = ids[8]

    def doc_of(position):
        count = jnp.zeros(position.shape, jnp.int32)
        for n in range(starts.shape[1]):
            count = count + (starts[0, n] <= position).astype(jnp.int32)
        return count

    lane = lax.broadcasted_iota(jnp.int32, (1, length), 1)
    key_pos = (jnp.bitwise_xor(lane // rows, z)) * rows + lane % rows
    key_docs = doc_of(key_pos)
    head_of = lax.broadcasted_iota(jnp.int32, (1, width), 1) // HEAD_DIM
    head_values = [jnp.where(head_of == h, values, jnp.zeros_like(values)) for h in range(heads)]

    def one_block(s, carry):
        place = at(s * rows, rows, 128)
        query_pos = ids[8 + s] * rows + lax.broadcasted_iota(jnp.int32, (rows, 1), 0)
        distance = jnp.abs(query_pos - key_pos).astype(F32)
        same_doc = doc_of(query_pos) == key_docs
        block = q_out[place, :] * BF16(1.0 / math.sqrt(HEAD_DIM))
        total_out = jnp.zeros((rows, width), F32)
        for h in range(heads):
            query = jnp.where(head_of == h, block, jnp.zeros_like(block))
            scores = dot_nt(query, keys) - slopes[z * heads + h] * distance
            scores = jnp.where(same_doc, scores, -1e30)
            expon = jnp.exp(scores - jnp.max(scores, axis=-1, keepdims=True))
            probs = (expon / jnp.sum(expon, axis=-1, keepdims=True)).astype(BF16)
            probs_out[h, place, :] = probs
            total_out = total_out + dot(probs, head_values[h])
        attended[place, :] = total_out.astype(BF16)
        return carry

    lax.fori_loop(0, SEQ, one_block, 0)
    half = length // 2
    packed[0:length, :] = attended[:, 0:128]
    packed[length:, 0:64] = attended[0:half, 128:192]
    packed[length:, 64:128] = attended[half:, 128:192]


def middle_forward(ids, *refs):
    packs, x_blocks = refs[0:4], refs[4:8]
    w_out, vectors, gate_up, down = refs[8:12]
    outs = refs[12:16]
    first_ref, normed_ref, stats_ref, attn = refs[16:20]
    acc = refs[20]
    rows = x_blocks[0].shape[0]
    length = SEQ * rows
    width = attn.shape[2]
    for t in range(SEQ):
        for u in range(SEQ):
            place = slice(u * rows, (u + 1) * rows)
            b = t ^ u
            attn[t, place, 0:128] = packs[t][b * rows : (b + 1) * rows, :]
            start = length + (b % 2) * rows
            attn[t, place, 128:192] = packs[t][start : start + rows, (b // 2) * 64 : (b // 2) * 64 + 64]
    w_parts = [w_out[at(ids[8 + t] * width, width, 64), :] for t in range(SEQ)]
    for u in range(SEQ):
        place = slice(u * rows, (u + 1) * rows)
        branch = dot(attn[0, place, :], w_parts[0])
        for t in range(1, SEQ):
            branch = branch + dot(attn[t, place, :], w_parts[t])
        first_sum = x_blocks[u][...].astype(F32) + branch
        normalized, _ = norm_parts(first_sum)
        normed_ref[place, :] = (normalized * vectors[0:1, :] + vectors[1:2, :]).astype(BF16)
        if u == 0:
            first_ref[...] = first_sum
            lane = lax.broadcasted_iota(jnp.int32, stats_ref.shape, 1)
            stats_ref[...] = jnp.where(lane == 0, total(branch * branch), 0.0) + jnp.where(
                lane == 1, total(first_sum * first_sum), 0.0
            )
    normed = normed_ref[...]
    step = 256
    for start in range(0, down.shape[0], step):
        cols = slice(start, start + step)
        gate = dot(normed, gate_up[0, :, cols])
        up = dot(normed, gate_up[1, :, cols])
        hidden = (gelu(gate) * up).astype(BF16)
        part = dot(hidden, down[cols, :])
        if start == 0:
            acc[...] = part
        else:
            acc[...] += part
    for s in range(SEQ):
        outs[s][...] = acc[s * rows : (s + 1) * rows, :].astype(outs[s].dtype)


def final_norm(*refs):
    parts = refs[0:4]
    normed_ref, cot_ref, vectors, stats_in = refs[4:8]
    out_ref, grad_feed_ref, grad_second_ref, sums_ref, stats_ref = refs[8:13]
    feed_out = parts[0][...]
    for s in range(1, CHIPS):
        feed_out = feed_out + parts[s][...].astype(F32)
    second = normed_ref[0 : cot_ref.shape[0], :].astype(F32) + feed_out
    normalized, inv_std = norm_parts(second)
    gain = vectors[2:3, :]
    out_ref[...] = (normalized * gain + vectors[3:4, :]).astype(BF16)
    grad = cot_ref[...].astype(F32)
    grad_second = norm_back(grad, normalized, inv_std, gain)
    grad_second_ref[...] = grad_second
    grad_feed_ref[...] = grad_second.astype(BF16)
    sums_ref[0:1, :] = column_sum(grad * normalized)
    sums_ref[1:2, :] = column_sum(grad)
    sums_ref[2:8, :] = jnp.zeros((6, gain.shape[1]), F32)
    lane = lax.broadcasted_iota(jnp.int32, stats_ref.shape, 1)
    stats_ref[...] = (
        stats_in[...]
        + jnp.where(lane == 2, total(feed_out * feed_out), 0.0)
        + jnp.where(lane == 3, total(second * second), 0.0)
    )


def feed_back(*refs):
    normed_ref, grad_blocks = refs[0], refs[1:5]
    gate_up, down = refs[5:7]
    outs = refs[7:11]
    hidden_ref, dgate_ref, dup_ref, grads = refs[11:15]
    acc = refs[15]
    rows = grad_blocks[0].shape[0]
    for s in range(SEQ):
        grads[s * rows : (s + 1) * rows, :] = grad_blocks[s][...]
    normed = normed_ref[...]
    grad_feed = grads[...]
    step = 256
    for start in range(0, down.shape[0], step):
        cols = slice(start, start + step)
        gate = dot(normed, gate_up[0, :, cols])
        up = dot(normed, gate_up[1, :, cols])
        grad_hidden = dot_nt(grad_feed, down[cols, :])
        act, slope = gelu_parts(gate)
        hidden_ref[:, cols] = (act * up).astype(BF16)
        dgate = (grad_hidden * up * slope).astype(BF16)
        dup = (grad_hidden * act).astype(BF16)
        dgate_ref[:, cols] = dgate
        dup_ref[:, cols] = dup
        part = dot_nt(dgate, gate_up[0, :, cols]) + dot_nt(dup, gate_up[1, :, cols])
        if start == 0:
            acc[...] = part
        else:
            acc[...] += part
    for s in range(SEQ):
        outs[s][...] = acc[s * rows : (s + 1) * rows, :].astype(outs[s].dtype)


def split_rows(ids, acc, keep, send, where):
    shard = acc.shape[0] // INNER
    for t in range(CHIPS):
        keep[(t,) + where] = acc[at(ids[2 * t] * shard, shard, 32), :]
        send[(t,) + where] = acc[at(ids[2 * t + 1] * shard, shard, 32), :].astype(BF16)


def feed_weights(ids, *refs):
    normed, grads, hidden, dgate, dup = refs[0:5]
    keep, send = refs[5:7]
    acc = refs[7]
    for n, (left, right) in enumerate(((normed, dgate), (normed, dup), (hidden, grads))):
        acc[...] = dot_tn(left[...], right[...])
        split_rows(ids, acc, keep, send, (n,))


def pair_sum(*refs):
    keep, received = refs[0:2]
    for t in range(CHIPS):
        refs[2 + t][...] = (keep[t] + received[t].astype(F32)).astype(refs[2 + t].dtype)


def plane_sum(*refs):
    out = refs[-1]
    acc = refs[0][...].astype(F32)
    for ref in refs[1:-1]:
        acc = acc + ref[...].astype(F32)
    out[...] = acc.astype(out.dtype)


def feed_final(ids, *refs):
    blocks, out, down_out = refs[0:4], refs[4], refs[5]
    rows, model = blocks[0].shape[1:]
    hidden = out.shape[1] // 2
    window = hidden // INNER
    units = window // SEQ
    group = lax.broadcasted_iota(jnp.int32, (rows, window), 1) // units
    for g in range(2):
        for w in range(model // window):
            parts = [b[g, :, w * window : (w + 1) * window].astype(F32) for b in blocks]
            for i in range(SEQ):
                acc = jnp.zeros((rows, window), F32)
                for s in range(SEQ):
                    pos = ids[8 + s]
                    shift = lax.rem(units * (pos - i) + window, window)
                    acc = jnp.where(group == pos, pltpu.roll(parts[s], shift, 1), acc)
                start = g * hidden + (SEQ * w + i) * window
                out[:, start : start + window] = acc
    for s in range(SEQ):
        down_out[at(ids[8 + s] * units, units, 32), :] = blocks[s][2].astype(F32)


def project_back(ids, *refs):
    parts = refs[0:4]
    grad_second, first_ref, vectors, w_out = refs[4:8]
    sums_in, stats_ref = refs[8:10]
    grad_first_ref = refs[10]
    grad_outs, sums_ref = refs[11:15], refs[15]
    grad = grad_second[...] + parts[0][...]
    for s in range(1, SEQ):
        grad = grad + parts[s][...].astype(F32)
    normalized, inv_std = norm_parts(first_ref[...])
    grad_first = norm_back(grad, normalized, inv_std, vectors[0:1, :])
    grad_first_ref[...] = grad_first
    grad_branch = grad_first.astype(BF16)
    rows, model = grad_branch.shape
    width = grad_outs[0].shape[1] // 2
    high = stats_ref[...].astype(BF16)
    low = (stats_ref[...] - high.astype(F32)).astype(BF16)
    stats_rows = jnp.concatenate([high, low], axis=0)
    stats_rows = jnp.concatenate([stats_rows, jnp.zeros((PAD, 2 * width - 128), BF16)], axis=1)
    row = lax.broadcasted_iota(jnp.int32, (model, width), 0)
    column = lax.broadcasted_iota(jnp.int32, (model, width), 1)
    for s in range(SEQ):
        start = ids[8 + s] * width
        mine = w_out[at(start, width, 64), :]
        grad_outs[s][0:rows, 0:width] = dot_nt(grad_branch, mine).astype(BF16)
        grad_outs[s][rows : rows + PAD, :] = stats_rows
        chosen = (row == start + column).astype(F32).astype(BF16)
        grad_outs[s][0:rows, width:] = dot(grad_branch, chosen).astype(BF16)
    sums_ref[0:1, :] = column_sum(grad * normalized)
    sums_ref[1:2, :] = column_sum(grad)
    sums_ref[2:4, :] = sums_in[0:2, :]
    sums_ref[4:PAD, :] = jnp.zeros((PAD - 4, model), F32)


def attention_back(*refs):
    grad_blocks = refs[0:4]
    q_ref, k_ref, v_ref, probs_ref, w_qkv = refs[4:9]
    outs, grad_qkv = refs[9:13], refs[13]
    grads, grad_q, grad_k, grad_v = refs[14:18]
    rows = outs[0].shape[0]
    for s in range(SEQ):
        place = slice(s * rows, (s + 1) * rows)
        grads[place, :] = grad_blocks[s][0:rows, 0 : grads.shape[1]]
    queries, keys, values = q_ref[...], k_ref[...], v_ref[...]
    width = keys.shape[1]
    heads = width // HEAD_DIM
    head_of = lax.broadcasted_iota(jnp.int32, (1, width), 1) // HEAD_DIM
    scale = 1.0 / math.sqrt(HEAD_DIM)
    for h in range(heads):
        mine = head_of == h
        head_keys = jnp.where(mine, keys, jnp.zeros_like(keys))
        for s in range(SEQ):
            place = slice(s * rows, (s + 1) * rows)
            grad_out = jnp.where(mine, grads[place, :], jnp.zeros((rows, width), BF16))
            query = jnp.where(mine, queries[place, :], jnp.zeros((rows, width), BF16))
            probs_low = probs_ref[h, place, :]
            probs = probs_low.astype(F32)
            grad_probs = dot_nt(grad_out, values)
            delta = jnp.sum(probs * grad_probs, axis=-1, keepdims=True)
            grad_scores = (probs * (grad_probs - delta)).astype(BF16)
            dq = dot(grad_scores, head_keys)
            dk = dot_tn(grad_scores, query)
            dv = dot_tn(probs_low, grad_out)
            if h == 0:
                grad_q[place, :] = dq
            else:
                grad_q[place, :] += dq
            if h == 0 and s == 0:
                grad_k[...] = dk
                grad_v[...] = dv
            else:
                grad_k[...] += dk
                grad_v[...] += dv
    low = (
        (grad_q[...] * scale).astype(BF16),
        (grad_k[...] * scale).astype(BF16),
        grad_v[...].astype(BF16),
    )
    grad_input = dot_nt(low[0], w_qkv[0]) + dot_nt(low[1], w_qkv[1]) + dot_nt(low[2], w_qkv[2])
    for s in range(SEQ):
        outs[s][...] = grad_input[s * rows : (s + 1) * rows, :].astype(outs[s].dtype)
    for part in range(3):
        grad_qkv[:, part * width : (part + 1) * width] = low[part]


def attention_weights(ids, *refs):
    grad_qkv, x_blocks, attn, columns = refs[0], refs[1:5], refs[5], refs[6:10]
    sums = refs[10]
    keep, send = refs[11:13]
    xs, grads, out_acc, acc = refs[13:17]
    rows = x_blocks[0].shape[0]
    width = grads.shape[1]
    for s in range(SEQ):
        place = slice(s * rows, (s + 1) * rows)
        xs[place, :] = x_blocks[s][...]
        grads[place, :] = columns[s][0:rows, width:]
    for t in range(SEQ):
        out_acc[at(ids[8 + t] * width, width, 64), :] = dot_tn(attn[t], grads[...])
    acc[:, 0 : 3 * width] = dot_tn(xs[...], grad_qkv[...])
    acc[:, 3 * width : 4 * width] = out_acc[...]
    shard = acc.shape[0] // INNER
    split_rows(ids, acc, keep, send, (slice(0, shard),))
    for t in range(CHIPS):
        keep[t, shard : shard + PAD, :] = sums[...]
        send[t, shard : shard + PAD, :] = sums[...].astype(BF16)


def input_final(*refs):
    grad_first, parts, stats_in, grad_blocks = refs[0], refs[1:5], refs[5], refs[6:9]
    out, means = refs[9:11]
    acc = grad_first[...] + parts[0][...]
    for s in range(1, SEQ):
        acc = acc + parts[s][...].astype(F32)
    out[...] = acc.astype(BF16)
    rows, model = out.shape
    stats = stats_in[...]
    for ref in grad_blocks:
        extra = ref[rows : rows + PAD, 0:128].astype(F32)
        stats = stats + (extra[0:8] + extra[8:16])
    means[...] = jnp.sqrt(stats * (1.0 / (SEQ * rows * model)))


def attention_final(ids, *refs):
    blocks, qkv_out, out, vectors, stage = refs[0:4], refs[4], refs[5], refs[6], refs[7]
    for s in range(SEQ):
        stage[ids[8 + s]] = blocks[s][...].astype(F32)
    shard, model = out.shape
    width = model // SEQ
    for pos in range(SEQ):
        for part in range(3):
            start = (part * SEQ + pos) * width
            qkv_out[:, start : start + width] = stage[pos, 0:shard, part * width : (part + 1) * width]
        out[:, pos * width : (pos + 1) * width] = stage[pos, 0:shard, 3 * width : 4 * width]
    sums = stage[0, shard : shard + 8, :]
    for pos in range(1, SEQ):
        sums = sums + stage[pos, shard : shard + 8, :]
    shift = model - ids[0] * shard
    vectors[...] = pltpu.roll(sums, lax.rem(shift, model), 1)[:, 0:128]


def after(values, *deps):
    return lax.optimization_barrier((values, deps))[0]


def body(
    layer_input,
    w_qkv,
    w_out,
    ln1_gain,
    ln1_bias,
    w_gate_up,
    w_down,
    ln2_gain,
    ln2_bias,
    doc_starts,
    cotangent,
):
    dp = lax.axis_size("dp")
    stride = dp // INNER
    rows, model = layer_input.shape[1:]
    columns = tuple(tuple(range(g * stride, (g + 1) * stride)) for g in range(INNER))
    cores = tuple(
        tuple((2 * t + core) * stride + r for t in range(CHIPS))
        for core in range(2)
        for r in range(stride)
    )

    def gather_outer(value):
        if stride == 1:
            return value
        return lax.all_gather(value, "dp", axis=0, tiled=True, axis_index_groups=columns)

    def scatter_outer(value):
        if stride == 1:
            return value
        return lax.psum_scatter(
            value, "dp", scatter_dimension=0, tiled=True, axis_index_groups=columns
        )

    def swap(value, s):
        return lax.ppermute(value, "dp", [(i, i ^ (s * stride)) for i in range(dp)])

    def pass_seq(value, s):
        return lax.ppermute(value, "seq", [(i, i ^ s) for i in range(SEQ)])

    def gather_seq(value):
        far = pass_seq(value, 2)
        near = pass_seq(value, 1)
        return [value, near, far, pass_seq(far, 1)]

    def reduce_seq(pieces):
        return [pieces[0]] + [pass_seq(pieces[s], s) for s in range(1, SEQ)]

    j = lax.axis_index("dp") // stride
    z = lax.axis_index("seq")
    ids = jnp.concatenate(
        [
            jnp.bitwise_xor(j, jnp.arange(INNER, dtype=jnp.int32)),
            jnp.bitwise_xor(z, jnp.arange(SEQ, dtype=jnp.int32)),
        ]
    )
    slopes = jnp.asarray(SLOPES)

    w_qkv, w_out, w_gate_up, w_down = map(gather_outer, (w_qkv, w_out, w_gate_up, w_down))
    vectors = [gather_outer(v) for v in (ln1_gain, ln1_bias, ln2_gain, ln2_bias)]
    shard = w_out.shape[0]
    head_width = HEADS // SEQ * HEAD_DIM

    x_own = layer_input[0]
    x_blocks = gather_seq(x_own)

    own_qkv = jnp.concatenate(
        [
            lax.dynamic_slice(w_qkv, (0, part * model + z * head_width), (shard, head_width))
            for part in range(3)
        ],
        axis=1,
    )
    qkv_even = [own_qkv] + [swap(own_qkv, s) for s in (2, 4, 6)]
    qkv_odd = swap(jnp.concatenate(qkv_even, axis=0), 1)

    params = jnp.pad(jnp.stack(vectors, axis=0), ((0, PAD - 4), (0, model - shard)))
    (piece,) = call(
        select_units,
        [((4 * shard + PAD, model), BF16)],
        [ids],
        w_gate_up,
        w_down,
        w_out,
        params,
        mib=8,
    )
    piece = after(piece, qkv_even, x_blocks[1:3])
    feed_even = [piece] + [swap(piece, s) for s in (2, 4, 6)]

    length = SEQ * rows
    packed, queries, keys, values, probs, qkv_full = call(
        attention_forward,
        [((length * 3 // 2, 128), BF16)]
        + [((length, head_width), BF16)] * 3
        + [((HEADS // SEQ, length, length), BF16), ((3, model, head_width), BF16)],
        [ids, doc_starts, slopes],
        *x_blocks,
        *qkv_even,
        qkv_odd,
        scratch=[((length, model), BF16), ((length, head_width), BF16)],
        mib=16,
        flops=2 * length * head_width * (3 * model + 2 * length),
    )
    packs = gather_seq(packed)

    feed_even = after(feed_even, packs[1:3])
    feed_odd = swap(jnp.concatenate(feed_even, axis=0), 1)
    units = w_down.shape[0] // SEQ * INNER
    gate_up_full, down_full, out_full, norm_vectors = call(
        gather_weights,
        [
            ((2, model, units), BF16),
            ((units, model), BF16),
            ((model, model), BF16),
            ((8, model), F32),
        ],
        [ids],
        *feed_even,
        feed_odd,
        mib=16,
    )

    shares = [((rows, model), F32)] + [((rows, model), BF16)] * 3
    *feed_parts, first_sum, normed, stats1, attn = call(
        middle_forward,
        shares
        + [
            ((rows, model), F32),
            ((length, model), BF16),
            ((8, 128), F32),
            ((SEQ, length, head_width), BF16),
        ],
        [ids],
        *packs,
        *x_blocks,
        out_full,
        norm_vectors,
        gate_up_full,
        down_full,
        scratch=[((length, model), F32)],
        mib=16,
        flops=2 * length * model * (model + 3 * units),
    )

    output, grad_feed, grad_second, sums2, stats2 = call(
        final_norm,
        [
            ((rows, model), BF16),
            ((rows, model), BF16),
            ((rows, model), F32),
            ((8, model), F32),
            ((8, 128), F32),
        ],
        [],
        *reduce_seq(feed_parts),
        normed,
        cotangent[0],
        norm_vectors,
        stats1,
    )

    *back_parts, hidden, dgate, dup, grads = call(
        feed_back,
        shares + [((length, units), BF16)] * 3 + [((length, model), BF16)],
        [],
        normed,
        *gather_seq(grad_feed),
        gate_up_full,
        down_full,
        scratch=[((length, model), F32)],
        mib=18,
        flops=10 * length * model * units,
    )
    back_parts = reduce_seq(back_parts)

    feed_keep, feed_send = call(
        feed_weights,
        [((CHIPS, 3, shard, model), F32), ((CHIPS, 3, shard, model), BF16)],
        [ids],
        normed,
        grads,
        hidden,
        dgate,
        dup,
        scratch=[((model, model), F32)],
        mib=18,
        flops=6 * length * model * units,
    )

    def pair(keep, send):
        shape = keep.shape[1:]
        return call(pair_sum, [(shape, F32)] + [(shape, BF16)] * 3, [], keep, swap(send, 1))

    def reduce_plane(pieces):
        shape = pieces[0].shape
        pieces = [pieces[0]] + [swap(pieces[t], 2 * t) for t in range(1, CHIPS)]
        return call(plane_sum, [(shape, BF16)], [], *pieces)[0]

    feed_pieces = pair(feed_keep, feed_send)
    grad_second = after(grad_second, feed_pieces)
    feed_pieces = after(feed_pieces, back_parts)

    grad_first, *projected = call(
        project_back,
        [((rows, model), F32)]
        + [((rows + PAD, 2 * head_width), BF16)] * SEQ
        + [((PAD, model), F32)],
        [ids],
        *back_parts,
        grad_second,
        first_sum,
        norm_vectors,
        out_full,
        sums2,
        stats2,
        mib=10,
        flops=4 * rows * model * model,
    )
    grad_attn = reduce_seq(projected[0:4])
    sums = projected[4]
    feed_share = reduce_plane(feed_pieces)
    feed_blocks = gather_seq(after(feed_share, grad_attn))

    *input_parts, grad_qkv = call(
        attention_back,
        shares + [((length, 3 * head_width), BF16)],
        [],
        *grad_attn,
        queries,
        keys,
        values,
        probs,
        qkv_full,
        scratch=[((length, head_width), BF16)] + [((length, head_width), F32)] * 3,
        mib=16,
        flops=2 * length * head_width * (3 * model + 5 * length),
    )
    input_parts = reduce_seq(input_parts)

    sums = after(sums, feed_share)

    attn_keep, attn_send = call(
        attention_weights,
        [
            ((CHIPS, shard + PAD, model), F32),
            ((CHIPS, shard + PAD, model), BF16),
        ],
        [ids],
        grad_qkv,
        *x_blocks,
        attn,
        *grad_attn,
        sums,
        scratch=[
            ((length, model), BF16),
            ((length, head_width), BF16),
            ((model, head_width), F32),
            ((model, model), F32),
        ],
        mib=16,
        flops=2 * length * model * model,
    )

    grad_gate_up_w, grad_down_w = call(
        feed_final,
        [(w_gate_up.shape, F32), (w_down.shape, F32)],
        [ids],
        *feed_blocks,
        mib=10,
    )
    attn_pieces = after(pair(attn_keep, attn_send), input_parts)
    attn_share = after(reduce_plane(attn_pieces), feed_blocks[2])
    grad_qkv_w, grad_out_w, vector_grads = call(
        attention_final,
        [((shard, 3 * model), F32), ((shard, model), F32), ((8, 128), F32)],
        [ids],
        *gather_seq(attn_share),
        scratch=[((SEQ, shard + PAD, model), F32)],
    )

    input_grad, means = call(
        input_final,
        [((rows, model), BF16), ((8, 128), F32)],
        [],
        grad_first,
        *input_parts,
        stats2,
        *grad_attn[1:],
    )
    vector_grads = [scatter_outer(vector_grads[n, :shard]) for n in range(4)]
    return (
        output[None],
        input_grad[None],
        scatter_outer(grad_qkv_w),
        scatter_outer(grad_out_w),
        vector_grads[0],
        vector_grads[1],
        scatter_outer(grad_gate_up_w),
        scatter_outer(grad_down_w),
        vector_grads[2],
        vector_grads[3],
        means[0:1, 0:4],
    )


def solution(mesh):
    return jax.shard_map(
        body,
        mesh=mesh,
        in_specs=(
            P("dp", "seq", None),
            P("dp", None),
            P("dp", None),
            P("dp"),
            P("dp"),
            P("dp", None),
            P("dp", None),
            P("dp"),
            P("dp"),
            P("dp", None),
            P("dp", "seq", None),
        ),
        out_specs=(
            P("dp", "seq", None),
            P("dp", "seq", None),
            P("dp", None),
            P("dp", None),
            P("dp"),
            P("dp"),
            P("dp", None),
            P("dp", None),
            P("dp"),
            P("dp"),
            P("dp", None),
        ),
        check_vma=False,
    )
```

profile of v0, /device:TPU:0, one launch (start us, length us, event | category | flops | bytes accessed | tf_op | source)
XLA Modules:
  0.0 229.5 jit_solution(13747878401018584826)
XLA Ops:
  2.0 4.0 %collective-permute-start.5 = (bf16[96,576]{1,0:T(8,128)(2,1)S(1)}, bf16[96,576]{1,0:T(8,128)(2,1)S(1)}, u32[]{:S(2)}, u32[]{:S(2)}) collective-permute-start(bf16[96,576]{1,0:T(8,128)(2,1)S(1)} %pad_maximum_fusion.2.refs_4_), channel_id=1, source_target_pairs={{0,24},{4,28},{8,16},{12,20},{16,8},{20,12},{24,0},{28,4},{1,25},{... | collective-permute-start | bytes 331784 | tf_op jit(solution)/shard_map/ppermute | solution.py:539
  6.6 3.0 %collective-permute-start.1 = (bf16[128,768]{1,0:T(8,128)(2,1)}, bf16[128,768]{1,0:T(8,128)(2,1)S(1)}, u32[]{:S(2)}, u32[]{:S(2)}) collective-permute-start(bf16[128,768]{1,0:T(8,128)(2,1)} %bitcast.16), channel_id=1, source_target_pairs={{0,2},{1,3},{2,0},{3,1},{4,6},{5,7},{6,4},{7,5},{8,10},{9,11},{10,... | collective-permute-start | bytes 589832 | tf_op jit(solution)/shard_map/ppermute | solution.py:542
  15.6 2.6 %collective-permute-done.1.refs_2_.refs_6_.refs_3_ = bf16[128,768]{1,0:T(8,128)(2,1)S(1)} collective-permute-done((bf16[128,768]{1,0:T(8,128)(2,1)}, bf16[128,768]{1,0:T(8,128)(2,1)S(1)}, u32[]{:S(2)}, u32[]{:S(2)}) %collective-permute-start.1) | collective-permute-done | bytes 196640 | tf_op jit(solution)/shard_map/ppermute | solution.py:542
  18.4 2.5 %collective-permute-start.12 = (bf16[400,768]{1,0:T(8,128)(2,1)S(1)}, bf16[400,768]{1,0:T(8,128)(2,1)S(1)}, u32[]{:S(2)}, u32[]{:S(2)}) collective-permute-start(bf16[400,768]{1,0:T(8,128)(2,1)S(1)} %select_units.1.refs_0_), channel_id=1, source_target_pairs={{0,24},{4,28},{8,16},{12,20},{16,8},{20,12},{24,0},{28,4},{1,25},{... | collective-permute-start | bytes 1843208 | tf_op jit(solution)/shard_map/ppermute | solution.py:539
  23.4 4.2 %collective-permute-done.2.refs_3_.refs_7_.refs_4_ = bf16[128,768]{1,0:T(8,128)(2,1)S(1)} collective-permute-done((bf16[128,768]{1,0:T(8,128)(2,1)S(1)}, bf16[128,768]{1,0:T(8,128)(2,1)S(1)}, u32[]{:S(2)}, u32[]{:S(2)}) %collective-permute-start.2) | collective-permute-done | bytes 196640 | tf_op jit(solution)/shard_map/ppermute | solution.py:542
  27.6 6.4 %attention_forward.1 = (bf16[768,128]{1,0:T(8,128)(2,1)S(1)}, bf16[512,192]{1,0:T(8,128)(2,1)S(1)}, bf16[512,192]{1,0:T(8,128)(2,1)S(1)}, bf16[512,192]{1,0:T(8,...) custom-call(s32[12]{0:T(128)S(1)} %pad_add_fusion.ids, s32[1,8]{1,0:T(1,128)S(1)} %copy-done.5, ...), custom_call_target="tpu_custom_call" | custom-call | flops 654311424 | bytes 4915200 | tf_op jit(solution)/shard_map/attention_forward/pallas_call | solution.py:83
  38.1 6.2 %collective-permute-done.8.refs_2_ = bf16[768,128]{1,0:T(8,128)(2,1)S(1)} collective-permute-done((bf16[768,128]{1,0:T(8,128)(2,1)S(1)}, bf16[768,128]{1,0:T(8,128)(2,1)S(1)}, u32[]{:S(2)}, u32[]{:S(2)}) %collective-permute-start.8) | collective-permute-done | bytes 196640 | tf_op jit(solution)/shard_map/ppermute | solution.py:542
  49.5 2.8 %collective-permute-done.13.refs_4_ = bf16[1600,768]{1,0:T(8,128)(2,1)S(1)} collective-permute-done((bf16[1600,768]{1,0:T(8,128)(2,1)S(1)}, bf16[1600,768]{1,0:T(8,128)(2,1)S(1)}, u32[]{:S(2)}, u32[]{:S(2)}) %collective-permute-start.13) | collective-permute-done | bytes 2457632 | tf_op jit(solution)/shard_map/ppermute | solution.py:539
  55.0 4.2 %middle_forward.1 = (f32[128,768]{1,0:T(8,128)S(1)}, bf16[128,768]{1,0:T(8,128)(2,1)S(1)}, bf16[128,768]{1,0:T(8,128)(2,1)S(1)}, bf16[128,768]{1,0:T(8,128)(2,1)...) custom-call(s32[12]{0:T(128)S(1)} %pad_add_fusion.ids, ...), custom_call_target="tpu_custom_call" | custom-call | flops 2415919104 | bytes 9269248 | tf_op jit(solution)/shard_map/middle_forward/pallas_call | solution.py:83
  61.0 3.3 %collective-permute-start.15 = (bf16[128,768]{1,0:T(8,128)(2,1)S(1)}, bf16[128,768]{1,0:T(8,128)(2,1)S(1)}, u32[]{:S(2)}, u32[]{:S(2)}) collective-permute-start(bf16[128,768]{1,0:T(8,128)(2,1)S(1)} %get-tuple-element.101), channel_id=1, source_target_pairs={{0,2},{1,3},{2,0},{3,1},{4,6},{5,7},{6,4},{7,5},{8,10},{9,11},{10,... | collective-permute-start | bytes 589832 | tf_op jit(solution)/shard_map/ppermute | solution.py:542
  64.2 4.7 %collective-permute-done.14.refs_1_ = bf16[128,768]{1,0:T(8,128)(2,1)S(1)} collective-permute-done((bf16[128,768]{1,0:T(8,128)(2,1)S(1)}, bf16[128,768]{1,0:T(8,128)(2,1)S(1)}, u32[]{:S(2)}, u32[]{:S(2)}) %collective-permute-start.14) | collective-permute-done | bytes 196640 | tf_op jit(solution)/shard_map/ppermute | solution.py:542
  69.0 9.5 %collective-permute-done.15.refs_2_ = bf16[128,768]{1,0:T(8,128)(2,1)S(1)} collective-permute-done((bf16[128,768]{1,0:T(8,128)(2,1)S(1)}, bf16[128,768]{1,0:T(8,128)(2,1)S(1)}, u32[]{:S(2)}, u32[]{:S(2)}) %collective-permute-start.15) | collective-permute-done | bytes 196640 | tf_op jit(solution)/shard_map/ppermute | solution.py:542
  79.5 4.5 %collective-permute-start.18 = (bf16[128,768]{1,0:T(8,128)(2,1)S(1)}, bf16[128,768]{1,0:T(8,128)(2,1)S(1)}, u32[]{:S(2)}, u32[]{:S(2)}) collective-permute-start(bf16[128,768]{1,0:T(8,128)(2,1)S(1)} %get-tuple-element.106.refs_1_), channel_id=1, source_target_pairs={{0,2},{1,3},{2,0},{3,1},{4,6},{5,7},{6,4},{7,5},{8,10},{9,11},{10,... | collective-permute-start | bytes 589832 | tf_op jit(solution)/shard_map/ppermute | solution.py:542
  84.1 8.2 %collective-permute-done.18.refs_3_ = bf16[128,768]{1,0:T(8,128)(2,1)S(1)} collective-permute-done((bf16[128,768]{1,0:T(8,128)(2,1)S(1)}, bf16[128,768]{1,0:T(8,128)(2,1)S(1)}, u32[]{:S(2)}, u32[]{:S(2)}) %collective-permute-start.18) | collective-permute-done | bytes 196640 | tf_op jit(solution)/shard_map/ppermute | solution.py:542
  92.9 5.5 %collective-permute-done.19.refs_4_ = bf16[128,768]{1,0:T(8,128)(2,1)S(1)} collective-permute-done((bf16[128,768]{1,0:T(8,128)(2,1)S(1)}, bf16[128,768]{1,0:T(8,128)(2,1)S(1)}, u32[]{:S(2)}, u32[]{:S(2)}) %collective-permute-start.19) | collective-permute-done | bytes 196640 | tf_op jit(solution)/shard_map/ppermute | solution.py:542
  98.4 4.3 %feed_back.1 = (f32[128,768]{1,0:T(8,128)S(1)}, bf16[128,768]{1,0:T(8,128)(2,1)S(1)}, bf16[128,768]{1,0:T(8,128)(2,1)S(1)}, bf16[128,768]{1,0:T(8,128)(2,1)S(1)}...) custom-call(bf16[512,768]{1,0:T(8,128)(2,1)S(1)} %get-tuple-element., ...), custom_call_target="tpu_custom_call" | custom-call | flops 3019898880 | bytes 9240576 | tf_op jit(solution)/shard_map/feed_back/pallas_call | solution.py:83
  102.6 3.0 %feed_weights.1 = (f32[4,3,96,768]{3,2,1,0:T(8,128)S(1)}, bf16[4,3,96,768]{3,2,1,0:T(8,128)(2,1)S(1)}) custom-call(s32[12]{0:T(128)S(1)} %pad_add_fusion.ids, bf16[512,768]{1,0:T(8,128)(2,1)S(1)} %get-tuple-element.103.refs_4_.refs_0_, bf16[512,768]{1,0:T(8,128)(2,1)S(1)} %get-tuple-element.112.refs_1_, bf16[512,768]{1,0:T(8,128)(2,1)S(1)} %get-tuple-element.113.refs_2_, ...), custom_call_target="tpu_custom_call" | custom-call | flops 1811939328 | bytes 9240576 | tf_op jit(solution)/shard_map/feed_weights/pallas_call | solution.py:83
  106.7 3.5 %collective-permute-start.22 = (bf16[128,768]{1,0:T(8,128)(2,1)S(1)}, bf16[128,768]{1,0:T(8,128)(2,1)S(1)}, u32[]{:S(2)}, u32[]{:S(2)}) collective-permute-start(bf16[128,768]{1,0:T(8,128)(2,1)S(1)} %get-tuple-element.110), channel_id=1, source_target_pairs={{0,3},{1,2},{2,1},{3,0},{4,7},{5,6},{6,5},{7,4},{8,11},{9,10},{10,... | collective-permute-start | bytes 589832 | tf_op jit(solution)/shard_map/ppermute | solution.py:542
  110.6 5.3 %collective-permute-done.20.refs_1_ = bf16[128,768]{1,0:T(8,128)(2,1)S(1)} collective-permute-done((bf16[128,768]{1,0:T(8,128)(2,1)S(1)}, bf16[128,768]{1,0:T(8,128)(2,1)S(1)}, u32[]{:S(2)}, u32[]{:S(2)}) %collective-permute-start.20) | collective-permute-done | bytes 196640 | tf_op jit(solution)/shard_map/ppermute | solution.py:542
  115.9 7.4 %collective-permute-done.21.refs_2_ = bf16[128,768]{1,0:T(8,128)(2,1)S(1)} collective-permute-done((bf16[128,768]{1,0:T(8,128)(2,1)S(1)}, bf16[128,768]{1,0:T(8,128)(2,1)S(1)}, u32[]{:S(2)}, u32[]{:S(2)}) %collective-permute-start.21) | collective-permute-done | bytes 196640 | tf_op jit(solution)/shard_map/ppermute | solution.py:542
  128.6 4.0 %collective-permute-start.24 = (bf16[144,384]{1,0:T(8,128)(2,1)S(1)}, bf16[144,384]{1,0:T(8,128)(2,1)S(1)}, u32[]{:S(2)}, u32[]{:S(2)}) collective-permute-start(bf16[144,384]{1,0:T(8,128)(2,1)S(1)} %get-tuple-element.128), channel_id=1, source_target_pairs={{0,1},{1,0},{2,3},{3,2},{4,5},{5,4},{6,7},{7,6},{8,9},{9,8},{10,11... | collective-permute-start | bytes 331784 | tf_op jit(solution)/shard_map/ppermute | solution.py:542
  132.7 3.0 %collective-permute-done.24.refs_1_.refs_6_.refs_7_ = bf16[144,384]{1,0:T(8,128)(2,1)S(1)} collective-permute-done((bf16[144,384]{1,0:T(8,128)(2,1)S(1)}, bf16[144,384]{1,0:T(8,128)(2,1)S(1)}, u32[]{:S(2)}, u32[]{:S(2)}) %collective-permute-start.24) | collective-permute-done | bytes 110624 | tf_op jit(solution)/shard_map/ppermute | solution.py:542
  137.6 5.3 %collective-permute-done.25.refs_2_.refs_7_.refs_8_ = bf16[144,384]{1,0:T(8,128)(2,1)S(1)} collective-permute-done((bf16[144,384]{1,0:T(8,128)(2,1)S(1)}, bf16[144,384]{1,0:T(8,128)(2,1)S(1)}, u32[]{:S(2)}, u32[]{:S(2)}) %collective-permute-start.25) | collective-permute-done | bytes 110624 | tf_op jit(solution)/shard_map/ppermute | solution.py:542
  142.9 6.0 %attention_back.1 = (f32[128,768]{1,0:T(8,128)S(1)}, bf16[128,768]{1,0:T(8,128)(2,1)S(1)}, bf16[128,768]{1,0:T(8,128)(2,1)S(1)}, bf16[128,768]{1,0:T(8,128)(2,1)S(1)}, bf16[512,576]{1,0:T(8,128)(2,1)S(1)}) custom-call(bf16[144,384]{1,0:T(8,128)(2,1)S(1)} %get-tuple-element.127.refs_0_.refs_6_, ...), custom_call_target="tpu_custom_call" | custom-call | flops 956301312 | bytes 5062656 | tf_op jit(solution)/shard_map/attention_back/pallas_call | solution.py:83
  153.3 2.7 %collective-permute-start.28 = (bf16[128,768]{1,0:T(8,128)(2,1)S(1)}, bf16[128,768]{1,0:T(8,128)(2,1)S(1)}, u32[]{:S(2)}, u32[]{:S(2)}) collective-permute-start(bf16[128,768]{1,0:T(8,128)(2,1)S(1)} %get-tuple-element.138), channel_id=1, source_target_pairs={{0,2},{1,3},{2,0},{3,1},{4,6},{5,7},{6,4},{7,5},{8,10},{9,11},{10,... | collective-permute-start | bytes 589832 | tf_op jit(solution)/shard_map/ppermute | solution.py:542
  157.7 10.3 %collective-permute-done.27.refs_2_ = bf16[128,768]{1,0:T(8,128)(2,1)S(1)} collective-permute-done((bf16[128,768]{1,0:T(8,128)(2,1)S(1)}, bf16[128,768]{1,0:T(8,128)(2,1)S(1)}, u32[]{:S(2)}, u32[]{:S(2)}) %collective-permute-start.27) | collective-permute-done | bytes 196640 | tf_op jit(solution)/shard_map/ppermute | solution.py:542
  168.0 19.4 %collective-permute-done.28.refs_3_ = bf16[128,768]{1,0:T(8,128)(2,1)S(1)} collective-permute-done((bf16[128,768]{1,0:T(8,128)(2,1)S(1)}, bf16[128,768]{1,0:T(8,128)(2,1)S(1)}, u32[]{:S(2)}, u32[]{:S(2)}) %collective-permute-start.28) | collective-permute-done | bytes 196640 | tf_op jit(solution)/shard_map/ppermute | solution.py:542
  190.9 4.2 %collective-permute-start.41 = (bf16[3,96,768]{2,1,0:T(8,128)(2,1)S(1)}, bf16[3,96,768]{2,1,0:T(8,128)(2,1)S(1)}, u32[]{:S(2)}, u32[]{:S(2)}) collective-permute-start(bf16[3,96,768]{2,1,0:T(8,128)(2,1)S(1)} %plane_sum.2.refs_0_), channel_id=1, source_target_pairs={{0,1},{1,0},{2,3},{3,2},{4,5},{5,4},{6,7},{7,6},{8,9},{9,8},{10,11... | collective-permute-start | bytes 1327112 | tf_op jit(solution)/shard_map/ppermute | solution.py:542
  197.6 4.9 %collective-permute-start.39 = (bf16[112,768]{1,0:T(8,128)(2,1)S(1)}, bf16[112,768]{1,0:T(8,128)(2,1)S(1)}, u32[]{:S(2)}, u32[]{:S(2)}) collective-permute-start(bf16[112,768]{1,0:T(8,128)(2,1)S(1)} %plane_sum.3.refs_0_), channel_id=1, source_target_pairs={{0,2},{1,3},{2,0},{3,1},{4,6},{5,7},{6,4},{7,5},{8,10},{9,11},{10,... | collective-permute-start | bytes 516104 | tf_op jit(solution)/shard_map/ppermute | solution.py:542
  202.6 16.3 %collective-permute-done.39.refs_2_ = bf16[112,768]{1,0:T(8,128)(2,1)S(1)} collective-permute-done((bf16[112,768]{1,0:T(8,128)(2,1)S(1)}, bf16[112,768]{1,0:T(8,128)(2,1)S(1)}, u32[]{:S(2)}, u32[]{:S(2)}) %collective-permute-start.39) | collective-permute-done | bytes 172064 | tf_op jit(solution)/shard_map/ppermute | solution.py:542
  218.8 2.5 %collective-permute-start.40 = (bf16[112,768]{1,0:T(8,128)(2,1)S(1)}, bf16[112,768]{1,0:T(8,128)(2,1)S(1)}, u32[]{:S(2)}, u32[]{:S(2)}) collective-permute-start(bf16[112,768]{1,0:T(8,128)(2,1)S(1)} %collective-permute-done.39.refs_2_), channel_id=1, source_target_pairs={{0,1},{1,0},{2,3},{3,2},{4,5},{5,4},{6,7},{7,6},{8,9},{9,8},{10,11... | collective-permute-start | bytes 516104 | tf_op jit(solution)/shard_map/ppermute | solution.py:542
  222.6 4.5 %feed_final.1 = (f32[96,6144]{1,0:T(8,128)}, f32[384,768]{1,0:T(8,128)}) custom-call(s32[12]{0:T(128)S(1)} %pad_add_fusion.ids, bf16[3,96,768]{2,1,0:T(8,128)(2,1)S(1)} %plane_sum.2.refs_0_, bf16[3,96,768]{2,1,0:T(8,128)(2,1)S(1)} %collective-permute-done.41.refs_1_, bf16[3,96,768]{2,1,0:T(8,128)(2,1)S(1)} %collective-permute-done.37.refs_2_, ...), custom_call_target="tpu_custom_call" | custom-call | bytes 5308416 | tf_op jit(solution)/shard_map/feed_final/pallas_call | solution.py:83
  (95 shorter events, 50.4 us)
Async XLA Ops:
  2.0 9.9 %collective-permute-start.5 = (bf16[96,576]{1,0:T(8,128)(2,1)S(1)}, bf16[96,576]{1,0:T(8,128)(2,1)S(1)}, u32[]{:S(2)}, u32[]{:S(2)}) collective-permute-start(bf16[96,576]{1,0:T(8,128)(2,1)S(1)} %pad_maximum_fusion.2.refs_4_), channel_id=1, source_target_pairs={{0,24},{4,28},{8,16},{12,20},{16,8},{20,12},{24,0},{28,4},{1,25},{... | collective-permute-start | bytes 331784 | tf_op jit(solution)/shard_map/ppermute | solution.py:539
  6.6 11.6 %collective-permute-start.1 = (bf16[128,768]{1,0:T(8,128)(2,1)}, bf16[128,768]{1,0:T(8,128)(2,1)S(1)}, u32[]{:S(2)}, u32[]{:S(2)}) collective-permute-start(bf16[128,768]{1,0:T(8,128)(2,1)} %bitcast.16), channel_id=1, source_target_pairs={{0,2},{1,3},{2,0},{3,1},{4,6},{5,7},{6,4},{7,5},{8,10},{9,11},{10,... | collective-permute-start | bytes 589832 | tf_op jit(solution)/shard_map/ppermute | solution.py:542
  9.6 8.8 %collective-permute-start = (bf16[128,768]{1,0:T(8,128)(2,1)}, bf16[128,768]{1,0:T(8,128)(2,1)S(1)}, u32[]{:S(2)}, u32[]{:S(2)}) collective-permute-start(bf16[128,768]{1,0:T(8,128)(2,1)} %bitcast.17), channel_id=1, source_target_pairs={{0,1},{1,0},{2,3},{3,2},{4,5},{5,4},{6,7},{7,6},{8,9},{9,8},{10,11... | collective-permute-start | bytes 589832 | tf_op jit(solution)/shard_map/ppermute | solution.py:542
  12.3 15.3 %collective-permute-start.6 = (bf16[384,576]{1,0:T(8,128)(2,1)S(1)}, bf16[384,576]{1,0:T(8,128)(2,1)S(1)}, u32[]{:S(2)}, u32[]{:S(2)}) collective-permute-start(bf16[384,576]{1,0:T(8,128)(2,1)S(1)} %pad_maximum_fusion.1), channel_id=1, source_target_pairs={{0,4},{4,0},{8,12},{12,8},{16,20},{20,16},{24,28},{28,24},{1,5},{5... | collective-permute-start | bytes 1327112 | tf_op jit(solution)/shard_map/ppermute | solution.py:539
  18.4 26.3 %collective-permute-start.12 = (bf16[400,768]{1,0:T(8,128)(2,1)S(1)}, bf16[400,768]{1,0:T(8,128)(2,1)S(1)}, u32[]{:S(2)}, u32[]{:S(2)}) collective-permute-start(bf16[400,768]{1,0:T(8,128)(2,1)S(1)} %select_units.1.refs_0_), channel_id=1, source_target_pairs={{0,24},{4,28},{8,16},{12,20},{16,8},{20,12},{24,0},{28,4},{1,25},{... | collective-permute-start | bytes 1843208 | tf_op jit(solution)/shard_map/ppermute | solution.py:539
  20.9 25.9 %collective-permute-start.11 = (bf16[400,768]{1,0:T(8,128)(2,1)S(1)}, bf16[400,768]{1,0:T(8,128)(2,1)S(1)}, u32[]{:S(2)}, u32[]{:S(2)}) collective-permute-start(bf16[400,768]{1,0:T(8,128)(2,1)S(1)} %select_units.1.refs_0_), channel_id=1, source_target_pairs={{0,16},{4,20},{8,24},{12,28},{16,0},{20,4},{24,8},{28,12},{1,17},{... | collective-permute-start | bytes 1843208 | tf_op jit(solution)/shard_map/ppermute | solution.py:539
  21.4 25.6 %collective-permute-start.10 = (bf16[400,768]{1,0:T(8,128)(2,1)S(1)}, bf16[400,768]{1,0:T(8,128)(2,1)S(1)}, u32[]{:S(2)}, u32[]{:S(2)}) collective-permute-start(bf16[400,768]{1,0:T(8,128)(2,1)S(1)} %select_units.1.refs_0_), channel_id=1, source_target_pairs={{0,8},{4,12},{8,0},{12,4},{16,24},{20,28},{24,16},{28,20},{1,9},{5... | collective-permute-start | bytes 1843208 | tf_op jit(solution)/shard_map/ppermute | solution.py:539
  34.0 10.4 %collective-permute-start.8 = (bf16[768,128]{1,0:T(8,128)(2,1)S(1)}, bf16[768,128]{1,0:T(8,128)(2,1)S(1)}, u32[]{:S(2)}, u32[]{:S(2)}) collective-permute-start(bf16[768,128]{1,0:T(8,128)(2,1)S(1)} %get-tuple-element.89.refs_0_), channel_id=1, source_target_pairs={{0,2},{1,3},{2,0},{3,1},{4,6},{5,7},{6,4},{7,5},{8,10},{9,11},{10,... | collective-permute-start | bytes 589832 | tf_op jit(solution)/shard_map/ppermute | solution.py:542
  36.4 8.3 %collective-permute-start.7 = (bf16[768,128]{1,0:T(8,128)(2,1)S(1)}, bf16[768,128]{1,0:T(8,128)(2,1)S(1)}, u32[]{:S(2)}, u32[]{:S(2)}) collective-permute-start(bf16[768,128]{1,0:T(8,128)(2,1)S(1)} %get-tuple-element.89.refs_0_), channel_id=1, source_target_pairs={{0,1},{1,0},{2,3},{3,2},{4,5},{5,4},{6,7},{7,6},{8,9},{9,8},{10,11... | collective-permute-start | bytes 589832 | tf_op jit(solution)/shard_map/ppermute | solution.py:542
  59.1 9.8 %collective-permute-start.14 = (bf16[128,768]{1,0:T(8,128)(2,1)S(1)}, bf16[128,768]{1,0:T(8,128)(2,1)S(1)}, u32[]{:S(2)}, u32[]{:S(2)}) collective-permute-start(bf16[128,768]{1,0:T(8,128)(2,1)S(1)} %get-tuple-element.100), channel_id=1, source_target_pairs={{0,1},{1,0},{2,3},{3,2},{4,5},{5,4},{6,7},{7,6},{8,9},{9,8},{10,11... | collective-permute-start | bytes 589832 | tf_op jit(solution)/shard_map/ppermute | solution.py:542
  61.0 17.5 %collective-permute-start.15 = (bf16[128,768]{1,0:T(8,128)(2,1)S(1)}, bf16[128,768]{1,0:T(8,128)(2,1)S(1)}, u32[]{:S(2)}, u32[]{:S(2)}) collective-permute-start(bf16[128,768]{1,0:T(8,128)(2,1)S(1)} %get-tuple-element.101), channel_id=1, source_target_pairs={{0,2},{1,3},{2,0},{3,1},{4,6},{5,7},{6,4},{7,5},{8,10},{9,11},{10,... | collective-permute-start | bytes 589832 | tf_op jit(solution)/shard_map/ppermute | solution.py:542
  64.2 14.2 %collective-permute-start.16 = (bf16[128,768]{1,0:T(8,128)(2,1)S(1)}, bf16[128,768]{1,0:T(8,128)(2,1)S(1)}, u32[]{:S(2)}, u32[]{:S(2)}) collective-permute-start(bf16[128,768]{1,0:T(8,128)(2,1)S(1)} %get-tuple-element.102), channel_id=1, source_target_pairs={{0,3},{1,2},{2,1},{3,0},{4,7},{5,6},{6,5},{7,4},{8,11},{9,10},{10,... | collective-permute-start | bytes 589832 | tf_op jit(solution)/shard_map/ppermute | solution.py:542
  79.5 12.8 %collective-permute-start.18 = (bf16[128,768]{1,0:T(8,128)(2,1)S(1)}, bf16[128,768]{1,0:T(8,128)(2,1)S(1)}, u32[]{:S(2)}, u32[]{:S(2)}) collective-permute-start(bf16[128,768]{1,0:T(8,128)(2,1)S(1)} %get-tuple-element.106.refs_1_), channel_id=1, source_target_pairs={{0,2},{1,3},{2,0},{3,1},{4,6},{5,7},{6,4},{7,5},{8,10},{9,11},{10,... | collective-permute-start | bytes 589832 | tf_op jit(solution)/shard_map/ppermute | solution.py:542
  84.0 8.9 %collective-permute-start.17 = (bf16[128,768]{1,0:T(8,128)(2,1)S(1)}, bf16[128,768]{1,0:T(8,128)(2,1)S(1)}, u32[]{:S(2)}, u32[]{:S(2)}) collective-permute-start(bf16[128,768]{1,0:T(8,128)(2,1)S(1)} %get-tuple-element.106.refs_1_), channel_id=1, source_target_pairs={{0,1},{1,0},{2,3},{3,2},{4,5},{5,4},{6,7},{7,6},{8,9},{9,8},{10,11... | collective-permute-start | bytes 589832 | tf_op jit(solution)/shard_map/ppermute | solution.py:542
  105.8 10.1 %collective-permute-start.20 = (bf16[128,768]{1,0:T(8,128)(2,1)S(1)}, bf16[128,768]{1,0:T(8,128)(2,1)S(1)}, u32[]{:S(2)}, u32[]{:S(2)}) collective-permute-start(bf16[128,768]{1,0:T(8,128)(2,1)S(1)} %get-tuple-element.108), channel_id=1, source_target_pairs={{0,1},{1,0},{2,3},{3,2},{4,5},{5,4},{6,7},{7,6},{8,9},{9,8},{10,11... | collective-permute-start | bytes 589832 | tf_op jit(solution)/shard_map/ppermute | solution.py:542
  106.1 17.1 %collective-permute-start.21 = (bf16[128,768]{1,0:T(8,128)(2,1)S(1)}, bf16[128,768]{1,0:T(8,128)(2,1)S(1)}, u32[]{:S(2)}, u32[]{:S(2)}) collective-permute-start(bf16[128,768]{1,0:T(8,128)(2,1)S(1)} %get-tuple-element.109), channel_id=1, source_target_pairs={{0,2},{1,3},{2,0},{3,1},{4,6},{5,7},{6,4},{7,5},{8,10},{9,11},{10,... | collective-permute-start | bytes 589832 | tf_op jit(solution)/shard_map/ppermute | solution.py:542
  106.7 16.6 %collective-permute-start.22 = (bf16[128,768]{1,0:T(8,128)(2,1)S(1)}, bf16[128,768]{1,0:T(8,128)(2,1)S(1)}, u32[]{:S(2)}, u32[]{:S(2)}) collective-permute-start(bf16[128,768]{1,0:T(8,128)(2,1)S(1)} %get-tuple-element.110), channel_id=1, source_target_pairs={{0,3},{1,2},{2,1},{3,0},{4,7},{5,6},{6,5},{7,4},{8,11},{9,10},{10,... | collective-permute-start | bytes 589832 | tf_op jit(solution)/shard_map/ppermute | solution.py:542
  123.3 25.7 %collective-permute-start.30 = (bf16[3,96,768]{2,1,0:T(8,128)(2,1)S(1)}, bf16[3,96,768]{2,1,0:T(8,128)(2,1)S(1)}, u32[]{:S(2)}, u32[]{:S(2)}) collective-permute-start(bf16[3,96,768]{2,1,0:T(8,128)(2,1)S(1)} %get-tuple-element.145), channel_id=1, source_target_pairs={{0,8},{4,12},{8,0},{12,4},{16,24},{20,28},{24,16},{28,20},{1,9},{5... | collective-permute-start | bytes 1327112 | tf_op jit(solution)/shard_map/ppermute | solution.py:539
  124.7 24.3 %collective-permute-start.31 = (bf16[3,96,768]{2,1,0:T(8,128)(2,1)S(1)}, bf16[3,96,768]{2,1,0:T(8,128)(2,1)S(1)}, u32[]{:S(2)}, u32[]{:S(2)}) collective-permute-start(bf16[3,96,768]{2,1,0:T(8,128)(2,1)S(1)} %get-tuple-element.146), channel_id=1, source_target_pairs={{0,16},{4,20},{8,24},{12,28},{16,0},{20,4},{24,8},{28,12},{1,17},{... | collective-permute-start | bytes 1327112 | tf_op jit(solution)/shard_map/ppermute | solution.py:539
  125.5 23.5 %collective-permute-start.32 = (bf16[3,96,768]{2,1,0:T(8,128)(2,1)S(1)}, bf16[3,96,768]{2,1,0:T(8,128)(2,1)S(1)}, u32[]{:S(2)}, u32[]{:S(2)}) collective-permute-start(bf16[3,96,768]{2,1,0:T(8,128)(2,1)S(1)} %get-tuple-element.147), channel_id=1, source_target_pairs={{0,24},{4,28},{8,16},{12,20},{16,8},{20,12},{24,0},{28,4},{1,25},{... | collective-permute-start | bytes 1327112 | tf_op jit(solution)/shard_map/ppermute | solution.py:539
  132.7 10.3 %collective-permute-start.25 = (bf16[144,384]{1,0:T(8,128)(2,1)S(1)}, bf16[144,384]{1,0:T(8,128)(2,1)S(1)}, u32[]{:S(2)}, u32[]{:S(2)}) collective-permute-start(bf16[144,384]{1,0:T(8,128)(2,1)S(1)} %get-tuple-element.129), channel_id=1, source_target_pairs={{0,2},{1,3},{2,0},{3,1},{4,6},{5,7},{6,4},{7,5},{8,10},{9,11},{10,... | collective-permute-start | bytes 331784 | tf_op jit(solution)/shard_map/ppermute | solution.py:542
  151.3 43.9 %collective-permute-start.37 = (bf16[3,96,768]{2,1,0:T(8,128)(2,1)S(1)}, bf16[3,96,768]{2,1,0:T(8,128)(2,1)S(1)}, u32[]{:S(2)}, u32[]{:S(2)}) collective-permute-start(bf16[3,96,768]{2,1,0:T(8,128)(2,1)S(1)} %plane_sum.2.refs_0_), channel_id=1, source_target_pairs={{0,2},{1,3},{2,0},{3,1},{4,6},{5,7},{6,4},{7,5},{8,10},{9,11},{10,... | collective-permute-start | bytes 1327112 | tf_op jit(solution)/shard_map/ppermute | solution.py:542
  153.2 14.8 %collective-permute-start.27 = (bf16[128,768]{1,0:T(8,128)(2,1)S(1)}, bf16[128,768]{1,0:T(8,128)(2,1)S(1)}, u32[]{:S(2)}, u32[]{:S(2)}) collective-permute-start(bf16[128,768]{1,0:T(8,128)(2,1)S(1)} %get-tuple-element.137), channel_id=1, source_target_pairs={{0,1},{1,0},{2,3},{3,2},{4,5},{5,4},{6,7},{7,6},{8,9},{9,8},{10,11... | collective-permute-start | bytes 589832 | tf_op jit(solution)/shard_map/ppermute | solution.py:542
  153.3 34.1 %collective-permute-start.28 = (bf16[128,768]{1,0:T(8,128)(2,1)S(1)}, bf16[128,768]{1,0:T(8,128)(2,1)S(1)}, u32[]{:S(2)}, u32[]{:S(2)}) collective-permute-start(bf16[128,768]{1,0:T(8,128)(2,1)S(1)} %get-tuple-element.138), channel_id=1, source_target_pairs={{0,2},{1,3},{2,0},{3,1},{4,6},{5,7},{6,4},{7,5},{8,10},{9,11},{10,... | collective-permute-start | bytes 589832 | tf_op jit(solution)/shard_map/ppermute | solution.py:542
  156.0 31.4 %collective-permute-start.29 = (bf16[128,768]{1,0:T(8,128)(2,1)S(1)}, bf16[128,768]{1,0:T(8,128)(2,1)S(1)}, u32[]{:S(2)}, u32[]{:S(2)}) collective-permute-start(bf16[128,768]{1,0:T(8,128)(2,1)S(1)} %get-tuple-element.139), channel_id=1, source_target_pairs={{0,3},{1,2},{2,1},{3,0},{4,7},{5,6},{6,5},{7,4},{8,11},{9,10},{10,... | collective-permute-start | bytes 589832 | tf_op jit(solution)/shard_map/ppermute | solution.py:542
  188.8 8.7 %collective-permute-start.35 = (bf16[112,768]{1,0:T(8,128)(2,1)S(1)}, bf16[112,768]{1,0:T(8,128)(2,1)S(1)}, u32[]{:S(2)}, u32[]{:S(2)}) collective-permute-start(bf16[112,768]{1,0:T(8,128)(2,1)S(1)} %get-tuple-element.157), channel_id=1, source_target_pairs={{0,16},{4,20},{8,24},{12,28},{16,0},{20,4},{24,8},{28,12},{1,17},{... | collective-permute-start | bytes 516104 | tf_op jit(solution)/shard_map/ppermute | solution.py:539
  189.6 7.9 %collective-permute-start.36 = (bf16[112,768]{1,0:T(8,128)(2,1)S(1)}, bf16[112,768]{1,0:T(8,128)(2,1)S(1)}, u32[]{:S(2)}, u32[]{:S(2)}) collective-permute-start(bf16[112,768]{1,0:T(8,128)(2,1)S(1)} %get-tuple-element.158), channel_id=1, source_target_pairs={{0,24},{4,28},{8,16},{12,20},{16,8},{20,12},{24,0},{28,4},{1,25},{... | collective-permute-start | bytes 516104 | tf_op jit(solution)/shard_map/ppermute | solution.py:539
  190.9 31.8 %collective-permute-start.41 = (bf16[3,96,768]{2,1,0:T(8,128)(2,1)S(1)}, bf16[3,96,768]{2,1,0:T(8,128)(2,1)S(1)}, u32[]{:S(2)}, u32[]{:S(2)}) collective-permute-start(bf16[3,96,768]{2,1,0:T(8,128)(2,1)S(1)} %plane_sum.2.refs_0_), channel_id=1, source_target_pairs={{0,1},{1,0},{2,3},{3,2},{4,5},{5,4},{6,7},{7,6},{8,9},{9,8},{10,11... | collective-permute-start | bytes 1327112 | tf_op jit(solution)/shard_map/ppermute | solution.py:542
  195.1 27.5 %collective-permute-start.42 = (bf16[3,96,768]{2,1,0:T(8,128)(2,1)S(1)}, bf16[3,96,768]{2,1,0:T(8,128)(2,1)S(1)}, u32[]{:S(2)}, u32[]{:S(2)}) collective-permute-start(bf16[3,96,768]{2,1,0:T(8,128)(2,1)S(1)} %collective-permute-done.37.refs_2_), channel_id=1, source_target_pairs={{0,1},{1,0},{2,3},{3,2},{4,5},{5,4},{6,7},{7,6},{8,9},{9,8},{10,11... | collective-permute-start | bytes 1327112 | tf_op jit(solution)/shard_map/ppermute | solution.py:542
  197.6 21.2 %collective-permute-start.39 = (bf16[112,768]{1,0:T(8,128)(2,1)S(1)}, bf16[112,768]{1,0:T(8,128)(2,1)S(1)}, u32[]{:S(2)}, u32[]{:S(2)}) collective-permute-start(bf16[112,768]{1,0:T(8,128)(2,1)S(1)} %plane_sum.3.refs_0_), channel_id=1, source_target_pairs={{0,2},{1,3},{2,0},{3,1},{4,6},{5,7},{6,4},{7,5},{8,10},{9,11},{10,... | collective-permute-start | bytes 516104 | tf_op jit(solution)/shard_map/ppermute | solution.py:542
  202.5 24.7 %collective-permute-start.38 = (bf16[112,768]{1,0:T(8,128)(2,1)S(1)}, bf16[112,768]{1,0:T(8,128)(2,1)S(1)}, u32[]{:S(2)}, u32[]{:S(2)}) collective-permute-start(bf16[112,768]{1,0:T(8,128)(2,1)S(1)} %plane_sum.3.refs_0_), channel_id=1, source_target_pairs={{0,1},{1,0},{2,3},{3,2},{4,5},{5,4},{6,7},{7,6},{8,9},{9,8},{10,11... | collective-permute-start | bytes 516104 | tf_op jit(solution)/shard_map/ppermute | solution.py:542
  218.8 8.3 %collective-permute-start.40 = (bf16[112,768]{1,0:T(8,128)(2,1)S(1)}, bf16[112,768]{1,0:T(8,128)(2,1)S(1)}, u32[]{:S(2)}, u32[]{:S(2)}) collective-permute-start(bf16[112,768]{1,0:T(8,128)(2,1)S(1)} %collective-permute-done.39.refs_2_), channel_id=1, source_target_pairs={{0,1},{1,0},{2,3},{3,2},{4,5},{5,4},{6,7},{7,6},{8,9},{9,8},{10,11... | collective-permute-start | bytes 516104 | tf_op jit(solution)/shard_map/ppermute | solution.py:542
  (18 other events, 186.5 us)
where the time goes:
time: 230 us
  waiting for transfers between devices  119 us (52%)
  starting transfers between devices  65.4 us (28%)
  Pallas kernels  38.9 us (17%)
  local copies, waits for them, and re-layouts  4.22 us (2%)
    ppermute x27, waiting for transfers between devices, pass_seq(): return lax.ppermute(value, 'seq', [(i, i ^ s) for i in range(SEQ)])  111 us
    ppermute x27, starting transfers between devices, pass_seq(): return lax.ppermute(value, 'seq', [(i, i ^ s) for i in range(SEQ)])  50 us
    pallas_call x17, Pallas kernels, call(): pl.pallas_call(kernel, out_shape=out_shape, in_specs=specs, out_specs=[pl...  38.9 us
    ppermute x16, starting transfers between devices, swap(): return lax.ppermute(value, 'dp', [(i, i ^ s * stride) for i in range(dp)])  15.4 us
    ppermute x16, waiting for transfers between devices, swap(): return lax.ppermute(value, 'dp', [(i, i ^ s * stride) for i in range(dp)])  7.82 us
  transfers between devices with their start and end apart: 43, of which 23 were waited for; matrix products, arithmetic and copies ran while one was open for 1% of the time, Pallas kernels for 10%

commit v1 on v0

--- a/solution.py
+++ b/solution.py
@@ -326,6 +326,41 @@
         refs[2 + t][...] = (keep[t] + received[t].astype(F32)).astype(refs[2 + t].dtype)
 
 
+def step_one(*refs):
+    keep, received = refs[0:2]
+    left, left_next, right, right_next, to_x, to_y = refs[2:8]
+    half = left.shape[-1]
+
+    def part(t, side):
+        cols = slice(side * half, (side + 1) * half)
+        return keep[t, :, :, cols] + received[t, :, :, cols].astype(F32)
+
+    left[...] = part(0, 0)
+    left_next[...] = part(2, 0)
+    right[...] = part(0, 1)
+    right_next[...] = part(1, 1)
+    to_x[0] = part(1, 0).astype(BF16)
+    to_x[1] = part(3, 0).astype(BF16)
+    to_y[0] = part(2, 1).astype(BF16)
+    to_y[1] = part(3, 1).astype(BF16)
+
+
+def step_two(*refs):
+    left, left_next, right, right_next, from_x, from_y = refs[0:6]
+    left_out, right_out, to_y, to_x = refs[6:10]
+    left_out[...] = left[...] + from_x[0].astype(F32)
+    to_y[...] = (left_next[...] + from_x[1].astype(F32)).astype(BF16)
+    right_out[...] = right[...] + from_y[0].astype(F32)
+    to_x[...] = (right_next[...] + from_y[1].astype(F32)).astype(BF16)
+
+
+def step_three(*refs):
+    left, right, from_y, from_x, out = refs
+    half = left.shape[-1]
+    out[:, :, 0:half] = (left[...] + from_y[...].astype(F32)).astype(BF16)
+    out[:, :, half:] = (right[...] + from_x[...].astype(F32)).astype(BF16)
+
+
 def plane_sum(*refs):
     out = refs[-1]
     acc = refs[0][...].astype(F32)
@@ -695,14 +730,25 @@
         shape = keep.shape[1:]
         return call(pair_sum, [(shape, F32)] + [(shape, BF16)] * 3, [], keep, swap(send, 1))
 
-    def reduce_plane(pieces):
-        shape = pieces[0].shape
-        pieces = [pieces[0]] + [swap(pieces[t], 2 * t) for t in range(1, CHIPS)]
-        return call(plane_sum, [(shape, BF16)], [], *pieces)[0]
-
-    feed_pieces = pair(feed_keep, feed_send)
-    grad_second = after(grad_second, feed_pieces)
-    feed_pieces = after(feed_pieces, back_parts)
+    half_shape = (3, shard, model // 2)
+    *feed_pieces, to_x, to_y = call(
+        step_one,
+        [(half_shape, F32)] * 4 + [((2,) + half_shape, BF16)] * 2,
+        [],
+        after(feed_keep, back_parts[1]),
+        swap(feed_send, 1),
+        mib=10,
+    )
+    left, right, to_y, to_x = call(
+        step_two,
+        [(half_shape, F32)] * 2 + [(half_shape, BF16)] * 2,
+        [],
+        *feed_pieces,
+        swap(to_x, 2),
+        swap(to_y, 4),
+        mib=10,
+    )
+    grad_second = after(grad_second, to_y)
 
     grad_first, *projected = call(
         project_back,
@@ -722,7 +768,10 @@
     )
     grad_attn = reduce_seq(projected[0:4])
     sums = projected[4]
-    feed_share = reduce_plane(feed_pieces)
+    (feed_share,) = call(
+        step_three, [((3, shard, model), BF16)], [], left, right, swap(to_y, 4), swap(to_x, 2)
+    )
+    queries = after(queries, feed_share)
     feed_blocks = gather_seq(after(feed_share, grad_attn))
 
     *input_parts, grad_qkv = call(
@@ -741,7 +790,6 @@
     )
     input_parts = reduce_seq(input_parts)
 
-    sums = after(sums, feed_share)
 
     attn_keep, attn_send = call(
         attention_weights,
@@ -772,8 +820,10 @@
         *feed_blocks,
         mib=10,
     )
-    attn_pieces = after(pair(attn_keep, attn_send), input_parts)
-    attn_share = after(reduce_plane(attn_pieces), feed_blocks[2])
+    attn_pieces = pair(attn_keep, attn_send)
+    attn_pieces = [attn_pieces[0]] + [swap(attn_pieces[t], 2 * t) for t in range(1, CHIPS)]
+    attn_pieces = after(attn_pieces, input_parts, feed_blocks[1:3])
+    (attn_share,) = call(plane_sum, [((shard + PAD, model), BF16)], [], *attn_pieces)
     grad_qkv_w, grad_out_w, vector_grads = call(
         attention_final,
         [((shard, 3 * model), F32), ((shard, model), F32), ((8, 128), F32)],

time: 230 us -> 224 us (0.974)
  waiting for transfers between devices: 119 us -> 113 us
    ppermute x27, waiting for transfers between devices: 111 us -> 97.2 us  [pass_seq(): return lax.ppermute(value, 'seq', [(i, i ^ s) for i in range(SEQ)])]
    ppermute x16 -> x17, waiting for transfers between devices: 7.82 us -> 16.1 us  [swap(): return lax.ppermute(value, 'dp', [(i, i ^ s * stride) for i in range(dp)])]
    ppermute x16 -> x17, starting transfers between devices: 15.4 us -> 15.8 us  [swap(): return lax.ppermute(value, 'dp', [(i, i ^ s * stride) for i in range(dp)])]
    pallas_call x17 -> x18, Pallas kernels: 38.9 us -> 39.1 us  [call(): pl.pallas_call(kernel, out_shape=out_shape, in_specs=specs, out_specs=[pl...]
  transfers between devices with their start and end apart: 43 -> 44, of which waited for: 23 -> 25; matrix products, arithmetic and copies ran while one was open for 1% -> 1% of each run, Pallas kernels for 10% -> 7%
where the time goes in v1:
time: 224 us
  waiting for transfers between devices  113 us (50%)
  starting transfers between devices  64.6 us (29%)
  Pallas kernels  39.1 us (17%)
  local copies, waits for them, and re-layouts  4.22 us (2%)
    ppermute x27, waiting for transfers between devices, pass_seq(): return lax.ppermute(value, 'seq', [(i, i ^ s) for i in range(SEQ)])  97.2 us
    ppermute x27, starting transfers between devices, pass_seq(): return lax.ppermute(value, 'seq', [(i, i ^ s) for i in range(SEQ)])  48.8 us
    pallas_call x18, Pallas kernels, call(): pl.pallas_call(kernel, out_shape=out_shape, in_specs=specs, out_specs=[pl...  39.1 us
    ppermute x17, waiting for transfers between devices, swap(): return lax.ppermute(value, 'dp', [(i, i ^ s * stride) for i in range(dp)])  16.1 us
    ppermute x17, starting transfers between devices, swap(): return lax.ppermute(value, 'dp', [(i, i ^ s * stride) for i in range(dp)])  15.8 us
  transfers between devices with their start and end apart: 44, of which 25 were waited for; matrix products, arithmetic and copies ran while one was open for 1% of the time, Pallas kernels for 7%

profile of v1, /device:TPU:0, one launch (start us, length us, event | category | flops | bytes accessed | tf_op | source)
XLA Modules:
  0.0 223.6 jit_solution(5208333282029125607)
XLA Ops:
  2.0 4.0 %collective-permute-start.5 = (bf16[96,576]{1,0:T(8,128)(2,1)S(1)}, bf16[96,576]{1,0:T(8,128)(2,1)S(1)}, u32[]{:S(2)}, u32[]{:S(2)}) collective-permute-start(bf16[96,576]{1,0:T(8,128)(2,1)S(1)} %pad_maximum_fusion.2.refs_4_), channel_id=1, source_target_pairs={{0,24},{4,28},{8,16},{12,20},{16,8},{20,12},{24,0},{28,4},{1,25},{... | collective-permute-start | bytes 331784 | tf_op jit(solution)/shard_map/ppermute | solution.py:574
  6.6 3.0 %collective-permute-start.1 = (bf16[128,768]{1,0:T(8,128)(2,1)}, bf16[128,768]{1,0:T(8,128)(2,1)S(1)}, u32[]{:S(2)}, u32[]{:S(2)}) collective-permute-start(bf16[128,768]{1,0:T(8,128)(2,1)} %bitcast.16), channel_id=1, source_target_pairs={{0,2},{1,3},{2,0},{3,1},{4,6},{5,7},{6,4},{7,5},{8,10},{9,11},{10,... | collective-permute-start | bytes 589832 | tf_op jit(solution)/shard_map/ppermute | solution.py:577
  15.6 2.6 %collective-permute-done.1.refs_2_.refs_6_.refs_3_ = bf16[128,768]{1,0:T(8,128)(2,1)S(1)} collective-permute-done((bf16[128,768]{1,0:T(8,128)(2,1)}, bf16[128,768]{1,0:T(8,128)(2,1)S(1)}, u32[]{:S(2)}, u32[]{:S(2)}) %collective-permute-start.1) | collective-permute-done | bytes 196640 | tf_op jit(solution)/shard_map/ppermute | solution.py:577
  18.4 2.5 %collective-permute-start.12 = (bf16[400,768]{1,0:T(8,128)(2,1)S(1)}, bf16[400,768]{1,0:T(8,128)(2,1)S(1)}, u32[]{:S(2)}, u32[]{:S(2)}) collective-permute-start(bf16[400,768]{1,0:T(8,128)(2,1)S(1)} %select_units.1.refs_0_), channel_id=1, source_target_pairs={{0,24},{4,28},{8,16},{12,20},{16,8},{20,12},{24,0},{28,4},{1,25},{... | collective-permute-start | bytes 1843208 | tf_op jit(solution)/shard_map/ppermute | solution.py:574
  23.4 4.2 %collective-permute-done.2.refs_3_.refs_7_.refs_4_ = bf16[128,768]{1,0:T(8,128)(2,1)S(1)} collective-permute-done((bf16[128,768]{1,0:T(8,128)(2,1)S(1)}, bf16[128,768]{1,0:T(8,128)(2,1)S(1)}, u32[]{:S(2)}, u32[]{:S(2)}) %collective-permute-start.2) | collective-permute-done | bytes 196640 | tf_op jit(solution)/shard_map/ppermute | solution.py:577
  27.6 6.4 %attention_forward.1 = (bf16[768,128]{1,0:T(8,128)(2,1)S(1)}, bf16[512,192]{1,0:T(8,128)(2,1)S(1)}, bf16[512,192]{1,0:T(8,128)(2,1)S(1)}, bf16[512,192]{1,0:T(8,...) custom-call(s32[12]{0:T(128)S(1)} %pad_add_fusion.ids, s32[1,8]{1,0:T(1,128)S(1)} %copy-done.5, ...), custom_call_target="tpu_custom_call" | custom-call | flops 654311424 | bytes 4915200 | tf_op jit(solution)/shard_map/attention_forward/pallas_call | solution.py:83
  38.1 6.2 %collective-permute-done.8.refs_2_ = bf16[768,128]{1,0:T(8,128)(2,1)S(1)} collective-permute-done((bf16[768,128]{1,0:T(8,128)(2,1)S(1)}, bf16[768,128]{1,0:T(8,128)(2,1)S(1)}, u32[]{:S(2)}, u32[]{:S(2)}) %collective-permute-start.8) | collective-permute-done | bytes 196640 | tf_op jit(solution)/shard_map/ppermute | solution.py:577
  49.5 2.8 %collective-permute-done.13.refs_4_ = bf16[1600,768]{1,0:T(8,128)(2,1)S(1)} collective-permute-done((bf16[1600,768]{1,0:T(8,128)(2,1)S(1)}, bf16[1600,768]{1,0:T(8,128)(2,1)S(1)}, u32[]{:S(2)}, u32[]{:S(2)}) %collective-permute-start.13) | collective-permute-done | bytes 2457632 | tf_op jit(solution)/shard_map/ppermute | solution.py:574
  55.0 4.2 %middle_forward.1 = (f32[128,768]{1,0:T(8,128)S(1)}, bf16[128,768]{1,0:T(8,128)(2,1)S(1)}, bf16[128,768]{1,0:T(8,128)(2,1)S(1)}, bf16[128,768]{1,0:T(8,128)(2,1)...) custom-call(s32[12]{0:T(128)S(1)} %pad_add_fusion.ids, ...), custom_call_target="tpu_custom_call" | custom-call | flops 2415919104 | bytes 9269248 | tf_op jit(solution)/shard_map/middle_forward/pallas_call | solution.py:83
  61.0 3.3 %collective-permute-start.15 = (bf16[128,768]{1,0:T(8,128)(2,1)S(1)}, bf16[128,768]{1,0:T(8,128)(2,1)S(1)}, u32[]{:S(2)}, u32[]{:S(2)}) collective-permute-start(bf16[128,768]{1,0:T(8,128)(2,1)S(1)} %get-tuple-element.103), channel_id=1, source_target_pairs={{0,2},{1,3},{2,0},{3,1},{4,6},{5,7},{6,4},{7,5},{8,10},{9,11},{10,... | collective-permute-start | bytes 589832 | tf_op jit(solution)/shard_map/ppermute | solution.py:577
  64.3 4.7 %collective-permute-done.14.refs_1_ = bf16[128,768]{1,0:T(8,128)(2,1)S(1)} collective-permute-done((bf16[128,768]{1,0:T(8,128)(2,1)S(1)}, bf16[128,768]{1,0:T(8,128)(2,1)S(1)}, u32[]{:S(2)}, u32[]{:S(2)}) %collective-permute-start.14) | collective-permute-done | bytes 196640 | tf_op jit(solution)/shard_map/ppermute | solution.py:577
  69.0 9.4 %collective-permute-done.15.refs_2_ = bf16[128,768]{1,0:T(8,128)(2,1)S(1)} collective-permute-done((bf16[128,768]{1,0:T(8,128)(2,1)S(1)}, bf16[128,768]{1,0:T(8,128)(2,1)S(1)}, u32[]{:S(2)}, u32[]{:S(2)}) %collective-permute-start.15) | collective-permute-done | bytes 196640 | tf_op jit(solution)/shard_map/ppermute | solution.py:577
  79.5 4.6 %collective-permute-start.18 = (bf16[128,768]{1,0:T(8,128)(2,1)S(1)}, bf16[128,768]{1,0:T(8,128)(2,1)S(1)}, u32[]{:S(2)}, u32[]{:S(2)}) collective-permute-start(bf16[128,768]{1,0:T(8,128)(2,1)S(1)} %get-tuple-element.108.refs_1_), channel_id=1, source_target_pairs={{0,2},{1,3},{2,0},{3,1},{4,6},{5,7},{6,4},{7,5},{8,10},{9,11},{10,... | collective-permute-start | bytes 589832 | tf_op jit(solution)/shard_map/ppermute | solution.py:577
  84.1 8.2 %collective-permute-done.18.refs_3_ = bf16[128,768]{1,0:T(8,128)(2,1)S(1)} collective-permute-done((bf16[128,768]{1,0:T(8,128)(2,1)S(1)}, bf16[128,768]{1,0:T(8,128)(2,1)S(1)}, u32[]{:S(2)}, u32[]{:S(2)}) %collective-permute-start.18) | collective-permute-done | bytes 196640 | tf_op jit(solution)/shard_map/ppermute | solution.py:577
  93.0 5.5 %collective-permute-done.19.refs_4_ = bf16[128,768]{1,0:T(8,128)(2,1)S(1)} collective-permute-done((bf16[128,768]{1,0:T(8,128)(2,1)S(1)}, bf16[128,768]{1,0:T(8,128)(2,1)S(1)}, u32[]{:S(2)}, u32[]{:S(2)}) %collective-permute-start.19) | collective-permute-done | bytes 196640 | tf_op jit(solution)/shard_map/ppermute | solution.py:577
  98.4 4.3 %feed_back.1 = (f32[128,768]{1,0:T(8,128)S(1)}, bf16[128,768]{1,0:T(8,128)(2,1)S(1)}, bf16[128,768]{1,0:T(8,128)(2,1)S(1)}, bf16[128,768]{1,0:T(8,128)(2,1)S(1)}...) custom-call(bf16[512,768]{1,0:T(8,128)(2,1)S(1)} %get-tuple-element., ...), custom_call_target="tpu_custom_call" | custom-call | flops 3019898880 | bytes 9240576 | tf_op jit(solution)/shard_map/feed_back/pallas_call | solution.py:83
  102.7 3.1 %feed_weights.1 = (f32[4,3,96,768]{3,2,1,0:T(8,128)S(1)}, bf16[4,3,96,768]{3,2,1,0:T(8,128)(2,1)S(1)}) custom-call(s32[12]{0:T(128)S(1)} %pad_add_fusion.ids, bf16[512,768]{1,0:T(8,128)(2,1)S(1)} %get-tuple-element.105.refs_4_.refs_0_, bf16[512,768]{1,0:T(8,128)(2,1)S(1)} %get-tuple-element.114.refs_1_, bf16[512,768]{1,0:T(8,128)(2,1)S(1)} %get-tuple-element.115.refs_2_, ...), custom_call_target="tpu_custom_call" | custom-call | flops 1811939328 | bytes 9240576 | tf_op jit(solution)/shard_map/feed_weights/pallas_call | solution.py:83
  106.2 7.0 %collective-permute-done.20.refs_1_ = bf16[128,768]{1,0:T(8,128)(2,1)S(1)} collective-permute-done((bf16[128,768]{1,0:T(8,128)(2,1)S(1)}, bf16[128,768]{1,0:T(8,128)(2,1)S(1)}, u32[]{:S(2)}, u32[]{:S(2)}) %collective-permute-start.20) | collective-permute-done | bytes 196640 | tf_op jit(solution)/shard_map/ppermute | solution.py:577
  115.9 2.6 %collective-permute-start.22 = (bf16[128,768]{1,0:T(8,128)(2,1)S(1)}, bf16[128,768]{1,0:T(8,128)(2,1)S(1)}, u32[]{:S(2)}, u32[]{:S(2)}) collective-permute-start(bf16[128,768]{1,0:T(8,128)(2,1)S(1)} %get-tuple-element.112), channel_id=1, source_target_pairs={{0,3},{1,2},{2,1},{3,0},{4,7},{5,6},{6,5},{7,4},{8,11},{9,10},{10,... | collective-permute-start | bytes 589832 | tf_op jit(solution)/shard_map/ppermute | solution.py:577
  118.5 6.8 %collective-permute-done.24.refs_4_ = bf16[2,3,96,384]{3,2,1,0:T(8,128)(2,1)S(1)} collective-permute-done((bf16[2,3,96,384]{3,2,1,0:T(8,128)(2,1)S(1)}, bf16[2,3,96,384]{3,2,1,0:T(8,128)(2,1)S(1)}, u32[]{:S(2)}, u32[]{:S(2)}) %collective-permute-start.24) | collective-permute-done | bytes 442400 | tf_op jit(solution)/shard_map/ppermute | solution.py:574
  132.7 4.7 %collective-permute-start.26 = (bf16[144,384]{1,0:T(8,128)(2,1)S(1)}, bf16[144,384]{1,0:T(8,128)(2,1)S(1)}, u32[]{:S(2)}, u32[]{:S(2)}) collective-permute-start(bf16[144,384]{1,0:T(8,128)(2,1)S(1)} %get-tuple-element.134), channel_id=1, source_target_pairs={{0,1},{1,0},{2,3},{3,2},{4,5},{5,4},{6,7},{7,6},{8,9},{9,8},{10,11... | collective-permute-start | bytes 331784 | tf_op jit(solution)/shard_map/ppermute | solution.py:577
  137.5 2.4 %collective-permute-start.28 = (bf16[144,384]{1,0:T(8,128)(2,1)S(1)}, bf16[144,384]{1,0:T(8,128)(2,1)S(1)}, u32[]{:S(2)}, u32[]{:S(2)}) collective-permute-start(bf16[144,384]{1,0:T(8,128)(2,1)S(1)} %get-tuple-element.136), channel_id=1, source_target_pairs={{0,3},{1,2},{2,1},{3,0},{4,7},{5,6},{6,5},{7,4},{8,11},{9,10},{10,... | collective-permute-start | bytes 331784 | tf_op jit(solution)/shard_map/ppermute | solution.py:577
  140.9 7.2 %collective-permute-done.27.refs_2_.refs_7_.refs_8_ = bf16[144,384]{1,0:T(8,128)(2,1)S(1)} collective-permute-done((bf16[144,384]{1,0:T(8,128)(2,1)S(1)}, bf16[144,384]{1,0:T(8,128)(2,1)S(1)}, u32[]{:S(2)}, u32[]{:S(2)}) %collective-permute-start.27) | collective-permute-done | bytes 110624 | tf_op jit(solution)/shard_map/ppermute | solution.py:577
  148.1 6.0 %attention_back.1 = (f32[128,768]{1,0:T(8,128)S(1)}, bf16[128,768]{1,0:T(8,128)(2,1)S(1)}, bf16[128,768]{1,0:T(8,128)(2,1)S(1)}, bf16[128,768]{1,0:T(8,128)(2,1)S(1)}, bf16[512,576]{1,0:T(8,128)(2,1)S(1)}) custom-call(bf16[144,384]{1,0:T(8,128)(2,1)S(1)} %get-tuple-element.133.refs_0_.refs_6_, ...), custom_call_target="tpu_custom_call" | custom-call | flops 956301312 | bytes 5062656 | tf_op jit(solution)/shard_map/attention_back/pallas_call | solution.py:83
  163.4 24.1 %collective-permute-done.31.refs_2_ = bf16[128,768]{1,0:T(8,128)(2,1)S(1)} collective-permute-done((bf16[128,768]{1,0:T(8,128)(2,1)S(1)}, bf16[128,768]{1,0:T(8,128)(2,1)S(1)}, u32[]{:S(2)}, u32[]{:S(2)}) %collective-permute-start.31) | collective-permute-done | bytes 196640 | tf_op jit(solution)/shard_map/ppermute | solution.py:577
  189.4 4.5 %collective-permute-done.33.refs_4_ = bf16[128,768]{1,0:T(8,128)(2,1)S(1)} collective-permute-done((bf16[128,768]{1,0:T(8,128)(2,1)S(1)}, bf16[128,768]{1,0:T(8,128)(2,1)S(1)}, u32[]{:S(2)}, u32[]{:S(2)}) %collective-permute-start.33) | collective-permute-done | bytes 196640 | tf_op jit(solution)/shard_map/ppermute | solution.py:577
  195.1 2.7 %collective-permute-start.43 = (bf16[3,96,768]{2,1,0:T(8,128)(2,1)S(1)}, bf16[3,96,768]{2,1,0:T(8,128)(2,1)S(1)}, u32[]{:S(2)}, u32[]{:S(2)}) collective-permute-start(bf16[3,96,768]{2,1,0:T(8,128)(2,1)S(1)} %collective-permute-done.39.refs_2_), channel_id=1, source_target_pairs={{0,1},{1,0},{2,3},{3,2},{4,5},{5,4},{6,7},{7,6},{8,9},{9,8},{10,11... | collective-permute-start | bytes 1327112 | tf_op jit(solution)/shard_map/ppermute | solution.py:577
  197.8 2.7 %collective-permute-done.37.refs_3_ = bf16[112,768]{1,0:T(8,128)(2,1)S(1)} collective-permute-done((bf16[112,768]{1,0:T(8,128)(2,1)S(1)}, bf16[112,768]{1,0:T(8,128)(2,1)S(1)}, u32[]{:S(2)}, u32[]{:S(2)}) %collective-permute-start.37) | collective-permute-done | bytes 172064 | tf_op jit(solution)/shard_map/ppermute | solution.py:574
  200.7 3.9 %collective-permute-start.41 = (bf16[112,768]{1,0:T(8,128)(2,1)S(1)}, bf16[112,768]{1,0:T(8,128)(2,1)S(1)}, u32[]{:S(2)}, u32[]{:S(2)}) collective-permute-start(bf16[112,768]{1,0:T(8,128)(2,1)S(1)} %plane_sum.1.refs_0_), channel_id=1, source_target_pairs={{0,2},{1,3},{2,0},{3,1},{4,6},{5,7},{6,4},{7,5},{8,10},{9,11},{10,... | collective-permute-start | bytes 516104 | tf_op jit(solution)/shard_map/ppermute | solution.py:577
  204.6 7.5 %collective-permute-done.41.refs_2_ = bf16[112,768]{1,0:T(8,128)(2,1)S(1)} collective-permute-done((bf16[112,768]{1,0:T(8,128)(2,1)S(1)}, bf16[112,768]{1,0:T(8,128)(2,1)S(1)}, u32[]{:S(2)}, u32[]{:S(2)}) %collective-permute-start.41) | collective-permute-done | bytes 172064 | tf_op jit(solution)/shard_map/ppermute | solution.py:577
  212.1 3.3 %collective-permute-start.42 = (bf16[112,768]{1,0:T(8,128)(2,1)S(1)}, bf16[112,768]{1,0:T(8,128)(2,1)S(1)}, u32[]{:S(2)}, u32[]{:S(2)}) collective-permute-start(bf16[112,768]{1,0:T(8,128)(2,1)S(1)} %collective-permute-done.41.refs_2_), channel_id=1, source_target_pairs={{0,1},{1,0},{2,3},{3,2},{4,5},{5,4},{6,7},{7,6},{8,9},{9,8},{10,11... | collective-permute-start | bytes 516104 | tf_op jit(solution)/shard_map/ppermute | solution.py:577
  216.7 4.5 %feed_final.1 = (f32[96,6144]{1,0:T(8,128)}, f32[384,768]{1,0:T(8,128)}) custom-call(s32[12]{0:T(128)S(1)} %pad_add_fusion.ids, bf16[3,96,768]{2,1,0:T(8,128)(2,1)S(1)} %step_three.1.refs_0_, bf16[3,96,768]{2,1,0:T(8,128)(2,1)S(1)} %collective-permute-done.38.refs_1_, bf16[3,96,768]{2,1,0:T(8,128)(2,1)S(1)} %collective-permute-done.39.refs_2_, ...), custom_call_target="tpu_custom_call" | custom-call | bytes 5308416 | tf_op jit(solution)/shard_map/feed_final/pallas_call | solution.py:83
  (98 shorter events, 53.8 us)
Async XLA Ops:
  2.0 9.9 %collective-permute-start.5 = (bf16[96,576]{1,0:T(8,128)(2,1)S(1)}, bf16[96,576]{1,0:T(8,128)(2,1)S(1)}, u32[]{:S(2)}, u32[]{:S(2)}) collective-permute-start(bf16[96,576]{1,0:T(8,128)(2,1)S(1)} %pad_maximum_fusion.2.refs_4_), channel_id=1, source_target_pairs={{0,24},{4,28},{8,16},{12,20},{16,8},{20,12},{24,0},{28,4},{1,25},{... | collective-permute-start | bytes 331784 | tf_op jit(solution)/shard_map/ppermute | solution.py:574
  6.6 11.6 %collective-permute-start.1 = (bf16[128,768]{1,0:T(8,128)(2,1)}, bf16[128,768]{1,0:T(8,128)(2,1)S(1)}, u32[]{:S(2)}, u32[]{:S(2)}) collective-permute-start(bf16[128,768]{1,0:T(8,128)(2,1)} %bitcast.16), channel_id=1, source_target_pairs={{0,2},{1,3},{2,0},{3,1},{4,6},{5,7},{6,4},{7,5},{8,10},{9,11},{10,... | collective-permute-start | bytes 589832 | tf_op jit(solution)/shard_map/ppermute | solution.py:577
  9.6 8.8 %collective-permute-start = (bf16[128,768]{1,0:T(8,128)(2,1)}, bf16[128,768]{1,0:T(8,128)(2,1)S(1)}, u32[]{:S(2)}, u32[]{:S(2)}) collective-permute-start(bf16[128,768]{1,0:T(8,128)(2,1)} %bitcast.17), channel_id=1, source_target_pairs={{0,1},{1,0},{2,3},{3,2},{4,5},{5,4},{6,7},{7,6},{8,9},{9,8},{10,11... | collective-permute-start | bytes 589832 | tf_op jit(solution)/shard_map/ppermute | solution.py:577
  12.3 15.3 %collective-permute-start.6 = (bf16[384,576]{1,0:T(8,128)(2,1)S(1)}, bf16[384,576]{1,0:T(8,128)(2,1)S(1)}, u32[]{:S(2)}, u32[]{:S(2)}) collective-permute-start(bf16[384,576]{1,0:T(8,128)(2,1)S(1)} %pad_maximum_fusion.1), channel_id=1, source_target_pairs={{0,4},{4,0},{8,12},{12,8},{16,20},{20,16},{24,28},{28,24},{1,5},{5... | collective-permute-start | bytes 1327112 | tf_op jit(solution)/shard_map/ppermute | solution.py:574
  18.4 26.3 %collective-permute-start.12 = (bf16[400,768]{1,0:T(8,128)(2,1)S(1)}, bf16[400,768]{1,0:T(8,128)(2,1)S(1)}, u32[]{:S(2)}, u32[]{:S(2)}) collective-permute-start(bf16[400,768]{1,0:T(8,128)(2,1)S(1)} %select_units.1.refs_0_), channel_id=1, source_target_pairs={{0,24},{4,28},{8,16},{12,20},{16,8},{20,12},{24,0},{28,4},{1,25},{... | collective-permute-start | bytes 1843208 | tf_op jit(solution)/shard_map/ppermute | solution.py:574
  20.9 25.9 %collective-permute-start.11 = (bf16[400,768]{1,0:T(8,128)(2,1)S(1)}, bf16[400,768]{1,0:T(8,128)(2,1)S(1)}, u32[]{:S(2)}, u32[]{:S(2)}) collective-permute-start(bf16[400,768]{1,0:T(8,128)(2,1)S(1)} %select_units.1.refs_0_), channel_id=1, source_target_pairs={{0,16},{4,20},{8,24},{12,28},{16,0},{20,4},{24,8},{28,12},{1,17},{... | collective-permute-start | bytes 1843208 | tf_op jit(solution)/shard_map/ppermute | solution.py:574
  21.4 25.6 %collective-permute-start.10 = (bf16[400,768]{1,0:T(8,128)(2,1)S(1)}, bf16[400,768]{1,0:T(8,128)(2,1)S(1)}, u32[]{:S(2)}, u32[]{:S(2)}) collective-permute-start(bf16[400,768]{1,0:T(8,128)(2,1)S(1)} %select_units.1.refs_0_), channel_id=1, source_target_pairs={{0,8},{4,12},{8,0},{12,4},{16,24},{20,28},{24,16},{28,20},{1,9},{5... | collective-permute-start | bytes 1843208 | tf_op jit(solution)/shard_map/ppermute | solution.py:574
  34.0 10.4 %collective-permute-start.8 = (bf16[768,128]{1,0:T(8,128)(2,1)S(1)}, bf16[768,128]{1,0:T(8,128)(2,1)S(1)}, u32[]{:S(2)}, u32[]{:S(2)}) collective-permute-start(bf16[768,128]{1,0:T(8,128)(2,1)S(1)} %get-tuple-element.91.refs_0_), channel_id=1, source_target_pairs={{0,2},{1,3},{2,0},{3,1},{4,6},{5,7},{6,4},{7,5},{8,10},{9,11},{10,... | collective-permute-start | bytes 589832 | tf_op jit(solution)/shard_map/ppermute | solution.py:577
  59.2 9.8 %collective-permute-start.14 = (bf16[128,768]{1,0:T(8,128)(2,1)S(1)}, bf16[128,768]{1,0:T(8,128)(2,1)S(1)}, u32[]{:S(2)}, u32[]{:S(2)}) collective-permute-start(bf16[128,768]{1,0:T(8,128)(2,1)S(1)} %get-tuple-element.102), channel_id=1, source_target_pairs={{0,1},{1,0},{2,3},{3,2},{4,5},{5,4},{6,7},{7,6},{8,9},{9,8},{10,11... | collective-permute-start | bytes 589832 | tf_op jit(solution)/shard_map/ppermute | solution.py:577
  61.0 17.4 %collective-permute-start.15 = (bf16[128,768]{1,0:T(8,128)(2,1)S(1)}, bf16[128,768]{1,0:T(8,128)(2,1)S(1)}, u32[]{:S(2)}, u32[]{:S(2)}) collective-permute-start(bf16[128,768]{1,0:T(8,128)(2,1)S(1)} %get-tuple-element.103), channel_id=1, source_target_pairs={{0,2},{1,3},{2,0},{3,1},{4,6},{5,7},{6,4},{7,5},{8,10},{9,11},{10,... | collective-permute-start | bytes 589832 | tf_op jit(solution)/shard_map/ppermute | solution.py:577
  64.3 14.2 %collective-permute-start.16 = (bf16[128,768]{1,0:T(8,128)(2,1)S(1)}, bf16[128,768]{1,0:T(8,128)(2,1)S(1)}, u32[]{:S(2)}, u32[]{:S(2)}) collective-permute-start(bf16[128,768]{1,0:T(8,128)(2,1)S(1)} %get-tuple-element.104), channel_id=1, source_target_pairs={{0,3},{1,2},{2,1},{3,0},{4,7},{5,6},{6,5},{7,4},{8,11},{9,10},{10,... | collective-permute-start | bytes 589832 | tf_op jit(solution)/shard_map/ppermute | solution.py:577
  79.5 12.8 %collective-permute-start.18 = (bf16[128,768]{1,0:T(8,128)(2,1)S(1)}, bf16[128,768]{1,0:T(8,128)(2,1)S(1)}, u32[]{:S(2)}, u32[]{:S(2)}) collective-permute-start(bf16[128,768]{1,0:T(8,128)(2,1)S(1)} %get-tuple-element.108.refs_1_), channel_id=1, source_target_pairs={{0,2},{1,3},{2,0},{3,1},{4,6},{5,7},{6,4},{7,5},{8,10},{9,11},{10,... | collective-permute-start | bytes 589832 | tf_op jit(solution)/shard_map/ppermute | solution.py:577
  84.1 8.9 %collective-permute-start.17 = (bf16[128,768]{1,0:T(8,128)(2,1)S(1)}, bf16[128,768]{1,0:T(8,128)(2,1)S(1)}, u32[]{:S(2)}, u32[]{:S(2)}) collective-permute-start(bf16[128,768]{1,0:T(8,128)(2,1)S(1)} %get-tuple-element.108.refs_1_), channel_id=1, source_target_pairs={{0,1},{1,0},{2,3},{3,2},{4,5},{5,4},{6,7},{7,6},{8,9},{9,8},{10,11... | collective-permute-start | bytes 589832 | tf_op jit(solution)/shard_map/ppermute | solution.py:577
  113.6 11.7 %collective-permute-start.24 = (bf16[2,3,96,384]{3,2,1,0:T(8,128)(2,1)S(1)}, bf16[2,3,96,384]{3,2,1,0:T(8,128)(2,1)S(1)}, u32[]{:S(2)}, u32[]{:S(2)}) collective-permute-start(bf16[2,3,96,384]{3,2,1,0:T(8,128)(2,1)S(1)} %get-tuple-element.125), channel_id=1, source_target_pairs={{0,8},{4,12},{8,0},{12,4},{16,24},{20,28},{24,16},{28,20},{1,9},{5... | collective-permute-start | bytes 1327112 | tf_op jit(solution)/shard_map/ppermute | solution.py:574
  115.1 11.4 %collective-permute-start.25 = (bf16[2,3,96,384]{3,2,1,0:T(8,128)(2,1)S(1)}, bf16[2,3,96,384]{3,2,1,0:T(8,128)(2,1)S(1)}, u32[]{:S(2)}, u32[]{:S(2)}) collective-permute-start(bf16[2,3,96,384]{3,2,1,0:T(8,128)(2,1)S(1)} %get-tuple-element.126), channel_id=1, source_target_pairs={{0,16},{4,20},{8,24},{12,28},{16,0},{20,4},{24,8},{28,12},{1,17},{... | collective-permute-start | bytes 1327112 | tf_op jit(solution)/shard_map/ppermute | solution.py:574
  115.9 15.0 %collective-permute-start.21 = (bf16[128,768]{1,0:T(8,128)(2,1)S(1)}, bf16[128,768]{1,0:T(8,128)(2,1)S(1)}, u32[]{:S(2)}, u32[]{:S(2)}) collective-permute-start(bf16[128,768]{1,0:T(8,128)(2,1)S(1)} %get-tuple-element.111), channel_id=1, source_target_pairs={{0,2},{1,3},{2,0},{3,1},{4,6},{5,7},{6,4},{7,5},{8,10},{9,11},{10,... | collective-permute-start | bytes 589832 | tf_op jit(solution)/shard_map/ppermute | solution.py:577
  115.9 14.9 %collective-permute-start.22 = (bf16[128,768]{1,0:T(8,128)(2,1)S(1)}, bf16[128,768]{1,0:T(8,128)(2,1)S(1)}, u32[]{:S(2)}, u32[]{:S(2)}) collective-permute-start(bf16[128,768]{1,0:T(8,128)(2,1)S(1)} %get-tuple-element.112), channel_id=1, source_target_pairs={{0,3},{1,2},{2,1},{3,0},{4,7},{5,6},{6,5},{7,4},{8,11},{9,10},{10,... | collective-permute-start | bytes 589832 | tf_op jit(solution)/shard_map/ppermute | solution.py:577
  126.6 13.3 %collective-permute-start.30 = (bf16[3,96,384]{2,1,0:T(8,128)(2,1)S(1)}, bf16[3,96,384]{2,1,0:T(8,128)(2,1)S(1)}, u32[]{:S(2)}, u32[]{:S(2)}) collective-permute-start(bf16[3,96,384]{2,1,0:T(8,128)(2,1)S(1)} %get-tuple-element.140), channel_id=1, source_target_pairs={{0,8},{4,12},{8,0},{12,4},{16,24},{20,28},{24,16},{28,20},{1,9},{5... | collective-permute-start | bytes 663560 | tf_op jit(solution)/shard_map/ppermute | solution.py:574
  127.3 12.6 %collective-permute-start.29 = (bf16[3,96,384]{2,1,0:T(8,128)(2,1)S(1)}, bf16[3,96,384]{2,1,0:T(8,128)(2,1)S(1)}, u32[]{:S(2)}, u32[]{:S(2)}) collective-permute-start(bf16[3,96,384]{2,1,0:T(8,128)(2,1)S(1)} %get-tuple-element.127), channel_id=1, source_target_pairs={{0,16},{4,20},{8,24},{12,28},{16,0},{20,4},{24,8},{28,12},{1,17},{... | collective-permute-start | bytes 663560 | tf_op jit(solution)/shard_map/ppermute | solution.py:574
  137.4 10.6 %collective-permute-start.27 = (bf16[144,384]{1,0:T(8,128)(2,1)S(1)}, bf16[144,384]{1,0:T(8,128)(2,1)S(1)}, u32[]{:S(2)}, u32[]{:S(2)}) collective-permute-start(bf16[144,384]{1,0:T(8,128)(2,1)S(1)} %get-tuple-element.135), channel_id=1, source_target_pairs={{0,2},{1,3},{2,0},{3,1},{4,6},{5,7},{6,4},{7,5},{8,10},{9,11},{10,... | collective-permute-start | bytes 331784 | tf_op jit(solution)/shard_map/ppermute | solution.py:577
  137.5 10.6 %collective-permute-start.28 = (bf16[144,384]{1,0:T(8,128)(2,1)S(1)}, bf16[144,384]{1,0:T(8,128)(2,1)S(1)}, u32[]{:S(2)}, u32[]{:S(2)}) collective-permute-start(bf16[144,384]{1,0:T(8,128)(2,1)S(1)} %get-tuple-element.136), channel_id=1, source_target_pairs={{0,3},{1,2},{2,1},{3,0},{4,7},{5,6},{6,5},{7,4},{8,11},{9,10},{10,... | collective-permute-start | bytes 331784 | tf_op jit(solution)/shard_map/ppermute | solution.py:577
  156.1 39.0 %collective-permute-start.39 = (bf16[3,96,768]{2,1,0:T(8,128)(2,1)S(1)}, bf16[3,96,768]{2,1,0:T(8,128)(2,1)S(1)}, u32[]{:S(2)}, u32[]{:S(2)}) collective-permute-start(bf16[3,96,768]{2,1,0:T(8,128)(2,1)S(1)} %step_three.1.refs_0_), channel_id=1, source_target_pairs={{0,2},{1,3},{2,0},{3,1},{4,6},{5,7},{6,4},{7,5},{8,10},{9,11},{10,... | collective-permute-start | bytes 1327112 | tf_op jit(solution)/shard_map/ppermute | solution.py:577
  158.0 39.8 %collective-permute-start.38 = (bf16[3,96,768]{2,1,0:T(8,128)(2,1)S(1)}, bf16[3,96,768]{2,1,0:T(8,128)(2,1)S(1)}, u32[]{:S(2)}, u32[]{:S(2)}) collective-permute-start(bf16[3,96,768]{2,1,0:T(8,128)(2,1)S(1)} %step_three.1.refs_0_), channel_id=1, source_target_pairs={{0,1},{1,0},{2,3},{3,2},{4,5},{5,4},{6,7},{7,6},{8,9},{9,8},{10,11... | collective-permute-start | bytes 1327112 | tf_op jit(solution)/shard_map/ppermute | solution.py:577
  158.8 28.7 %collective-permute-start.31 = (bf16[128,768]{1,0:T(8,128)(2,1)S(1)}, bf16[128,768]{1,0:T(8,128)(2,1)S(1)}, u32[]{:S(2)}, u32[]{:S(2)}) collective-permute-start(bf16[128,768]{1,0:T(8,128)(2,1)S(1)} %get-tuple-element.147), channel_id=1, source_target_pairs={{0,1},{1,0},{2,3},{3,2},{4,5},{5,4},{6,7},{7,6},{8,9},{9,8},{10,11... | collective-permute-start | bytes 589832 | tf_op jit(solution)/shard_map/ppermute | solution.py:577
  160.1 28.7 %collective-permute-start.32 = (bf16[128,768]{1,0:T(8,128)(2,1)S(1)}, bf16[128,768]{1,0:T(8,128)(2,1)S(1)}, u32[]{:S(2)}, u32[]{:S(2)}) collective-permute-start(bf16[128,768]{1,0:T(8,128)(2,1)S(1)} %get-tuple-element.148), channel_id=1, source_target_pairs={{0,2},{1,3},{2,0},{3,1},{4,6},{5,7},{6,4},{7,5},{8,10},{9,11},{10,... | collective-permute-start | bytes 589832 | tf_op jit(solution)/shard_map/ppermute | solution.py:577
  161.7 32.2 %collective-permute-start.33 = (bf16[128,768]{1,0:T(8,128)(2,1)S(1)}, bf16[128,768]{1,0:T(8,128)(2,1)S(1)}, u32[]{:S(2)}, u32[]{:S(2)}) collective-permute-start(bf16[128,768]{1,0:T(8,128)(2,1)S(1)} %get-tuple-element.149), channel_id=1, source_target_pairs={{0,3},{1,2},{2,1},{3,0},{4,7},{5,6},{6,5},{7,4},{8,11},{9,10},{10,... | collective-permute-start | bytes 589832 | tf_op jit(solution)/shard_map/ppermute | solution.py:577
  187.5 10.3 %collective-permute-start.35 = (bf16[112,768]{1,0:T(8,128)(2,1)S(1)}, bf16[112,768]{1,0:T(8,128)(2,1)S(1)}, u32[]{:S(2)}, u32[]{:S(2)}) collective-permute-start(bf16[112,768]{1,0:T(8,128)(2,1)S(1)} %get-tuple-element.157), channel_id=1, source_target_pairs={{0,8},{4,12},{8,0},{12,4},{16,24},{20,28},{24,16},{28,20},{1,9},{5... | collective-permute-start | bytes 516104 | tf_op jit(solution)/shard_map/ppermute | solution.py:574
  188.7 9.1 %collective-permute-start.36 = (bf16[112,768]{1,0:T(8,128)(2,1)S(1)}, bf16[112,768]{1,0:T(8,128)(2,1)S(1)}, u32[]{:S(2)}, u32[]{:S(2)}) collective-permute-start(bf16[112,768]{1,0:T(8,128)(2,1)S(1)} %get-tuple-element.158), channel_id=1, source_target_pairs={{0,16},{4,20},{8,24},{12,28},{16,0},{20,4},{24,8},{28,12},{1,17},{... | collective-permute-start | bytes 516104 | tf_op jit(solution)/shard_map/ppermute | solution.py:574
  195.1 21.5 %collective-permute-start.43 = (bf16[3,96,768]{2,1,0:T(8,128)(2,1)S(1)}, bf16[3,96,768]{2,1,0:T(8,128)(2,1)S(1)}, u32[]{:S(2)}, u32[]{:S(2)}) collective-permute-start(bf16[3,96,768]{2,1,0:T(8,128)(2,1)S(1)} %collective-permute-done.39.refs_2_), channel_id=1, source_target_pairs={{0,1},{1,0},{2,3},{3,2},{4,5},{5,4},{6,7},{7,6},{8,9},{9,8},{10,11... | collective-permute-start | bytes 1327112 | tf_op jit(solution)/shard_map/ppermute | solution.py:577
  200.7 11.4 %collective-permute-start.41 = (bf16[112,768]{1,0:T(8,128)(2,1)S(1)}, bf16[112,768]{1,0:T(8,128)(2,1)S(1)}, u32[]{:S(2)}, u32[]{:S(2)}) collective-permute-start(bf16[112,768]{1,0:T(8,128)(2,1)S(1)} %plane_sum.1.refs_0_), channel_id=1, source_target_pairs={{0,2},{1,3},{2,0},{3,1},{4,6},{5,7},{6,4},{7,5},{8,10},{9,11},{10,... | collective-permute-start | bytes 516104 | tf_op jit(solution)/shard_map/ppermute | solution.py:577
  204.6 16.6 %collective-permute-start.40 = (bf16[112,768]{1,0:T(8,128)(2,1)S(1)}, bf16[112,768]{1,0:T(8,128)(2,1)S(1)}, u32[]{:S(2)}, u32[]{:S(2)}) collective-permute-start(bf16[112,768]{1,0:T(8,128)(2,1)S(1)} %plane_sum.1.refs_0_), channel_id=1, source_target_pairs={{0,1},{1,0},{2,3},{3,2},{4,5},{5,4},{6,7},{7,6},{8,9},{9,8},{10,11... | collective-permute-start | bytes 516104 | tf_op jit(solution)/shard_map/ppermute | solution.py:577
  212.1 9.1 %collective-permute-start.42 = (bf16[112,768]{1,0:T(8,128)(2,1)S(1)}, bf16[112,768]{1,0:T(8,128)(2,1)S(1)}, u32[]{:S(2)}, u32[]{:S(2)}) collective-permute-start(bf16[112,768]{1,0:T(8,128)(2,1)S(1)} %collective-permute-done.41.refs_2_), channel_id=1, source_target_pairs={{0,1},{1,0},{2,3},{3,2},{4,5},{5,4},{6,7},{7,6},{8,9},{9,8},{10,11... | collective-permute-start | bytes 516104 | tf_op jit(solution)/shard_map/ppermute | solution.py:577
  (19 other events, 197.1 us)

commit v2 on v1

--- a/solution.py
+++ b/solution.py
@@ -731,25 +731,6 @@
         return call(pair_sum, [(shape, F32)] + [(shape, BF16)] * 3, [], keep, swap(send, 1))
 
     half_shape = (3, shard, model // 2)
-    *feed_pieces, to_x, to_y = call(
-        step_one,
-        [(half_shape, F32)] * 4 + [((2,) + half_shape, BF16)] * 2,
-        [],
-        after(feed_keep, back_parts[1]),
-        swap(feed_send, 1),
-        mib=10,
-    )
-    left, right, to_y, to_x = call(
-        step_two,
-        [(half_shape, F32)] * 2 + [(half_shape, BF16)] * 2,
-        [],
-        *feed_pieces,
-        swap(to_x, 2),
-        swap(to_y, 4),
-        mib=10,
-    )
-    grad_second = after(grad_second, to_y)
-
     grad_first, *projected = call(
         project_back,
         [((rows, model), F32)]
@@ -767,11 +748,29 @@
         flops=4 * rows * model * model,
     )
     grad_attn = reduce_seq(projected[0:4])
+    *feed_pieces, to_x, to_y = call(
+        step_one,
+        [(half_shape, F32)] * 4 + [((2,) + half_shape, BF16)] * 2,
+        [],
+        after(feed_keep, grad_first),
+        swap(feed_send, 1),
+        mib=10,
+    )
+    left, right, to_y, to_x = call(
+        step_two,
+        [(half_shape, F32)] * 2 + [(half_shape, BF16)] * 2,
+        [],
+        *after(feed_pieces, grad_attn),
+        swap(to_x, 2),
+        swap(to_y, 4),
+        mib=10,
+    )
+
     sums = projected[4]
     (feed_share,) = call(
         step_three, [((3, shard, model), BF16)], [], left, right, swap(to_y, 4), swap(to_x, 2)
     )
-    queries = after(queries, feed_share)
+    sums = after(sums, feed_share)
     feed_blocks = gather_seq(after(feed_share, grad_attn))
 
     *input_parts, grad_qkv = call(
@@ -824,14 +823,6 @@
     attn_pieces = [attn_pieces[0]] + [swap(attn_pieces[t], 2 * t) for t in range(1, CHIPS)]
     attn_pieces = after(attn_pieces, input_parts, feed_blocks[1:3])
     (attn_share,) = call(plane_sum, [((shard + PAD, model), BF16)], [], *attn_pieces)
-    grad_qkv_w, grad_out_w, vector_grads = call(
-        attention_final,
-        [((shard, 3 * model), F32), ((shard, model), F32), ((8, 128), F32)],
-        [ids],
-        *gather_seq(attn_share),
-        scratch=[((SEQ, shard + PAD, model), F32)],
-    )
-
     input_grad, means = call(
         input_final,
         [((rows, model), BF16), ((8, 128), F32)],
@@ -841,6 +832,19 @@
         stats2,
         *grad_attn[1:],
     )
+    attn_near = pass_seq(attn_share, 1)
+    attn_far = after(pass_seq(attn_share, 2), grad_gate_up_w, input_grad)
+    grad_qkv_w, grad_out_w, vector_grads = call(
+        attention_final,
+        [((shard, 3 * model), F32), ((shard, model), F32), ((8, 128), F32)],
+        [ids],
+        attn_share,
+        attn_near,
+        attn_far,
+        pass_seq(attn_far, 1),
+        scratch=[((SEQ, shard + PAD, model), F32)],
+    )
+
     vector_grads = [scatter_outer(vector_grads[n, :shard]) for n in range(4)]
     return (
         output[None],

time: 224 us -> 214 us (0.955)
  waiting for transfers between devices: 113 us -> 108 us
  starting transfers between devices: 64.6 us -> 60 us
    ppermute x17, waiting for transfers between devices: 16.1 us -> 10.1 us  [swap(): return lax.ppermute(value, 'dp', [(i, i ^ s * stride) for i in range(dp)])]
    ppermute x27, starting transfers between devices: 48.8 us -> 43.6 us  [pass_seq(): return lax.ppermute(value, 'seq', [(i, i ^ s) for i in range(SEQ)])]
  transfers between devices with their start and end apart: 44 -> 44, of which waited for: 25 -> 26; matrix products, arithmetic and copies ran while one was open for 1% -> 1% of each run, Pallas kernels for 7% -> 10%
where the time goes in v2:
time: 214 us
  waiting for transfers between devices  108 us (50%)
  starting transfers between devices  60 us (28%)
  Pallas kernels  39.1 us (18%)
  local copies, waits for them, and re-layouts  4.22 us (2%)
    ppermute x27, waiting for transfers between devices, pass_seq(): return lax.ppermute(value, 'seq', [(i, i ^ s) for i in range(SEQ)])  98.4 us
    ppermute x27, starting transfers between devices, pass_seq(): return lax.ppermute(value, 'seq', [(i, i ^ s) for i in range(SEQ)])  43.6 us
    pallas_call x18, Pallas kernels, call(): pl.pallas_call(kernel, out_shape=out_shape, in_specs=specs, out_specs=[pl...  39.1 us
    ppermute x17, starting transfers between devices, swap(): return lax.ppermute(value, 'dp', [(i, i ^ s * stride) for i in range(dp)])  16.4 us
    ppermute x17, waiting for transfers between devices, swap(): return lax.ppermute(value, 'dp', [(i, i ^ s * stride) for i in range(dp)])  10.1 us
  transfers between devices with their start and end apart: 44, of which 26 were waited for; matrix products, arithmetic and copies ran while one was open for 1% of the time, Pallas kernels for 10%

profile of v2, /device:TPU:0, one launch (start us, length us, event | category | flops | bytes accessed | tf_op | source)
XLA Modules:
  0.0 214.1 jit_solution(2631831260980024710)
XLA Ops:
  2.0 4.0 %collective-permute-start.5 = (bf16[96,576]{1,0:T(8,128)(2,1)S(1)}, bf16[96,576]{1,0:T(8,128)(2,1)S(1)}, u32[]{:S(2)}, u32[]{:S(2)}) collective-permute-start(bf16[96,576]{1,0:T(8,128)(2,1)S(1)} %pad_maximum_fusion.2.refs_4_), channel_id=1, source_target_pairs={{0,24},{4,28},{8,16},{12,20},{16,8},{20,12},{24,0},{28,4},{1,25},{... | collective-permute-start | bytes 331784 | tf_op jit(solution)/shard_map/ppermute | solution.py:574
  6.6 3.0 %collective-permute-start.1 = (bf16[128,768]{1,0:T(8,128)(2,1)}, bf16[128,768]{1,0:T(8,128)(2,1)S(1)}, u32[]{:S(2)}, u32[]{:S(2)}) collective-permute-start(bf16[128,768]{1,0:T(8,128)(2,1)} %bitcast.16), channel_id=1, source_target_pairs={{0,2},{1,3},{2,0},{3,1},{4,6},{5,7},{6,4},{7,5},{8,10},{9,11},{10,... | collective-permute-start | bytes 589832 | tf_op jit(solution)/shard_map/ppermute | solution.py:577
  15.6 2.6 %collective-permute-done.1.refs_2_.refs_6_.refs_3_ = bf16[128,768]{1,0:T(8,128)(2,1)S(1)} collective-permute-done((bf16[128,768]{1,0:T(8,128)(2,1)}, bf16[128,768]{1,0:T(8,128)(2,1)S(1)}, u32[]{:S(2)}, u32[]{:S(2)}) %collective-permute-start.1) | collective-permute-done | bytes 196640 | tf_op jit(solution)/shard_map/ppermute | solution.py:577
  18.4 2.5 %collective-permute-start.12 = (bf16[400,768]{1,0:T(8,128)(2,1)S(1)}, bf16[400,768]{1,0:T(8,128)(2,1)S(1)}, u32[]{:S(2)}, u32[]{:S(2)}) collective-permute-start(bf16[400,768]{1,0:T(8,128)(2,1)S(1)} %select_units.1.refs_0_), channel_id=1, source_target_pairs={{0,24},{4,28},{8,16},{12,20},{16,8},{20,12},{24,0},{28,4},{1,25},{... | collective-permute-start | bytes 1843208 | tf_op jit(solution)/shard_map/ppermute | solution.py:574
  23.4 4.2 %collective-permute-done.2.refs_3_.refs_7_.refs_4_ = bf16[128,768]{1,0:T(8,128)(2,1)S(1)} collective-permute-done((bf16[128,768]{1,0:T(8,128)(2,1)S(1)}, bf16[128,768]{1,0:T(8,128)(2,1)S(1)}, u32[]{:S(2)}, u32[]{:S(2)}) %collective-permute-start.2) | collective-permute-done | bytes 196640 | tf_op jit(solution)/shard_map/ppermute | solution.py:577
  27.6 6.4 %attention_forward.1 = (bf16[768,128]{1,0:T(8,128)(2,1)S(1)}, bf16[512,192]{1,0:T(8,128)(2,1)S(1)}, bf16[512,192]{1,0:T(8,128)(2,1)S(1)}, bf16[512,192]{1,0:T(8,...) custom-call(s32[12]{0:T(128)S(1)} %pad_add_fusion.ids, s32[1,8]{1,0:T(1,128)S(1)} %copy-done.5, ...), custom_call_target="tpu_custom_call" | custom-call | flops 654311424 | bytes 4915200 | tf_op jit(solution)/shard_map/attention_forward/pallas_call | solution.py:83
  34.0 2.4 %collective-permute-start.8 = (bf16[768,128]{1,0:T(8,128)(2,1)S(1)}, bf16[768,128]{1,0:T(8,128)(2,1)S(1)}, u32[]{:S(2)}, u32[]{:S(2)}) collective-permute-start(bf16[768,128]{1,0:T(8,128)(2,1)S(1)} %get-tuple-element.95.refs_0_), channel_id=1, source_target_pairs={{0,2},{1,3},{2,0},{3,1},{4,6},{5,7},{6,4},{7,5},{8,10},{9,11},{10,... | collective-permute-start | bytes 589832 | tf_op jit(solution)/shard_map/ppermute | solution.py:577
  38.1 6.2 %collective-permute-done.8.refs_2_ = bf16[768,128]{1,0:T(8,128)(2,1)S(1)} collective-permute-done((bf16[768,128]{1,0:T(8,128)(2,1)S(1)}, bf16[768,128]{1,0:T(8,128)(2,1)S(1)}, u32[]{:S(2)}, u32[]{:S(2)}) %collective-permute-start.8) | collective-permute-done | bytes 196640 | tf_op jit(solution)/shard_map/ppermute | solution.py:577
  49.5 2.8 %collective-permute-done.13.refs_4_ = bf16[1600,768]{1,0:T(8,128)(2,1)S(1)} collective-permute-done((bf16[1600,768]{1,0:T(8,128)(2,1)S(1)}, bf16[1600,768]{1,0:T(8,128)(2,1)S(1)}, u32[]{:S(2)}, u32[]{:S(2)}) %collective-permute-start.13) | collective-permute-done | bytes 2457632 | tf_op jit(solution)/shard_map/ppermute | solution.py:574
  55.0 4.2 %middle_forward.1 = (f32[128,768]{1,0:T(8,128)S(1)}, bf16[128,768]{1,0:T(8,128)(2,1)S(1)}, bf16[128,768]{1,0:T(8,128)(2,1)S(1)}, bf16[128,768]{1,0:T(8,128)(2,1)...) custom-call(s32[12]{0:T(128)S(1)} %pad_add_fusion.ids, ...), custom_call_target="tpu_custom_call" | custom-call | flops 2415919104 | bytes 9269248 | tf_op jit(solution)/shard_map/middle_forward/pallas_call | solution.py:83
  61.0 3.3 %collective-permute-start.15 = (bf16[128,768]{1,0:T(8,128)(2,1)S(1)}, bf16[128,768]{1,0:T(8,128)(2,1)S(1)}, u32[]{:S(2)}, u32[]{:S(2)}) collective-permute-start(bf16[128,768]{1,0:T(8,128)(2,1)S(1)} %get-tuple-element.107), channel_id=1, source_target_pairs={{0,2},{1,3},{2,0},{3,1},{4,6},{5,7},{6,4},{7,5},{8,10},{9,11},{10,... | collective-permute-start | bytes 589832 | tf_op jit(solution)/shard_map/ppermute | solution.py:577
  64.3 4.7 %collective-permute-done.14.refs_1_ = bf16[128,768]{1,0:T(8,128)(2,1)S(1)} collective-permute-done((bf16[128,768]{1,0:T(8,128)(2,1)S(1)}, bf16[128,768]{1,0:T(8,128)(2,1)S(1)}, u32[]{:S(2)}, u32[]{:S(2)}) %collective-permute-start.14) | collective-permute-done | bytes 196640 | tf_op jit(solution)/shard_map/ppermute | solution.py:577
  69.0 9.5 %collective-permute-done.15.refs_2_ = bf16[128,768]{1,0:T(8,128)(2,1)S(1)} collective-permute-done((bf16[128,768]{1,0:T(8,128)(2,1)S(1)}, bf16[128,768]{1,0:T(8,128)(2,1)S(1)}, u32[]{:S(2)}, u32[]{:S(2)}) %collective-permute-start.15) | collective-permute-done | bytes 196640 | tf_op jit(solution)/shard_map/ppermute | solution.py:577
  79.5 4.6 %collective-permute-start.18 = (bf16[128,768]{1,0:T(8,128)(2,1)S(1)}, bf16[128,768]{1,0:T(8,128)(2,1)S(1)}, u32[]{:S(2)}, u32[]{:S(2)}) collective-permute-start(bf16[128,768]{1,0:T(8,128)(2,1)S(1)} %get-tuple-element.112.refs_1_), channel_id=1, source_target_pairs={{0,2},{1,3},{2,0},{3,1},{4,6},{5,7},{6,4},{7,5},{8,10},{9,11},{10,... | collective-permute-start | bytes 589832 | tf_op jit(solution)/shard_map/ppermute | solution.py:577
  84.1 8.2 %collective-permute-done.18.refs_3_ = bf16[128,768]{1,0:T(8,128)(2,1)S(1)} collective-permute-done((bf16[128,768]{1,0:T(8,128)(2,1)S(1)}, bf16[128,768]{1,0:T(8,128)(2,1)S(1)}, u32[]{:S(2)}, u32[]{:S(2)}) %collective-permute-start.18) | collective-permute-done | bytes 196640 | tf_op jit(solution)/shard_map/ppermute | solution.py:577
  93.0 5.5 %collective-permute-done.19.refs_4_ = bf16[128,768]{1,0:T(8,128)(2,1)S(1)} collective-permute-done((bf16[128,768]{1,0:T(8,128)(2,1)S(1)}, bf16[128,768]{1,0:T(8,128)(2,1)S(1)}, u32[]{:S(2)}, u32[]{:S(2)}) %collective-permute-start.19) | collective-permute-done | bytes 196640 | tf_op jit(solution)/shard_map/ppermute | solution.py:577
  98.4 4.3 %feed_back.1 = (f32[128,768]{1,0:T(8,128)S(1)}, bf16[128,768]{1,0:T(8,128)(2,1)S(1)}, bf16[128,768]{1,0:T(8,128)(2,1)S(1)}, bf16[128,768]{1,0:T(8,128)(2,1)S(1)}...) custom-call(bf16[512,768]{1,0:T(8,128)(2,1)S(1)} %get-tuple-element., ...), custom_call_target="tpu_custom_call" | custom-call | flops 3019898880 | bytes 9240576 | tf_op jit(solution)/shard_map/feed_back/pallas_call | solution.py:83
  102.8 3.0 %feed_weights.1 = (f32[4,3,96,768]{3,2,1,0:T(8,128)S(1)}, bf16[4,3,96,768]{3,2,1,0:T(8,128)(2,1)S(1)}) custom-call(s32[12]{0:T(128)S(1)} %pad_add_fusion.ids, bf16[512,768]{1,0:T(8,128)(2,1)S(1)} %get-tuple-element.109.refs_4_.refs_0_, bf16[512,768]{1,0:T(8,128)(2,1)S(1)} %get-tuple-element.139.refs_1_, bf16[512,768]{1,0:T(8,128)(2,1)S(1)} %get-tuple-element.140.refs_2_, ...), custom_call_target="tpu_custom_call" | custom-call | flops 1811939328 | bytes 9240576 | tf_op jit(solution)/shard_map/feed_weights/pallas_call | solution.py:83
  106.8 3.6 %collective-permute-start.22 = (bf16[128,768]{1,0:T(8,128)(2,1)S(1)}, bf16[128,768]{1,0:T(8,128)(2,1)S(1)}, u32[]{:S(2)}, u32[]{:S(2)}) collective-permute-start(bf16[128,768]{1,0:T(8,128)(2,1)S(1)} %get-tuple-element.116), channel_id=1, source_target_pairs={{0,3},{1,2},{2,1},{3,0},{4,7},{5,6},{6,5},{7,4},{8,11},{9,10},{10,... | collective-permute-start | bytes 589832 | tf_op jit(solution)/shard_map/ppermute | solution.py:577
  110.4 5.7 %collective-permute-done.20.refs_1_ = bf16[128,768]{1,0:T(8,128)(2,1)S(1)} collective-permute-done((bf16[128,768]{1,0:T(8,128)(2,1)S(1)}, bf16[128,768]{1,0:T(8,128)(2,1)S(1)}, u32[]{:S(2)}, u32[]{:S(2)}) %collective-permute-start.20) | collective-permute-done | bytes 196640 | tf_op jit(solution)/shard_map/ppermute | solution.py:577
  116.0 7.4 %collective-permute-done.21.refs_2_ = bf16[128,768]{1,0:T(8,128)(2,1)S(1)} collective-permute-done((bf16[128,768]{1,0:T(8,128)(2,1)S(1)}, bf16[128,768]{1,0:T(8,128)(2,1)S(1)}, u32[]{:S(2)}, u32[]{:S(2)}) %collective-permute-start.21) | collective-permute-done | bytes 196640 | tf_op jit(solution)/shard_map/ppermute | solution.py:577
  127.9 4.0 %collective-permute-start.23 = (bf16[144,384]{1,0:T(8,128)(2,1)S(1)}, bf16[144,384]{1,0:T(8,128)(2,1)S(1)}, u32[]{:S(2)}, u32[]{:S(2)}) collective-permute-start(bf16[144,384]{1,0:T(8,128)(2,1)S(1)} %get-tuple-element.123), channel_id=1, source_target_pairs={{0,1},{1,0},{2,3},{3,2},{4,5},{5,4},{6,7},{7,6},{8,9},{9,8},{10,11... | collective-permute-start | bytes 331784 | tf_op jit(solution)/shard_map/ppermute | solution.py:577
  131.9 2.4 %collective-permute-start.25 = (bf16[144,384]{1,0:T(8,128)(2,1)S(1)}, bf16[144,384]{1,0:T(8,128)(2,1)S(1)}, u32[]{:S(2)}, u32[]{:S(2)}) collective-permute-start(bf16[144,384]{1,0:T(8,128)(2,1)S(1)} %get-tuple-element.125), channel_id=1, source_target_pairs={{0,3},{1,2},{2,1},{3,0},{4,7},{5,6},{6,5},{7,4},{8,11},{9,10},{10,... | collective-permute-start | bytes 331784 | tf_op jit(solution)/shard_map/ppermute | solution.py:577
  135.4 6.6 %collective-permute-done.24.refs_2_.refs_7_.refs_8_ = bf16[144,384]{1,0:T(8,128)(2,1)S(1)} collective-permute-done((bf16[144,384]{1,0:T(8,128)(2,1)S(1)}, bf16[144,384]{1,0:T(8,128)(2,1)S(1)}, u32[]{:S(2)}, u32[]{:S(2)}) %collective-permute-start.24) | collective-permute-done | bytes 110624 | tf_op jit(solution)/shard_map/ppermute | solution.py:577
  144.1 6.0 %attention_back.1 = (f32[128,768]{1,0:T(8,128)S(1)}, bf16[128,768]{1,0:T(8,128)(2,1)S(1)}, bf16[128,768]{1,0:T(8,128)(2,1)S(1)}, bf16[128,768]{1,0:T(8,128)(2,1)S(1)}, bf16[512,576]{1,0:T(8,128)(2,1)S(1)}) custom-call(bf16[144,384]{1,0:T(8,128)(2,1)S(1)} %get-tuple-element.122.refs_0_.refs_6_, ...), custom_call_target="tpu_custom_call" | custom-call | flops 956301312 | bytes 5062656 | tf_op jit(solution)/shard_map/attention_back/pallas_call | solution.py:83
  157.3 18.6 %collective-permute-done.39.refs_2_ = bf16[3,96,768]{2,1,0:T(8,128)(2,1)S(1)} collective-permute-done((bf16[3,96,768]{2,1,0:T(8,128)(2,1)S(1)}, bf16[3,96,768]{2,1,0:T(8,128)(2,1)S(1)}, u32[]{:S(2)}, u32[]{:S(2)}) %collective-permute-start.39) | collective-permute-done | bytes 442400 | tf_op jit(solution)/shard_map/ppermute | solution.py:577
  177.7 6.4 %collective-permute-done.26.refs_2_ = bf16[128,768]{1,0:T(8,128)(2,1)S(1)} collective-permute-done((bf16[128,768]{1,0:T(8,128)(2,1)S(1)}, bf16[128,768]{1,0:T(8,128)(2,1)S(1)}, u32[]{:S(2)}, u32[]{:S(2)}) %collective-permute-start.26) | collective-permute-done | bytes 196640 | tf_op jit(solution)/shard_map/ppermute | solution.py:577
  186.2 3.7 %collective-permute-done.28.refs_4_ = bf16[128,768]{1,0:T(8,128)(2,1)S(1)} collective-permute-done((bf16[128,768]{1,0:T(8,128)(2,1)S(1)}, bf16[128,768]{1,0:T(8,128)(2,1)S(1)}, u32[]{:S(2)}, u32[]{:S(2)}) %collective-permute-start.28) | collective-permute-done | bytes 196640 | tf_op jit(solution)/shard_map/ppermute | solution.py:577
  191.5 4.7 %collective-permute-done.37.refs_3_ = bf16[112,768]{1,0:T(8,128)(2,1)S(1)} collective-permute-done((bf16[112,768]{1,0:T(8,128)(2,1)S(1)}, bf16[112,768]{1,0:T(8,128)(2,1)S(1)}, u32[]{:S(2)}, u32[]{:S(2)}) %collective-permute-start.37) | collective-permute-done | bytes 172064 | tf_op jit(solution)/shard_map/ppermute | solution.py:574
  196.3 3.5 %collective-permute-start.41 = (bf16[112,768]{1,0:T(8,128)(2,1)S(1)}, bf16[112,768]{1,0:T(8,128)(2,1)S(1)}, u32[]{:S(2)}, u32[]{:S(2)}) collective-permute-start(bf16[112,768]{1,0:T(8,128)(2,1)S(1)} %plane_sum.1.refs_0_), channel_id=1, source_target_pairs={{0,2},{1,3},{2,0},{3,1},{4,6},{5,7},{6,4},{7,5},{8,10},{9,11},{10,... | collective-permute-start | bytes 516104 | tf_op jit(solution)/shard_map/ppermute | solution.py:577
  200.6 4.5 %feed_final.1 = (f32[96,6144]{1,0:T(8,128)}, f32[384,768]{1,0:T(8,128)}) custom-call(s32[12]{0:T(128)S(1)} %pad_add_fusion.ids, bf16[3,96,768]{2,1,0:T(8,128)(2,1)S(1)} %step_three.1.refs_0_, bf16[3,96,768]{2,1,0:T(8,128)(2,1)S(1)} %collective-permute-done.38.refs_1_, bf16[3,96,768]{2,1,0:T(8,128)(2,1)S(1)} %collective-permute-done.39.refs_2_, ...), custom_call_target="tpu_custom_call" | custom-call | bytes 5308416 | tf_op jit(solution)/shard_map/feed_final/pallas_call | solution.py:83
  208.0 3.8 %collective-permute-done.43.refs_3_ = bf16[112,768]{1,0:T(8,128)(2,1)S(1)} collective-permute-done((bf16[112,768]{1,0:T(8,128)(2,1)S(1)}, bf16[112,768]{1,0:T(8,128)(2,1)S(1)}, u32[]{:S(2)}, u32[]{:S(2)}) %collective-permute-start.43) | collective-permute-done | bytes 172064 | tf_op jit(solution)/shard_map/ppermute | solution.py:577
  (98 shorter events, 51.2 us)
Async XLA Ops:
  2.0 9.9 %collective-permute-start.5 = (bf16[96,576]{1,0:T(8,128)(2,1)S(1)}, bf16[96,576]{1,0:T(8,128)(2,1)S(1)}, u32[]{:S(2)}, u32[]{:S(2)}) collective-permute-start(bf16[96,576]{1,0:T(8,128)(2,1)S(1)} %pad_maximum_fusion.2.refs_4_), channel_id=1, source_target_pairs={{0,24},{4,28},{8,16},{12,20},{16,8},{20,12},{24,0},{28,4},{1,25},{... | collective-permute-start | bytes 331784 | tf_op jit(solution)/shard_map/ppermute | solution.py:574
  6.6 11.6 %collective-permute-start.1 = (bf16[128,768]{1,0:T(8,128)(2,1)}, bf16[128,768]{1,0:T(8,128)(2,1)S(1)}, u32[]{:S(2)}, u32[]{:S(2)}) collective-permute-start(bf16[128,768]{1,0:T(8,128)(2,1)} %bitcast.16), channel_id=1, source_target_pairs={{0,2},{1,3},{2,0},{3,1},{4,6},{5,7},{6,4},{7,5},{8,10},{9,11},{10,... | collective-permute-start | bytes 589832 | tf_op jit(solution)/shard_map/ppermute | solution.py:577
  9.6 8.8 %collective-permute-start = (bf16[128,768]{1,0:T(8,128)(2,1)}, bf16[128,768]{1,0:T(8,128)(2,1)S(1)}, u32[]{:S(2)}, u32[]{:S(2)}) collective-permute-start(bf16[128,768]{1,0:T(8,128)(2,1)} %bitcast.17), channel_id=1, source_target_pairs={{0,1},{1,0},{2,3},{3,2},{4,5},{5,4},{6,7},{7,6},{8,9},{9,8},{10,11... | collective-permute-start | bytes 589832 | tf_op jit(solution)/shard_map/ppermute | solution.py:577
  12.3 15.3 %collective-permute-start.6 = (bf16[384,576]{1,0:T(8,128)(2,1)S(1)}, bf16[384,576]{1,0:T(8,128)(2,1)S(1)}, u32[]{:S(2)}, u32[]{:S(2)}) collective-permute-start(bf16[384,576]{1,0:T(8,128)(2,1)S(1)} %pad_maximum_fusion.1), channel_id=1, source_target_pairs={{0,4},{4,0},{8,12},{12,8},{16,20},{20,16},{24,28},{28,24},{1,5},{5... | collective-permute-start | bytes 1327112 | tf_op jit(solution)/shard_map/ppermute | solution.py:574
  18.4 26.3 %collective-permute-start.12 = (bf16[400,768]{1,0:T(8,128)(2,1)S(1)}, bf16[400,768]{1,0:T(8,128)(2,1)S(1)}, u32[]{:S(2)}, u32[]{:S(2)}) collective-permute-start(bf16[400,768]{1,0:T(8,128)(2,1)S(1)} %select_units.1.refs_0_), channel_id=1, source_target_pairs={{0,24},{4,28},{8,16},{12,20},{16,8},{20,12},{24,0},{28,4},{1,25},{... | collective-permute-start | bytes 1843208 | tf_op jit(solution)/shard_map/ppermute | solution.py:574
  20.9 25.9 %collective-permute-start.11 = (bf16[400,768]{1,0:T(8,128)(2,1)S(1)}, bf16[400,768]{1,0:T(8,128)(2,1)S(1)}, u32[]{:S(2)}, u32[]{:S(2)}) collective-permute-start(bf16[400,768]{1,0:T(8,128)(2,1)S(1)} %select_units.1.refs_0_), channel_id=1, source_target_pairs={{0,16},{4,20},{8,24},{12,28},{16,0},{20,4},{24,8},{28,12},{1,17},{... | collective-permute-start | bytes 1843208 | tf_op jit(solution)/shard_map/ppermute | solution.py:574
  21.4 25.6 %collective-permute-start.10 = (bf16[400,768]{1,0:T(8,128)(2,1)S(1)}, bf16[400,768]{1,0:T(8,128)(2,1)S(1)}, u32[]{:S(2)}, u32[]{:S(2)}) collective-permute-start(bf16[400,768]{1,0:T(8,128)(2,1)S(1)} %select_units.1.refs_0_), channel_id=1, source_target_pairs={{0,8},{4,12},{8,0},{12,4},{16,24},{20,28},{24,16},{28,20},{1,9},{5... | collective-permute-start | bytes 1843208 | tf_op jit(solution)/shard_map/ppermute | solution.py:574
  34.0 10.4 %collective-permute-start.8 = (bf16[768,128]{1,0:T(8,128)(2,1)S(1)}, bf16[768,128]{1,0:T(8,128)(2,1)S(1)}, u32[]{:S(2)}, u32[]{:S(2)}) collective-permute-start(bf16[768,128]{1,0:T(8,128)(2,1)S(1)} %get-tuple-element.95.refs_0_), channel_id=1, source_target_pairs={{0,2},{1,3},{2,0},{3,1},{4,6},{5,7},{6,4},{7,5},{8,10},{9,11},{10,... | collective-permute-start | bytes 589832 | tf_op jit(solution)/shard_map/ppermute | solution.py:577
  36.4 8.3 %collective-permute-start.7 = (bf16[768,128]{1,0:T(8,128)(2,1)S(1)}, bf16[768,128]{1,0:T(8,128)(2,1)S(1)}, u32[]{:S(2)}, u32[]{:S(2)}) collective-permute-start(bf16[768,128]{1,0:T(8,128)(2,1)S(1)} %get-tuple-element.95.refs_0_), channel_id=1, source_target_pairs={{0,1},{1,0},{2,3},{3,2},{4,5},{5,4},{6,7},{7,6},{8,9},{9,8},{10,11... | collective-permute-start | bytes 589832 | tf_op jit(solution)/shard_map/ppermute | solution.py:577
  59.2 9.8 %collective-permute-start.14 = (bf16[128,768]{1,0:T(8,128)(2,1)S(1)}, bf16[128,768]{1,0:T(8,128)(2,1)S(1)}, u32[]{:S(2)}, u32[]{:S(2)}) collective-permute-start(bf16[128,768]{1,0:T(8,128)(2,1)S(1)} %get-tuple-element.106), channel_id=1, source_target_pairs={{0,1},{1,0},{2,3},{3,2},{4,5},{5,4},{6,7},{7,6},{8,9},{9,8},{10,11... | collective-permute-start | bytes 589832 | tf_op jit(solution)/shard_map/ppermute | solution.py:577
  61.0 17.5 %collective-permute-start.15 = (bf16[128,768]{1,0:T(8,128)(2,1)S(1)}, bf16[128,768]{1,0:T(8,128)(2,1)S(1)}, u32[]{:S(2)}, u32[]{:S(2)}) collective-permute-start(bf16[128,768]{1,0:T(8,128)(2,1)S(1)} %get-tuple-element.107), channel_id=1, source_target_pairs={{0,2},{1,3},{2,0},{3,1},{4,6},{5,7},{6,4},{7,5},{8,10},{9,11},{10,... | collective-permute-start | bytes 589832 | tf_op jit(solution)/shard_map/ppermute | solution.py:577
  64.3 14.2 %collective-permute-start.16 = (bf16[128,768]{1,0:T(8,128)(2,1)S(1)}, bf16[128,768]{1,0:T(8,128)(2,1)S(1)}, u32[]{:S(2)}, u32[]{:S(2)}) collective-permute-start(bf16[128,768]{1,0:T(8,128)(2,1)S(1)} %get-tuple-element.108), channel_id=1, source_target_pairs={{0,3},{1,2},{2,1},{3,0},{4,7},{5,6},{6,5},{7,4},{8,11},{9,10},{10,... | collective-permute-start | bytes 589832 | tf_op jit(solution)/shard_map/ppermute | solution.py:577
  79.5 12.8 %collective-permute-start.18 = (bf16[128,768]{1,0:T(8,128)(2,1)S(1)}, bf16[128,768]{1,0:T(8,128)(2,1)S(1)}, u32[]{:S(2)}, u32[]{:S(2)}) collective-permute-start(bf16[128,768]{1,0:T(8,128)(2,1)S(1)} %get-tuple-element.112.refs_1_), channel_id=1, source_target_pairs={{0,2},{1,3},{2,0},{3,1},{4,6},{5,7},{6,4},{7,5},{8,10},{9,11},{10,... | collective-permute-start | bytes 589832 | tf_op jit(solution)/shard_map/ppermute | solution.py:577
  84.1 8.9 %collective-permute-start.17 = (bf16[128,768]{1,0:T(8,128)(2,1)S(1)}, bf16[128,768]{1,0:T(8,128)(2,1)S(1)}, u32[]{:S(2)}, u32[]{:S(2)}) collective-permute-start(bf16[128,768]{1,0:T(8,128)(2,1)S(1)} %get-tuple-element.112.refs_1_), channel_id=1, source_target_pairs={{0,1},{1,0},{2,3},{3,2},{4,5},{5,4},{6,7},{7,6},{8,9},{9,8},{10,11... | collective-permute-start | bytes 589832 | tf_op jit(solution)/shard_map/ppermute | solution.py:577
  105.8 19.5 %collective-permute-start.29 = (bf16[4,3,96,768]{3,2,1,0:T(8,128)(2,1)S(1)}, bf16[4,3,96,768]{3,2,1,0:T(8,128)(2,1)S(1)}, u32[]{:S(2)}, u32[]{:S(2)}) collective-permute-start(bf16[4,3,96,768]{3,2,1,0:T(8,128)(2,1)S(1)} %get-tuple-element.145), channel_id=1, source_target_pairs={{0,4},{4,0},{8,12},{12,8},{16,20},{20,16},{24,28},{28,24},{1,5},{5... | collective-permute-start | bytes 5308424 | tf_op jit(solution)/shard_map/ppermute | solution.py:574
  105.9 10.1 %collective-permute-start.20 = (bf16[128,768]{1,0:T(8,128)(2,1)S(1)}, bf16[128,768]{1,0:T(8,128)(2,1)S(1)}, u32[]{:S(2)}, u32[]{:S(2)}) collective-permute-start(bf16[128,768]{1,0:T(8,128)(2,1)S(1)} %get-tuple-element.114), channel_id=1, source_target_pairs={{0,1},{1,0},{2,3},{3,2},{4,5},{5,4},{6,7},{7,6},{8,9},{9,8},{10,11... | collective-permute-start | bytes 589832 | tf_op jit(solution)/shard_map/ppermute | solution.py:577
  106.2 17.1 %collective-permute-start.21 = (bf16[128,768]{1,0:T(8,128)(2,1)S(1)}, bf16[128,768]{1,0:T(8,128)(2,1)S(1)}, u32[]{:S(2)}, u32[]{:S(2)}) collective-permute-start(bf16[128,768]{1,0:T(8,128)(2,1)S(1)} %get-tuple-element.115), channel_id=1, source_target_pairs={{0,2},{1,3},{2,0},{3,1},{4,6},{5,7},{6,4},{7,5},{8,10},{9,11},{10,... | collective-permute-start | bytes 589832 | tf_op jit(solution)/shard_map/ppermute | solution.py:577
  106.8 16.6 %collective-permute-start.22 = (bf16[128,768]{1,0:T(8,128)(2,1)S(1)}, bf16[128,768]{1,0:T(8,128)(2,1)S(1)}, u32[]{:S(2)}, u32[]{:S(2)}) collective-permute-start(bf16[128,768]{1,0:T(8,128)(2,1)S(1)} %get-tuple-element.116), channel_id=1, source_target_pairs={{0,3},{1,2},{2,1},{3,0},{4,7},{5,6},{6,5},{7,4},{8,11},{9,10},{10,... | collective-permute-start | bytes 589832 | tf_op jit(solution)/shard_map/ppermute | solution.py:577
  125.7 16.3 %collective-permute-start.30 = (bf16[2,3,96,384]{3,2,1,0:T(8,128)(2,1)S(1)}, bf16[2,3,96,384]{3,2,1,0:T(8,128)(2,1)S(1)}, u32[]{:S(2)}, u32[]{:S(2)}) collective-permute-start(bf16[2,3,96,384]{3,2,1,0:T(8,128)(2,1)S(1)} %get-tuple-element.154), channel_id=1, source_target_pairs={{0,8},{4,12},{8,0},{12,4},{16,24},{20,28},{24,16},{28,20},{1,9},{5... | collective-permute-start | bytes 1327112 | tf_op jit(solution)/shard_map/ppermute | solution.py:574
  127.2 14.7 %collective-permute-start.31 = (bf16[2,3,96,384]{3,2,1,0:T(8,128)(2,1)S(1)}, bf16[2,3,96,384]{3,2,1,0:T(8,128)(2,1)S(1)}, u32[]{:S(2)}, u32[]{:S(2)}) collective-permute-start(bf16[2,3,96,384]{3,2,1,0:T(8,128)(2,1)S(1)} %get-tuple-element.155), channel_id=1, source_target_pairs={{0,16},{4,20},{8,24},{12,28},{16,0},{20,4},{24,8},{28,12},{1,17},{... | collective-permute-start | bytes 1327112 | tf_op jit(solution)/shard_map/ppermute | solution.py:574
  131.9 10.0 %collective-permute-start.24 = (bf16[144,384]{1,0:T(8,128)(2,1)S(1)}, bf16[144,384]{1,0:T(8,128)(2,1)S(1)}, u32[]{:S(2)}, u32[]{:S(2)}) collective-permute-start(bf16[144,384]{1,0:T(8,128)(2,1)S(1)} %get-tuple-element.124), channel_id=1, source_target_pairs={{0,2},{1,3},{2,0},{3,1},{4,6},{5,7},{6,4},{7,5},{8,10},{9,11},{10,... | collective-permute-start | bytes 331784 | tf_op jit(solution)/shard_map/ppermute | solution.py:577
  131.9 10.0 %collective-permute-start.25 = (bf16[144,384]{1,0:T(8,128)(2,1)S(1)}, bf16[144,384]{1,0:T(8,128)(2,1)S(1)}, u32[]{:S(2)}, u32[]{:S(2)}) collective-permute-start(bf16[144,384]{1,0:T(8,128)(2,1)S(1)} %get-tuple-element.125), channel_id=1, source_target_pairs={{0,3},{1,2},{2,1},{3,0},{4,7},{5,6},{6,5},{7,4},{8,11},{9,10},{10,... | collective-permute-start | bytes 331784 | tf_op jit(solution)/shard_map/ppermute | solution.py:577
  142.1 8.0 %collective-permute-start.32 = (bf16[3,96,384]{2,1,0:T(8,128)(2,1)S(1)}, bf16[3,96,384]{2,1,0:T(8,128)(2,1)S(1)}, u32[]{:S(2)}, u32[]{:S(2)}) collective-permute-start(bf16[3,96,384]{2,1,0:T(8,128)(2,1)S(1)} %get-tuple-element.158), channel_id=1, source_target_pairs={{0,16},{4,20},{8,24},{12,28},{16,0},{20,4},{24,8},{28,12},{1,17},{... | collective-permute-start | bytes 663560 | tf_op jit(solution)/shard_map/ppermute | solution.py:574
  152.2 25.3 %collective-permute-start.34 = (bf16[4,112,768]{2,1,0:T(8,128)(2,1)S(1)}, bf16[4,112,768]{2,1,0:T(8,128)(2,1)S(1)}, u32[]{:S(2)}, u32[]{:S(2)}) collective-permute-start(bf16[4,112,768]{2,1,0:T(8,128)(2,1)S(1)} %get-tuple-element.162), channel_id=1, source_target_pairs={{0,4},{4,0},{8,12},{12,8},{16,20},{20,16},{24,28},{28,24},{1,5},{5... | collective-permute-start | bytes 2064392 | tf_op jit(solution)/shard_map/ppermute | solution.py:574
  152.3 23.6 %collective-permute-start.39 = (bf16[3,96,768]{2,1,0:T(8,128)(2,1)S(1)}, bf16[3,96,768]{2,1,0:T(8,128)(2,1)S(1)}, u32[]{:S(2)}, u32[]{:S(2)}) collective-permute-start(bf16[3,96,768]{2,1,0:T(8,128)(2,1)S(1)} %step_three.1.refs_0_), channel_id=1, source_target_pairs={{0,2},{1,3},{2,0},{3,1},{4,6},{5,7},{6,4},{7,5},{8,10},{9,11},{10,... | collective-permute-start | bytes 1327112 | tf_op jit(solution)/shard_map/ppermute | solution.py:577
  154.5 37.0 %collective-permute-start.38 = (bf16[3,96,768]{2,1,0:T(8,128)(2,1)S(1)}, bf16[3,96,768]{2,1,0:T(8,128)(2,1)S(1)}, u32[]{:S(2)}, u32[]{:S(2)}) collective-permute-start(bf16[3,96,768]{2,1,0:T(8,128)(2,1)S(1)} %step_three.1.refs_0_), channel_id=1, source_target_pairs={{0,1},{1,0},{2,3},{3,2},{4,5},{5,4},{6,7},{7,6},{8,9},{9,8},{10,11... | collective-permute-start | bytes 1327112 | tf_op jit(solution)/shard_map/ppermute | solution.py:577
  154.6 29.5 %collective-permute-start.26 = (bf16[128,768]{1,0:T(8,128)(2,1)S(1)}, bf16[128,768]{1,0:T(8,128)(2,1)S(1)}, u32[]{:S(2)}, u32[]{:S(2)}) collective-permute-start(bf16[128,768]{1,0:T(8,128)(2,1)S(1)} %get-tuple-element.132), channel_id=1, source_target_pairs={{0,1},{1,0},{2,3},{3,2},{4,5},{5,4},{6,7},{7,6},{8,9},{9,8},{10,11... | collective-permute-start | bytes 589832 | tf_op jit(solution)/shard_map/ppermute | solution.py:577
  156.5 28.9 %collective-permute-start.27 = (bf16[128,768]{1,0:T(8,128)(2,1)S(1)}, bf16[128,768]{1,0:T(8,128)(2,1)S(1)}, u32[]{:S(2)}, u32[]{:S(2)}) collective-permute-start(bf16[128,768]{1,0:T(8,128)(2,1)S(1)} %get-tuple-element.133), channel_id=1, source_target_pairs={{0,2},{1,3},{2,0},{3,1},{4,6},{5,7},{6,4},{7,5},{8,10},{9,11},{10,... | collective-permute-start | bytes 589832 | tf_op jit(solution)/shard_map/ppermute | solution.py:577
  175.9 14.0 %collective-permute-start.28 = (bf16[128,768]{1,0:T(8,128)(2,1)S(1)}, bf16[128,768]{1,0:T(8,128)(2,1)S(1)}, u32[]{:S(2)}, u32[]{:S(2)}) collective-permute-start(bf16[128,768]{1,0:T(8,128)(2,1)S(1)} %get-tuple-element.134), channel_id=1, source_target_pairs={{0,3},{1,2},{2,1},{3,0},{4,7},{5,6},{6,5},{7,4},{8,11},{9,10},{10,... | collective-permute-start | bytes 589832 | tf_op jit(solution)/shard_map/ppermute | solution.py:577
  177.5 23.1 %collective-permute-start.42 = (bf16[3,96,768]{2,1,0:T(8,128)(2,1)S(1)}, bf16[3,96,768]{2,1,0:T(8,128)(2,1)S(1)}, u32[]{:S(2)}, u32[]{:S(2)}) collective-permute-start(bf16[3,96,768]{2,1,0:T(8,128)(2,1)S(1)} %collective-permute-done.39.refs_2_), channel_id=1, source_target_pairs={{0,1},{1,0},{2,3},{3,2},{4,5},{5,4},{6,7},{7,6},{8,9},{9,8},{10,11... | collective-permute-start | bytes 1327112 | tf_op jit(solution)/shard_map/ppermute | solution.py:577
  184.0 7.5 %collective-permute-start.35 = (bf16[112,768]{1,0:T(8,128)(2,1)S(1)}, bf16[112,768]{1,0:T(8,128)(2,1)S(1)}, u32[]{:S(2)}, u32[]{:S(2)}) collective-permute-start(bf16[112,768]{1,0:T(8,128)(2,1)S(1)} %get-tuple-element.164), channel_id=1, source_target_pairs={{0,8},{4,12},{8,0},{12,4},{16,24},{20,28},{24,16},{28,20},{1,9},{5... | collective-permute-start | bytes 516104 | tf_op jit(solution)/shard_map/ppermute | solution.py:574
  196.3 10.1 %collective-permute-start.41 = (bf16[112,768]{1,0:T(8,128)(2,1)S(1)}, bf16[112,768]{1,0:T(8,128)(2,1)S(1)}, u32[]{:S(2)}, u32[]{:S(2)}) collective-permute-start(bf16[112,768]{1,0:T(8,128)(2,1)S(1)} %plane_sum.1.refs_0_), channel_id=1, source_target_pairs={{0,2},{1,3},{2,0},{3,1},{4,6},{5,7},{6,4},{7,5},{8,10},{9,11},{10,... | collective-permute-start | bytes 516104 | tf_op jit(solution)/shard_map/ppermute | solution.py:577
  (19 other events, 192.8 us)

commit v3 on v2

--- a/solution.py
+++ b/solution.py
@@ -624,7 +624,7 @@
         mib=8,
     )
     piece = after(piece, qkv_even, x_blocks[1:3])
-    feed_even = [piece] + [swap(piece, s) for s in (2, 4, 6)]
+    even_x, even_y = swap(piece, 2), swap(piece, 4)
 
     length = SEQ * rows
     packed, queries, keys, values, probs, qkv_full = call(
@@ -641,6 +641,11 @@
         flops=2 * length * head_width * (3 * model + 2 * length),
     )
     packs = gather_seq(packed)
+    even_x, even_y = after((even_x, even_y), packed)
+    half = model // 2
+    diagonal = [swap(even_x[:, :half], 4), swap(even_y[:, half:], 2)]
+    feed_even = [piece, even_x, even_y, jnp.concatenate(diagonal, axis=1)]
+
 
     feed_even = after(feed_even, packs[1:3])
     feed_odd = swap(jnp.concatenate(feed_even, axis=0), 1)

time: 214 us -> 214 us (level)
  waiting for transfers between devices: 108 us -> 105 us
    ppermute x27, waiting for transfers between devices: 98.4 us -> 94.8 us  [pass_seq(): return lax.ppermute(value, 'seq', [(i, i ^ s) for i in range(SEQ)])]
    ppermute x17 -> x18, starting transfers between devices: 16.4 us -> 18.7 us  [swap(): return lax.ppermute(value, 'dp', [(i, i ^ s * stride) for i in range(dp)])]
    ppermute x17 -> x18, waiting for transfers between devices: 10.1 us -> 10.5 us  [swap(): return lax.ppermute(value, 'dp', [(i, i ^ s * stride) for i in range(dp)])]
  transfers between devices with their start and end apart: 44 -> 45, of which waited for: 26 -> 25; matrix products, arithmetic and copies ran while one was open for 1% -> 1% of each run, Pallas kernels for 10% -> 10%
where the time goes in v3:
time: 214 us; the launch traced here: 213 us
  waiting for transfers between devices  105 us (49%)
  starting transfers between devices  60.9 us (28%)
  Pallas kernels  39.2 us (18%)
  local copies, waits for them, and re-layouts  5.52 us (3%)
    ppermute x27, waiting for transfers between devices, pass_seq(): return lax.ppermute(value, 'seq', [(i, i ^ s) for i in range(SEQ)])  94.8 us
    ppermute x27, starting transfers between devices, pass_seq(): return lax.ppermute(value, 'seq', [(i, i ^ s) for i in range(SEQ)])  42.3 us
    pallas_call x18, Pallas kernels, call(): pl.pallas_call(kernel, out_shape=out_shape, in_specs=specs, out_specs=[pl...  39.2 us
    ppermute x18, starting transfers between devices, swap(): return lax.ppermute(value, 'dp', [(i, i ^ s * stride) for i in range(dp)])  18.7 us
    ppermute x18, waiting for transfers between devices, swap(): return lax.ppermute(value, 'dp', [(i, i ^ s * stride) for i in range(dp)])  10.5 us
  transfers between devices with their start and end apart: 45, of which 25 were waited for; matrix products, arithmetic and copies ran while one was open for 1% of the time, Pallas kernels for 10%

profile of v3, /device:TPU:0, one launch (start us, length us, event | category | flops | bytes accessed | tf_op | source)
XLA Modules:
  0.0 213.4 jit_solution(675801275785657966)
XLA Ops:
  1.9 4.0 %collective-permute-start.5 = (bf16[96,576]{1,0:T(8,128)(2,1)S(1)}, bf16[96,576]{1,0:T(8,128)(2,1)S(1)}, u32[]{:S(2)}, u32[]{:S(2)}) collective-permute-start(bf16[96,576]{1,0:T(8,128)(2,1)S(1)} %pad_maximum_fusion.3.refs_4_), channel_id=1, source_target_pairs={{0,24},{4,28},{8,16},{12,20},{16,8},{20,12},{24,0},{28,4},{1,25},{... | collective-permute-start | bytes 331784 | tf_op jit(solution)/shard_map/ppermute | solution.py:574
  6.6 3.0 %collective-permute-start.1 = (bf16[128,768]{1,0:T(8,128)(2,1)}, bf16[128,768]{1,0:T(8,128)(2,1)S(1)}, u32[]{:S(2)}, u32[]{:S(2)}) collective-permute-start(bf16[128,768]{1,0:T(8,128)(2,1)} %bitcast.16), channel_id=1, source_target_pairs={{0,2},{1,3},{2,0},{3,1},{4,6},{5,7},{6,4},{7,5},{8,10},{9,11},{10,... | collective-permute-start | bytes 589832 | tf_op jit(solution)/shard_map/ppermute | solution.py:577
  23.1 5.8 %collective-permute-done.2.refs_3_.refs_7_.refs_4_ = bf16[128,768]{1,0:T(8,128)(2,1)S(1)} collective-permute-done((bf16[128,768]{1,0:T(8,128)(2,1)S(1)}, bf16[128,768]{1,0:T(8,128)(2,1)S(1)}, u32[]{:S(2)}, u32[]{:S(2)}) %collective-permute-start.2) | collective-permute-done | bytes 196640 | tf_op jit(solution)/shard_map/ppermute | solution.py:577
  28.9 6.4 %attention_forward.1 = (bf16[768,128]{1,0:T(8,128)(2,1)S(1)}, bf16[512,192]{1,0:T(8,128)(2,1)S(1)}, bf16[512,192]{1,0:T(8,128)(2,1)S(1)}, bf16[512,192]{1,0:T(8,...) custom-call(s32[12]{0:T(128)S(1)} %pad_add_fusion.ids, s32[1,8]{1,0:T(1,128)S(1)} %copy-done.5, ...), custom_call_target="tpu_custom_call" | custom-call | flops 654311424 | bytes 4915200 | tf_op jit(solution)/shard_map/attention_forward/pallas_call | solution.py:83
  38.5 2.8 %collective-permute-start.7 = (bf16[768,128]{1,0:T(8,128)(2,1)S(1)}, bf16[768,128]{1,0:T(8,128)(2,1)S(1)}, u32[]{:S(2)}, u32[]{:S(2)}) collective-permute-start(bf16[768,128]{1,0:T(8,128)(2,1)S(1)} %get-tuple-element.97.refs_0_), channel_id=1, source_target_pairs={{0,1},{1,0},{2,3},{3,2},{4,5},{5,4},{6,7},{7,6},{8,9},{9,8},{10,11... | collective-permute-start | bytes 589832 | tf_op jit(solution)/shard_map/ppermute | solution.py:577
  41.3 2.9 %collective-permute-done.13 = bf16[400,384]{1,0:T(8,128)(2,1)S(1)} collective-permute-done((bf16[400,384]{1,0:T(8,128)(2,1)S(1)}, bf16[400,384]{1,0:T(8,128)(2,1)S(1)}, u32[]{:S(2)}, u32[]{:S(2)}) %collective-permute-start.13) | collective-permute-done | bytes 307232 | tf_op jit(solution)/shard_map/ppermute | solution.py:574
  44.6 2.9 %collective-permute-done.8.refs_2_ = bf16[768,128]{1,0:T(8,128)(2,1)S(1)} collective-permute-done((bf16[768,128]{1,0:T(8,128)(2,1)S(1)}, bf16[768,128]{1,0:T(8,128)(2,1)S(1)}, u32[]{:S(2)}, u32[]{:S(2)}) %collective-permute-start.8) | collective-permute-done | bytes 196640 | tf_op jit(solution)/shard_map/ppermute | solution.py:577
  49.5 3.4 %collective-permute-done.14.refs_4_ = bf16[1600,768]{1,0:T(8,128)(2,1)S(1)} collective-permute-done((bf16[1600,768]{1,0:T(8,128)(2,1)S(1)}, bf16[1600,768]{1,0:T(8,128)(2,1)S(1)}, u32[]{:S(2)}, u32[]{:S(2)}) %collective-permute-start.14) | collective-permute-done | bytes 2457632 | tf_op jit(solution)/shard_map/ppermute | solution.py:574
  55.5 4.2 %middle_forward.1 = (f32[128,768]{1,0:T(8,128)S(1)}, bf16[128,768]{1,0:T(8,128)(2,1)S(1)}, bf16[128,768]{1,0:T(8,128)(2,1)S(1)}, bf16[128,768]{1,0:T(8,128)(2,1)...) custom-call(s32[12]{0:T(128)S(1)} %pad_add_fusion.ids, ...), custom_call_target="tpu_custom_call" | custom-call | flops 2415919104 | bytes 9269248 | tf_op jit(solution)/shard_map/middle_forward/pallas_call | solution.py:83
  61.0 2.3 %collective-permute-start.16 = (bf16[128,768]{1,0:T(8,128)(2,1)S(1)}, bf16[128,768]{1,0:T(8,128)(2,1)S(1)}, u32[]{:S(2)}, u32[]{:S(2)}) collective-permute-start(bf16[128,768]{1,0:T(8,128)(2,1)S(1)} %get-tuple-element.111), channel_id=1, source_target_pairs={{0,2},{1,3},{2,0},{3,1},{4,6},{5,7},{6,4},{7,5},{8,10},{9,11},{10,... | collective-permute-start | bytes 589832 | tf_op jit(solution)/shard_map/ppermute | solution.py:577
  64.2 5.2 %collective-permute-done.15.refs_1_ = bf16[128,768]{1,0:T(8,128)(2,1)S(1)} collective-permute-done((bf16[128,768]{1,0:T(8,128)(2,1)S(1)}, bf16[128,768]{1,0:T(8,128)(2,1)S(1)}, u32[]{:S(2)}, u32[]{:S(2)}) %collective-permute-start.15) | collective-permute-done | bytes 196640 | tf_op jit(solution)/shard_map/ppermute | solution.py:577
  69.5 8.6 %collective-permute-done.16.refs_2_ = bf16[128,768]{1,0:T(8,128)(2,1)S(1)} collective-permute-done((bf16[128,768]{1,0:T(8,128)(2,1)S(1)}, bf16[128,768]{1,0:T(8,128)(2,1)S(1)}, u32[]{:S(2)}, u32[]{:S(2)}) %collective-permute-start.16) | collective-permute-done | bytes 196640 | tf_op jit(solution)/shard_map/ppermute | solution.py:577
  79.2 4.0 %collective-permute-start.19 = (bf16[128,768]{1,0:T(8,128)(2,1)S(1)}, bf16[128,768]{1,0:T(8,128)(2,1)S(1)}, u32[]{:S(2)}, u32[]{:S(2)}) collective-permute-start(bf16[128,768]{1,0:T(8,128)(2,1)S(1)} %get-tuple-element.116.refs_1_), channel_id=1, source_target_pairs={{0,2},{1,3},{2,0},{3,1},{4,6},{5,7},{6,4},{7,5},{8,10},{9,11},{10,... | collective-permute-start | bytes 589832 | tf_op jit(solution)/shard_map/ppermute | solution.py:577
  83.2 8.0 %collective-permute-done.19.refs_3_ = bf16[128,768]{1,0:T(8,128)(2,1)S(1)} collective-permute-done((bf16[128,768]{1,0:T(8,128)(2,1)S(1)}, bf16[128,768]{1,0:T(8,128)(2,1)S(1)}, u32[]{:S(2)}, u32[]{:S(2)}) %collective-permute-start.19) | collective-permute-done | bytes 196640 | tf_op jit(solution)/shard_map/ppermute | solution.py:577
  91.7 5.5 %collective-permute-done.20.refs_4_ = bf16[128,768]{1,0:T(8,128)(2,1)S(1)} collective-permute-done((bf16[128,768]{1,0:T(8,128)(2,1)S(1)}, bf16[128,768]{1,0:T(8,128)(2,1)S(1)}, u32[]{:S(2)}, u32[]{:S(2)}) %collective-permute-start.20) | collective-permute-done | bytes 196640 | tf_op jit(solution)/shard_map/ppermute | solution.py:577
  97.1 4.4 %feed_back.1 = (f32[128,768]{1,0:T(8,128)S(1)}, bf16[128,768]{1,0:T(8,128)(2,1)S(1)}, bf16[128,768]{1,0:T(8,128)(2,1)S(1)}, bf16[128,768]{1,0:T(8,128)(2,1)S(1)}...) custom-call(bf16[512,768]{1,0:T(8,128)(2,1)S(1)} %get-tuple-element., ...), custom_call_target="tpu_custom_call" | custom-call | flops 3019898880 | bytes 9240576 | tf_op jit(solution)/shard_map/feed_back/pallas_call | solution.py:83
  101.5 3.1 %feed_weights.1 = (f32[4,3,96,768]{3,2,1,0:T(8,128)S(1)}, bf16[4,3,96,768]{3,2,1,0:T(8,128)(2,1)S(1)}) custom-call(s32[12]{0:T(128)S(1)} %pad_add_fusion.ids, bf16[512,768]{1,0:T(8,128)(2,1)S(1)} %get-tuple-element.113.refs_4_.refs_0_, bf16[512,768]{1,0:T(8,128)(2,1)S(1)} %get-tuple-element.143.refs_1_, bf16[512,768]{1,0:T(8,128)(2,1)S(1)} %get-tuple-element.144.refs_2_, ...), custom_call_target="tpu_custom_call" | custom-call | flops 1811939328 | bytes 9240576 | tf_op jit(solution)/shard_map/feed_weights/pallas_call | solution.py:83
  106.2 2.9 %collective-permute-start.23 = (bf16[128,768]{1,0:T(8,128)(2,1)S(1)}, bf16[128,768]{1,0:T(8,128)(2,1)S(1)}, u32[]{:S(2)}, u32[]{:S(2)}) collective-permute-start(bf16[128,768]{1,0:T(8,128)(2,1)S(1)} %get-tuple-element.120), channel_id=1, source_target_pairs={{0,3},{1,2},{2,1},{3,0},{4,7},{5,6},{6,5},{7,4},{8,11},{9,10},{10,... | collective-permute-start | bytes 589832 | tf_op jit(solution)/shard_map/ppermute | solution.py:577
  109.1 6.0 %collective-permute-done.21.refs_1_ = bf16[128,768]{1,0:T(8,128)(2,1)S(1)} collective-permute-done((bf16[128,768]{1,0:T(8,128)(2,1)S(1)}, bf16[128,768]{1,0:T(8,128)(2,1)S(1)}, u32[]{:S(2)}, u32[]{:S(2)}) %collective-permute-start.21) | collective-permute-done | bytes 196640 | tf_op jit(solution)/shard_map/ppermute | solution.py:577
  115.1 7.0 %collective-permute-done.22.refs_2_ = bf16[128,768]{1,0:T(8,128)(2,1)S(1)} collective-permute-done((bf16[128,768]{1,0:T(8,128)(2,1)S(1)}, bf16[128,768]{1,0:T(8,128)(2,1)S(1)}, u32[]{:S(2)}, u32[]{:S(2)}) %collective-permute-start.22) | collective-permute-done | bytes 196640 | tf_op jit(solution)/shard_map/ppermute | solution.py:577
  127.5 3.9 %collective-permute-start.24 = (bf16[144,384]{1,0:T(8,128)(2,1)S(1)}, bf16[144,384]{1,0:T(8,128)(2,1)S(1)}, u32[]{:S(2)}, u32[]{:S(2)}) collective-permute-start(bf16[144,384]{1,0:T(8,128)(2,1)S(1)} %get-tuple-element.127), channel_id=1, source_target_pairs={{0,1},{1,0},{2,3},{3,2},{4,5},{5,4},{6,7},{7,6},{8,9},{9,8},{10,11... | collective-permute-start | bytes 331784 | tf_op jit(solution)/shard_map/ppermute | solution.py:577
  131.6 2.3 %collective-permute-start.26 = (bf16[144,384]{1,0:T(8,128)(2,1)S(1)}, bf16[144,384]{1,0:T(8,128)(2,1)S(1)}, u32[]{:S(2)}, u32[]{:S(2)}) collective-permute-start(bf16[144,384]{1,0:T(8,128)(2,1)S(1)} %get-tuple-element.129), channel_id=1, source_target_pairs={{0,3},{1,2},{2,1},{3,0},{4,7},{5,6},{6,5},{7,4},{8,11},{9,10},{10,... | collective-permute-start | bytes 331784 | tf_op jit(solution)/shard_map/ppermute | solution.py:577
  134.9 6.4 %collective-permute-done.25.refs_2_.refs_7_.refs_8_ = bf16[144,384]{1,0:T(8,128)(2,1)S(1)} collective-permute-done((bf16[144,384]{1,0:T(8,128)(2,1)S(1)}, bf16[144,384]{1,0:T(8,128)(2,1)S(1)}, u32[]{:S(2)}, u32[]{:S(2)}) %collective-permute-start.25) | collective-permute-done | bytes 110624 | tf_op jit(solution)/shard_map/ppermute | solution.py:577
  142.6 6.0 %attention_back.1 = (f32[128,768]{1,0:T(8,128)S(1)}, bf16[128,768]{1,0:T(8,128)(2,1)S(1)}, bf16[128,768]{1,0:T(8,128)(2,1)S(1)}, bf16[128,768]{1,0:T(8,128)(2,1)S(1)}, bf16[512,576]{1,0:T(8,128)(2,1)S(1)}) custom-call(bf16[144,384]{1,0:T(8,128)(2,1)S(1)} %get-tuple-element.126.refs_0_.refs_6_, ...), custom_call_target="tpu_custom_call" | custom-call | flops 956301312 | bytes 5062656 | tf_op jit(solution)/shard_map/attention_back/pallas_call | solution.py:83
  156.0 18.5 %collective-permute-done.40.refs_2_ = bf16[3,96,768]{2,1,0:T(8,128)(2,1)S(1)} collective-permute-done((bf16[3,96,768]{2,1,0:T(8,128)(2,1)S(1)}, bf16[3,96,768]{2,1,0:T(8,128)(2,1)S(1)}, u32[]{:S(2)}, u32[]{:S(2)}) %collective-permute-start.40) | collective-permute-done | bytes 442400 | tf_op jit(solution)/shard_map/ppermute | solution.py:577
  176.5 5.9 %collective-permute-done.27.refs_2_ = bf16[128,768]{1,0:T(8,128)(2,1)S(1)} collective-permute-done((bf16[128,768]{1,0:T(8,128)(2,1)S(1)}, bf16[128,768]{1,0:T(8,128)(2,1)S(1)}, u32[]{:S(2)}, u32[]{:S(2)}) %collective-permute-start.27) | collective-permute-done | bytes 196640 | tf_op jit(solution)/shard_map/ppermute | solution.py:577
  185.4 3.3 %collective-permute-done.29.refs_4_ = bf16[128,768]{1,0:T(8,128)(2,1)S(1)} collective-permute-done((bf16[128,768]{1,0:T(8,128)(2,1)S(1)}, bf16[128,768]{1,0:T(8,128)(2,1)S(1)}, u32[]{:S(2)}, u32[]{:S(2)}) %collective-permute-start.29) | collective-permute-done | bytes 196640 | tf_op jit(solution)/shard_map/ppermute | solution.py:577
  188.7 2.4 %collective-permute-start.38 = (bf16[112,768]{1,0:T(8,128)(2,1)S(1)}, bf16[112,768]{1,0:T(8,128)(2,1)S(1)}, u32[]{:S(2)}, u32[]{:S(2)}) collective-permute-start(bf16[112,768]{1,0:T(8,128)(2,1)S(1)} %get-tuple-element.170), channel_id=1, source_target_pairs={{0,24},{4,28},{8,16},{12,20},{16,8},{20,12},{24,0},{28,4},{1,25},{... | collective-permute-start | bytes 516104 | tf_op jit(solution)/shard_map/ppermute | solution.py:574
  191.1 3.8 %collective-permute-done.38.refs_3_ = bf16[112,768]{1,0:T(8,128)(2,1)S(1)} collective-permute-done((bf16[112,768]{1,0:T(8,128)(2,1)S(1)}, bf16[112,768]{1,0:T(8,128)(2,1)S(1)}, u32[]{:S(2)}, u32[]{:S(2)}) %collective-permute-start.38) | collective-permute-done | bytes 172064 | tf_op jit(solution)/shard_map/ppermute | solution.py:574
  195.1 3.6 %collective-permute-start.42 = (bf16[112,768]{1,0:T(8,128)(2,1)S(1)}, bf16[112,768]{1,0:T(8,128)(2,1)S(1)}, u32[]{:S(2)}, u32[]{:S(2)}) collective-permute-start(bf16[112,768]{1,0:T(8,128)(2,1)S(1)} %plane_sum.1.refs_0_), channel_id=1, source_target_pairs={{0,2},{1,3},{2,0},{3,1},{4,6},{5,7},{6,4},{7,5},{8,10},{9,11},{10,... | collective-permute-start | bytes 516104 | tf_op jit(solution)/shard_map/ppermute | solution.py:577
  199.4 4.5 %feed_final.1 = (f32[96,6144]{1,0:T(8,128)}, f32[384,768]{1,0:T(8,128)}) custom-call(s32[12]{0:T(128)S(1)} %pad_add_fusion.ids, bf16[3,96,768]{2,1,0:T(8,128)(2,1)S(1)} %step_three.1.refs_0_, bf16[3,96,768]{2,1,0:T(8,128)(2,1)S(1)} %collective-permute-done.39.refs_1_, bf16[3,96,768]{2,1,0:T(8,128)(2,1)S(1)} %collective-permute-done.40.refs_2_, ...), custom_call_target="tpu_custom_call" | custom-call | bytes 5308416 | tf_op jit(solution)/shard_map/feed_final/pallas_call | solution.py:83
  207.0 4.0 %collective-permute-done.44.refs_3_ = bf16[112,768]{1,0:T(8,128)(2,1)S(1)} collective-permute-done((bf16[112,768]{1,0:T(8,128)(2,1)S(1)}, bf16[112,768]{1,0:T(8,128)(2,1)S(1)}, u32[]{:S(2)}, u32[]{:S(2)}) %collective-permute-start.44) | collective-permute-done | bytes 172064 | tf_op jit(solution)/shard_map/ppermute | solution.py:577
  (103 shorter events, 55.2 us)
Async XLA Ops:
  1.9 14.4 %collective-permute-start.5 = (bf16[96,576]{1,0:T(8,128)(2,1)S(1)}, bf16[96,576]{1,0:T(8,128)(2,1)S(1)}, u32[]{:S(2)}, u32[]{:S(2)}) collective-permute-start(bf16[96,576]{1,0:T(8,128)(2,1)S(1)} %pad_maximum_fusion.3.refs_4_), channel_id=1, source_target_pairs={{0,24},{4,28},{8,16},{12,20},{16,8},{20,12},{24,0},{28,4},{1,25},{... | collective-permute-start | bytes 331784 | tf_op jit(solution)/shard_map/ppermute | solution.py:574
  5.9 10.5 %collective-permute-start.4 = (bf16[96,576]{1,0:T(8,128)(2,1)S(1)}, bf16[96,576]{1,0:T(8,128)(2,1)S(1)}, u32[]{:S(2)}, u32[]{:S(2)}) collective-permute-start(bf16[96,576]{1,0:T(8,128)(2,1)S(1)} %pad_maximum_fusion.3.refs_4_), channel_id=1, source_target_pairs={{0,16},{4,20},{8,24},{12,28},{16,0},{20,4},{24,8},{28,12},{1,17},{... | collective-permute-start | bytes 331784 | tf_op jit(solution)/shard_map/ppermute | solution.py:574
  6.4 10.0 %collective-permute-start.3 = (bf16[96,576]{1,0:T(8,128)(2,1)S(1)}, bf16[96,576]{1,0:T(8,128)(2,1)S(1)}, u32[]{:S(2)}, u32[]{:S(2)}) collective-permute-start(bf16[96,576]{1,0:T(8,128)(2,1)S(1)} %pad_maximum_fusion.3.refs_4_), channel_id=1, source_target_pairs={{0,8},{4,12},{8,0},{12,4},{16,24},{20,28},{24,16},{28,20},{1,9},{5... | collective-permute-start | bytes 331784 | tf_op jit(solution)/shard_map/ppermute | solution.py:574
  6.6 11.6 %collective-permute-start.1 = (bf16[128,768]{1,0:T(8,128)(2,1)}, bf16[128,768]{1,0:T(8,128)(2,1)S(1)}, u32[]{:S(2)}, u32[]{:S(2)}) collective-permute-start(bf16[128,768]{1,0:T(8,128)(2,1)} %bitcast.16), channel_id=1, source_target_pairs={{0,2},{1,3},{2,0},{3,1},{4,6},{5,7},{6,4},{7,5},{8,10},{9,11},{10,... | collective-permute-start | bytes 589832 | tf_op jit(solution)/shard_map/ppermute | solution.py:577
  9.6 8.8 %collective-permute-start = (bf16[128,768]{1,0:T(8,128)(2,1)}, bf16[128,768]{1,0:T(8,128)(2,1)S(1)}, u32[]{:S(2)}, u32[]{:S(2)}) collective-permute-start(bf16[128,768]{1,0:T(8,128)(2,1)} %bitcast.17), channel_id=1, source_target_pairs={{0,1},{1,0},{2,3},{3,2},{4,5},{5,4},{6,7},{7,6},{8,9},{9,8},{10,11... | collective-permute-start | bytes 589832 | tf_op jit(solution)/shard_map/ppermute | solution.py:577
  18.4 17.0 %collective-permute-start.11 = (bf16[400,768]{1,0:T(8,128)(2,1)S(1)}, bf16[400,768]{1,0:T(8,128)(2,1)S(1)}, u32[]{:S(2)}, u32[]{:S(2)}) collective-permute-start(bf16[400,768]{1,0:T(8,128)(2,1)S(1)} %select_units.1.refs_0_), channel_id=1, source_target_pairs={{0,16},{4,20},{8,24},{12,28},{16,0},{20,4},{24,8},{28,12},{1,17},{... | collective-permute-start | bytes 1843208 | tf_op jit(solution)/shard_map/ppermute | solution.py:574
  20.0 15.4 %collective-permute-start.10 = (bf16[400,768]{1,0:T(8,128)(2,1)S(1)}, bf16[400,768]{1,0:T(8,128)(2,1)S(1)}, u32[]{:S(2)}, u32[]{:S(2)}) collective-permute-start(bf16[400,768]{1,0:T(8,128)(2,1)S(1)} %select_units.1.refs_0_), channel_id=1, source_target_pairs={{0,8},{4,12},{8,0},{12,4},{16,24},{20,28},{24,16},{28,20},{1,9},{5... | collective-permute-start | bytes 1843208 | tf_op jit(solution)/shard_map/ppermute | solution.py:574
  35.4 8.8 %collective-permute-start.13 = (bf16[400,384]{1,0:T(8,128)(2,1)S(1)}, bf16[400,384]{1,0:T(8,128)(2,1)S(1)}, u32[]{:S(2)}, u32[]{:S(2)}) collective-permute-start(bf16[400,384]{1,0:T(8,128)(2,1)S(1)} %slice.22), channel_id=1, source_target_pairs={{0,8},{4,12},{8,0},{12,4},{16,24},{20,28},{24,16},{28,20},{1,9},{5... | collective-permute-start | bytes 921608 | tf_op jit(solution)/shard_map/ppermute | solution.py:574
  36.0 8.5 %collective-permute-start.12 = (bf16[400,384]{1,0:T(8,128)(2,1)S(1)}, bf16[400,384]{1,0:T(8,128)(2,1)S(1)}, u32[]{:S(2)}, u32[]{:S(2)}) collective-permute-start(bf16[400,384]{1,0:T(8,128)(2,1)S(1)} %slice.21), channel_id=1, source_target_pairs={{0,16},{4,20},{8,24},{12,28},{16,0},{20,4},{24,8},{28,12},{1,17},{... | collective-permute-start | bytes 921608 | tf_op jit(solution)/shard_map/ppermute | solution.py:574
  36.5 10.9 %collective-permute-start.8 = (bf16[768,128]{1,0:T(8,128)(2,1)S(1)}, bf16[768,128]{1,0:T(8,128)(2,1)S(1)}, u32[]{:S(2)}, u32[]{:S(2)}) collective-permute-start(bf16[768,128]{1,0:T(8,128)(2,1)S(1)} %get-tuple-element.97.refs_0_), channel_id=1, source_target_pairs={{0,2},{1,3},{2,0},{3,1},{4,6},{5,7},{6,4},{7,5},{8,10},{9,11},{10,... | collective-permute-start | bytes 589832 | tf_op jit(solution)/shard_map/ppermute | solution.py:577
  38.5 9.2 %collective-permute-start.7 = (bf16[768,128]{1,0:T(8,128)(2,1)S(1)}, bf16[768,128]{1,0:T(8,128)(2,1)S(1)}, u32[]{:S(2)}, u32[]{:S(2)}) collective-permute-start(bf16[768,128]{1,0:T(8,128)(2,1)S(1)} %get-tuple-element.97.refs_0_), channel_id=1, source_target_pairs={{0,1},{1,0},{2,3},{3,2},{4,5},{5,4},{6,7},{7,6},{8,9},{9,8},{10,11... | collective-permute-start | bytes 589832 | tf_op jit(solution)/shard_map/ppermute | solution.py:577
  59.8 9.7 %collective-permute-start.15 = (bf16[128,768]{1,0:T(8,128)(2,1)S(1)}, bf16[128,768]{1,0:T(8,128)(2,1)S(1)}, u32[]{:S(2)}, u32[]{:S(2)}) collective-permute-start(bf16[128,768]{1,0:T(8,128)(2,1)S(1)} %get-tuple-element.110), channel_id=1, source_target_pairs={{0,1},{1,0},{2,3},{3,2},{4,5},{5,4},{6,7},{7,6},{8,9},{9,8},{10,11... | collective-permute-start | bytes 589832 | tf_op jit(solution)/shard_map/ppermute | solution.py:577
  61.0 17.1 %collective-permute-start.16 = (bf16[128,768]{1,0:T(8,128)(2,1)S(1)}, bf16[128,768]{1,0:T(8,128)(2,1)S(1)}, u32[]{:S(2)}, u32[]{:S(2)}) collective-permute-start(bf16[128,768]{1,0:T(8,128)(2,1)S(1)} %get-tuple-element.111), channel_id=1, source_target_pairs={{0,2},{1,3},{2,0},{3,1},{4,6},{5,7},{6,4},{7,5},{8,10},{9,11},{10,... | collective-permute-start | bytes 589832 | tf_op jit(solution)/shard_map/ppermute | solution.py:577
  63.3 14.8 %collective-permute-start.17 = (bf16[128,768]{1,0:T(8,128)(2,1)S(1)}, bf16[128,768]{1,0:T(8,128)(2,1)S(1)}, u32[]{:S(2)}, u32[]{:S(2)}) collective-permute-start(bf16[128,768]{1,0:T(8,128)(2,1)S(1)} %get-tuple-element.112), channel_id=1, source_target_pairs={{0,3},{1,2},{2,1},{3,0},{4,7},{5,6},{6,5},{7,4},{8,11},{9,10},{10,... | collective-permute-start | bytes 589832 | tf_op jit(solution)/shard_map/ppermute | solution.py:577
  79.2 12.0 %collective-permute-start.19 = (bf16[128,768]{1,0:T(8,128)(2,1)S(1)}, bf16[128,768]{1,0:T(8,128)(2,1)S(1)}, u32[]{:S(2)}, u32[]{:S(2)}) collective-permute-start(bf16[128,768]{1,0:T(8,128)(2,1)S(1)} %get-tuple-element.116.refs_1_), channel_id=1, source_target_pairs={{0,2},{1,3},{2,0},{3,1},{4,6},{5,7},{6,4},{7,5},{8,10},{9,11},{10,... | collective-permute-start | bytes 589832 | tf_op jit(solution)/shard_map/ppermute | solution.py:577
  104.6 19.5 %collective-permute-start.30 = (bf16[4,3,96,768]{3,2,1,0:T(8,128)(2,1)S(1)}, bf16[4,3,96,768]{3,2,1,0:T(8,128)(2,1)S(1)}, u32[]{:S(2)}, u32[]{:S(2)}) collective-permute-start(bf16[4,3,96,768]{3,2,1,0:T(8,128)(2,1)S(1)} %get-tuple-element.149), channel_id=1, source_target_pairs={{0,4},{4,0},{8,12},{12,8},{16,20},{20,16},{24,28},{28,24},{1,5},{5... | collective-permute-start | bytes 5308424 | tf_op jit(solution)/shard_map/ppermute | solution.py:574
  104.7 10.5 %collective-permute-start.21 = (bf16[128,768]{1,0:T(8,128)(2,1)S(1)}, bf16[128,768]{1,0:T(8,128)(2,1)S(1)}, u32[]{:S(2)}, u32[]{:S(2)}) collective-permute-start(bf16[128,768]{1,0:T(8,128)(2,1)S(1)} %get-tuple-element.118), channel_id=1, source_target_pairs={{0,1},{1,0},{2,3},{3,2},{4,5},{5,4},{6,7},{7,6},{8,9},{9,8},{10,11... | collective-permute-start | bytes 589832 | tf_op jit(solution)/shard_map/ppermute | solution.py:577
  105.0 17.1 %collective-permute-start.22 = (bf16[128,768]{1,0:T(8,128)(2,1)S(1)}, bf16[128,768]{1,0:T(8,128)(2,1)S(1)}, u32[]{:S(2)}, u32[]{:S(2)}) collective-permute-start(bf16[128,768]{1,0:T(8,128)(2,1)S(1)} %get-tuple-element.119), channel_id=1, source_target_pairs={{0,2},{1,3},{2,0},{3,1},{4,6},{5,7},{6,4},{7,5},{8,10},{9,11},{10,... | collective-permute-start | bytes 589832 | tf_op jit(solution)/shard_map/ppermute | solution.py:577
  106.2 16.0 %collective-permute-start.23 = (bf16[128,768]{1,0:T(8,128)(2,1)S(1)}, bf16[128,768]{1,0:T(8,128)(2,1)S(1)}, u32[]{:S(2)}, u32[]{:S(2)}) collective-permute-start(bf16[128,768]{1,0:T(8,128)(2,1)S(1)} %get-tuple-element.120), channel_id=1, source_target_pairs={{0,3},{1,2},{2,1},{3,0},{4,7},{5,6},{6,5},{7,4},{8,11},{9,10},{10,... | collective-permute-start | bytes 589832 | tf_op jit(solution)/shard_map/ppermute | solution.py:577
  124.5 16.9 %collective-permute-start.31 = (bf16[2,3,96,384]{3,2,1,0:T(8,128)(2,1)S(1)}, bf16[2,3,96,384]{3,2,1,0:T(8,128)(2,1)S(1)}, u32[]{:S(2)}, u32[]{:S(2)}) collective-permute-start(bf16[2,3,96,384]{3,2,1,0:T(8,128)(2,1)S(1)} %get-tuple-element.158), channel_id=1, source_target_pairs={{0,8},{4,12},{8,0},{12,4},{16,24},{20,28},{24,16},{28,20},{1,9},{5... | collective-permute-start | bytes 1327112 | tf_op jit(solution)/shard_map/ppermute | solution.py:574
  126.0 15.4 %collective-permute-start.32 = (bf16[2,3,96,384]{3,2,1,0:T(8,128)(2,1)S(1)}, bf16[2,3,96,384]{3,2,1,0:T(8,128)(2,1)S(1)}, u32[]{:S(2)}, u32[]{:S(2)}) collective-permute-start(bf16[2,3,96,384]{3,2,1,0:T(8,128)(2,1)S(1)} %get-tuple-element.159), channel_id=1, source_target_pairs={{0,16},{4,20},{8,24},{12,28},{16,0},{20,4},{24,8},{28,12},{1,17},{... | collective-permute-start | bytes 1327112 | tf_op jit(solution)/shard_map/ppermute | solution.py:574
  131.5 9.9 %collective-permute-start.25 = (bf16[144,384]{1,0:T(8,128)(2,1)S(1)}, bf16[144,384]{1,0:T(8,128)(2,1)S(1)}, u32[]{:S(2)}, u32[]{:S(2)}) collective-permute-start(bf16[144,384]{1,0:T(8,128)(2,1)S(1)} %get-tuple-element.128), channel_id=1, source_target_pairs={{0,2},{1,3},{2,0},{3,1},{4,6},{5,7},{6,4},{7,5},{8,10},{9,11},{10,... | collective-permute-start | bytes 331784 | tf_op jit(solution)/shard_map/ppermute | solution.py:577
  131.6 9.8 %collective-permute-start.26 = (bf16[144,384]{1,0:T(8,128)(2,1)S(1)}, bf16[144,384]{1,0:T(8,128)(2,1)S(1)}, u32[]{:S(2)}, u32[]{:S(2)}) collective-permute-start(bf16[144,384]{1,0:T(8,128)(2,1)S(1)} %get-tuple-element.129), channel_id=1, source_target_pairs={{0,3},{1,2},{2,1},{3,0},{4,7},{5,6},{6,5},{7,4},{8,11},{9,10},{10,... | collective-permute-start | bytes 331784 | tf_op jit(solution)/shard_map/ppermute | solution.py:577
  150.8 25.6 %collective-permute-start.35 = (bf16[4,112,768]{2,1,0:T(8,128)(2,1)S(1)}, bf16[4,112,768]{2,1,0:T(8,128)(2,1)S(1)}, u32[]{:S(2)}, u32[]{:S(2)}) collective-permute-start(bf16[4,112,768]{2,1,0:T(8,128)(2,1)S(1)} %get-tuple-element.166), channel_id=1, source_target_pairs={{0,4},{4,0},{8,12},{12,8},{16,20},{20,16},{24,28},{28,24},{1,5},{5... | collective-permute-start | bytes 2064392 | tf_op jit(solution)/shard_map/ppermute | solution.py:574
  150.9 23.6 %collective-permute-start.40 = (bf16[3,96,768]{2,1,0:T(8,128)(2,1)S(1)}, bf16[3,96,768]{2,1,0:T(8,128)(2,1)S(1)}, u32[]{:S(2)}, u32[]{:S(2)}) collective-permute-start(bf16[3,96,768]{2,1,0:T(8,128)(2,1)S(1)} %step_three.1.refs_0_), channel_id=1, source_target_pairs={{0,2},{1,3},{2,0},{3,1},{4,6},{5,7},{6,4},{7,5},{8,10},{9,11},{10,... | collective-permute-start | bytes 1327112 | tf_op jit(solution)/shard_map/ppermute | solution.py:577
  153.1 38.0 %collective-permute-start.39 = (bf16[3,96,768]{2,1,0:T(8,128)(2,1)S(1)}, bf16[3,96,768]{2,1,0:T(8,128)(2,1)S(1)}, u32[]{:S(2)}, u32[]{:S(2)}) collective-permute-start(bf16[3,96,768]{2,1,0:T(8,128)(2,1)S(1)} %step_three.1.refs_0_), channel_id=1, source_target_pairs={{0,1},{1,0},{2,3},{3,2},{4,5},{5,4},{6,7},{7,6},{8,9},{9,8},{10,11... | collective-permute-start | bytes 1327112 | tf_op jit(solution)/shard_map/ppermute | solution.py:577
  153.4 29.0 %collective-permute-start.27 = (bf16[128,768]{1,0:T(8,128)(2,1)S(1)}, bf16[128,768]{1,0:T(8,128)(2,1)S(1)}, u32[]{:S(2)}, u32[]{:S(2)}) collective-permute-start(bf16[128,768]{1,0:T(8,128)(2,1)S(1)} %get-tuple-element.136), channel_id=1, source_target_pairs={{0,1},{1,0},{2,3},{3,2},{4,5},{5,4},{6,7},{7,6},{8,9},{9,8},{10,11... | collective-permute-start | bytes 589832 | tf_op jit(solution)/shard_map/ppermute | solution.py:577
  155.1 28.8 %collective-permute-start.28 = (bf16[128,768]{1,0:T(8,128)(2,1)S(1)}, bf16[128,768]{1,0:T(8,128)(2,1)S(1)}, u32[]{:S(2)}, u32[]{:S(2)}) collective-permute-start(bf16[128,768]{1,0:T(8,128)(2,1)S(1)} %get-tuple-element.137), channel_id=1, source_target_pairs={{0,2},{1,3},{2,0},{3,1},{4,6},{5,7},{6,4},{7,5},{8,10},{9,11},{10,... | collective-permute-start | bytes 589832 | tf_op jit(solution)/shard_map/ppermute | solution.py:577
  174.4 14.2 %collective-permute-start.29 = (bf16[128,768]{1,0:T(8,128)(2,1)S(1)}, bf16[128,768]{1,0:T(8,128)(2,1)S(1)}, u32[]{:S(2)}, u32[]{:S(2)}) collective-permute-start(bf16[128,768]{1,0:T(8,128)(2,1)S(1)} %get-tuple-element.138), channel_id=1, source_target_pairs={{0,3},{1,2},{2,1},{3,0},{4,7},{5,6},{6,5},{7,4},{8,11},{9,10},{10,... | collective-permute-start | bytes 589832 | tf_op jit(solution)/shard_map/ppermute | solution.py:577
  176.4 23.1 %collective-permute-start.43 = (bf16[3,96,768]{2,1,0:T(8,128)(2,1)S(1)}, bf16[3,96,768]{2,1,0:T(8,128)(2,1)S(1)}, u32[]{:S(2)}, u32[]{:S(2)}) collective-permute-start(bf16[3,96,768]{2,1,0:T(8,128)(2,1)S(1)} %collective-permute-done.40.refs_2_), channel_id=1, source_target_pairs={{0,1},{1,0},{2,3},{3,2},{4,5},{5,4},{6,7},{7,6},{8,9},{9,8},{10,11... | collective-permute-start | bytes 1327112 | tf_op jit(solution)/shard_map/ppermute | solution.py:577
  182.4 8.7 %collective-permute-start.36 = (bf16[112,768]{1,0:T(8,128)(2,1)S(1)}, bf16[112,768]{1,0:T(8,128)(2,1)S(1)}, u32[]{:S(2)}, u32[]{:S(2)}) collective-permute-start(bf16[112,768]{1,0:T(8,128)(2,1)S(1)} %get-tuple-element.168), channel_id=1, source_target_pairs={{0,8},{4,12},{8,0},{12,4},{16,24},{20,28},{24,16},{28,20},{1,9},{5... | collective-permute-start | bytes 516104 | tf_op jit(solution)/shard_map/ppermute | solution.py:574
  195.1 10.5 %collective-permute-start.42 = (bf16[112,768]{1,0:T(8,128)(2,1)S(1)}, bf16[112,768]{1,0:T(8,128)(2,1)S(1)}, u32[]{:S(2)}, u32[]{:S(2)}) collective-permute-start(bf16[112,768]{1,0:T(8,128)(2,1)S(1)} %plane_sum.1.refs_0_), channel_id=1, source_target_pairs={{0,2},{1,3},{2,0},{3,1},{4,6},{5,7},{6,4},{7,5},{8,10},{9,11},{10,... | collective-permute-start | bytes 516104 | tf_op jit(solution)/shard_map/ppermute | solution.py:577
  (20 other events, 199.4 us)

commit v4 on v3

--- a/solution.py
+++ b/solution.py
@@ -514,7 +514,7 @@
 
 
 def attention_final(ids, *refs):
-    blocks, qkv_out, out, vectors, stage = refs[0:4], refs[4], refs[5], refs[6], refs[7]
+    blocks, qkv_out, out, vectors, stage = refs[0:4], refs[4], refs[5], refs[6:10], refs[10]
     for s in range(SEQ):
         stage[ids[8 + s]] = blocks[s][...].astype(F32)
     shard, model = out.shape
@@ -528,7 +528,9 @@
     for pos in range(1, SEQ):
         sums = sums + stage[pos, shard : shard + 8, :]
     shift = model - ids[0] * shard
-    vectors[...] = pltpu.roll(sums, lax.rem(shift, model), 1)[:, 0:128]
+    moved = pltpu.roll(sums, lax.rem(shift, model), 1)
+    for n in range(4):
+        vectors[n][...] = moved[n : n + 1, 0:shard]
 
 
 def after(values, *deps):
@@ -839,9 +841,9 @@
     )
     attn_near = pass_seq(attn_share, 1)
     attn_far = after(pass_seq(attn_share, 2), grad_gate_up_w, input_grad)
-    grad_qkv_w, grad_out_w, vector_grads = call(
+    grad_qkv_w, grad_out_w, *vector_grads = call(
         attention_final,
-        [((shard, 3 * model), F32), ((shard, model), F32), ((8, 128), F32)],
+        [((shard, 3 * model), F32), ((shard, model), F32)] + [((1, shard), F32)] * 4,
         [ids],
         attn_share,
         attn_near,
@@ -850,7 +852,7 @@
         scratch=[((SEQ, shard + PAD, model), F32)],
     )
 
-    vector_grads = [scatter_outer(vector_grads[n, :shard]) for n in range(4)]
+    vector_grads = [scatter_outer(vector_grads[n].reshape(shard)) for n in range(4)]
     return (
         output[None],
         input_grad[None],

time: 214 us -> 213 us (level)
  no operation moved by 1% of the time
where the time goes in v4:
time: 213 us
  waiting for transfers between devices  105 us (49%)
  starting transfers between devices  60.9 us (29%)
  Pallas kernels  39.2 us (18%)
  local copies, waits for them, and re-layouts  4.99 us (2%)
    ppermute x27, waiting for transfers between devices, pass_seq(): return lax.ppermute(value, 'seq', [(i, i ^ s) for i in range(SEQ)])  94.8 us
    ppermute x27, starting transfers between devices, pass_seq(): return lax.ppermute(value, 'seq', [(i, i ^ s) for i in range(SEQ)])  42.3 us
    pallas_call x18, Pallas kernels, call(): pl.pallas_call(kernel, out_shape=out_shape, in_specs=specs, out_specs=[pl...  39.2 us
    ppermute x18, starting transfers between devices, swap(): return lax.ppermute(value, 'dp', [(i, i ^ s * stride) for i in range(dp)])  18.7 us
    ppermute x18, waiting for transfers between devices, swap(): return lax.ppermute(value, 'dp', [(i, i ^ s * stride) for i in range(dp)])  10.5 us
  transfers between devices with their start and end apart: 45, of which 25 were waited for; matrix products, arithmetic and copies ran while one was open for 1% of the time, Pallas kernels for 10%

profile of v4, /device:TPU:0, one launch (start us, length us, event | category | flops | bytes accessed | tf_op | source)
XLA Modules:
  0.0 212.9 jit_solution(10088701698284033610)
XLA Ops:
  1.9 4.0 %collective-permute-start.5 = (bf16[96,576]{1,0:T(8,128)(2,1)S(1)}, bf16[96,576]{1,0:T(8,128)(2,1)S(1)}, u32[]{:S(2)}, u32[]{:S(2)}) collective-permute-start(bf16[96,576]{1,0:T(8,128)(2,1)S(1)} %pad_maximum_fusion.3.refs_4_), channel_id=1, source_target_pairs={{0,24},{4,28},{8,16},{12,20},{16,8},{20,12},{24,0},{28,4},{1,25},{... | collective-permute-start | bytes 331784 | tf_op jit(solution)/shard_map/ppermute | solution.py:576
  6.6 3.0 %collective-permute-start.1 = (bf16[128,768]{1,0:T(8,128)(2,1)}, bf16[128,768]{1,0:T(8,128)(2,1)S(1)}, u32[]{:S(2)}, u32[]{:S(2)}) collective-permute-start(bf16[128,768]{1,0:T(8,128)(2,1)} %bitcast.12), channel_id=1, source_target_pairs={{0,2},{1,3},{2,0},{3,1},{4,6},{5,7},{6,4},{7,5},{8,10},{9,11},{10,... | collective-permute-start | bytes 589832 | tf_op jit(solution)/shard_map/ppermute | solution.py:579
  23.1 5.8 %collective-permute-done.2.refs_3_.refs_7_.refs_4_ = bf16[128,768]{1,0:T(8,128)(2,1)S(1)} collective-permute-done((bf16[128,768]{1,0:T(8,128)(2,1)S(1)}, bf16[128,768]{1,0:T(8,128)(2,1)S(1)}, u32[]{:S(2)}, u32[]{:S(2)}) %collective-permute-start.2) | collective-permute-done | bytes 196640 | tf_op jit(solution)/shard_map/ppermute | solution.py:579
  28.9 6.4 %attention_forward.1 = (bf16[768,128]{1,0:T(8,128)(2,1)S(1)}, bf16[512,192]{1,0:T(8,128)(2,1)S(1)}, bf16[512,192]{1,0:T(8,128)(2,1)S(1)}, bf16[512,192]{1,0:T(8,...) custom-call(s32[12]{0:T(128)S(1)} %pad_add_fusion.ids, s32[1,8]{1,0:T(1,128)S(1)} %copy-done.5, ...), custom_call_target="tpu_custom_call" | custom-call | flops 654311424 | bytes 4915200 | tf_op jit(solution)/shard_map/attention_forward/pallas_call | solution.py:83
  38.5 2.8 %collective-permute-start.7 = (bf16[768,128]{1,0:T(8,128)(2,1)S(1)}, bf16[768,128]{1,0:T(8,128)(2,1)S(1)}, u32[]{:S(2)}, u32[]{:S(2)}) collective-permute-start(bf16[768,128]{1,0:T(8,128)(2,1)S(1)} %get-tuple-element.100.refs_0_), channel_id=1, source_target_pairs={{0,1},{1,0},{2,3},{3,2},{4,5},{5,4},{6,7},{7,6},{8,9},{9,8},{10,11... | collective-permute-start | bytes 589832 | tf_op jit(solution)/shard_map/ppermute | solution.py:579
  41.3 2.9 %collective-permute-done.13 = bf16[400,384]{1,0:T(8,128)(2,1)S(1)} collective-permute-done((bf16[400,384]{1,0:T(8,128)(2,1)S(1)}, bf16[400,384]{1,0:T(8,128)(2,1)S(1)}, u32[]{:S(2)}, u32[]{:S(2)}) %collective-permute-start.13) | collective-permute-done | bytes 307232 | tf_op jit(solution)/shard_map/ppermute | solution.py:576
  44.6 2.9 %collective-permute-done.8.refs_2_ = bf16[768,128]{1,0:T(8,128)(2,1)S(1)} collective-permute-done((bf16[768,128]{1,0:T(8,128)(2,1)S(1)}, bf16[768,128]{1,0:T(8,128)(2,1)S(1)}, u32[]{:S(2)}, u32[]{:S(2)}) %collective-permute-start.8) | collective-permute-done | bytes 196640 | tf_op jit(solution)/shard_map/ppermute | solution.py:579
  49.5 3.4 %collective-permute-done.14.refs_4_ = bf16[1600,768]{1,0:T(8,128)(2,1)S(1)} collective-permute-done((bf16[1600,768]{1,0:T(8,128)(2,1)S(1)}, bf16[1600,768]{1,0:T(8,128)(2,1)S(1)}, u32[]{:S(2)}, u32[]{:S(2)}) %collective-permute-start.14) | collective-permute-done | bytes 2457632 | tf_op jit(solution)/shard_map/ppermute | solution.py:576
  55.5 4.2 %middle_forward.1 = (f32[128,768]{1,0:T(8,128)S(1)}, bf16[128,768]{1,0:T(8,128)(2,1)S(1)}, bf16[128,768]{1,0:T(8,128)(2,1)S(1)}, bf16[128,768]{1,0:T(8,128)(2,1)...) custom-call(s32[12]{0:T(128)S(1)} %pad_add_fusion.ids, ...), custom_call_target="tpu_custom_call" | custom-call | flops 2415919104 | bytes 9269248 | tf_op jit(solution)/shard_map/middle_forward/pallas_call | solution.py:83
  61.0 2.3 %collective-permute-start.16 = (bf16[128,768]{1,0:T(8,128)(2,1)S(1)}, bf16[128,768]{1,0:T(8,128)(2,1)S(1)}, u32[]{:S(2)}, u32[]{:S(2)}) collective-permute-start(bf16[128,768]{1,0:T(8,128)(2,1)S(1)} %get-tuple-element.114), channel_id=1, source_target_pairs={{0,2},{1,3},{2,0},{3,1},{4,6},{5,7},{6,4},{7,5},{8,10},{9,11},{10,... | collective-permute-start | bytes 589832 | tf_op jit(solution)/shard_map/ppermute | solution.py:579
  64.2 5.2 %collective-permute-done.15.refs_1_ = bf16[128,768]{1,0:T(8,128)(2,1)S(1)} collective-permute-done((bf16[128,768]{1,0:T(8,128)(2,1)S(1)}, bf16[128,768]{1,0:T(8,128)(2,1)S(1)}, u32[]{:S(2)}, u32[]{:S(2)}) %collective-permute-start.15) | collective-permute-done | bytes 196640 | tf_op jit(solution)/shard_map/ppermute | solution.py:579
  69.5 8.6 %collective-permute-done.16.refs_2_ = bf16[128,768]{1,0:T(8,128)(2,1)S(1)} collective-permute-done((bf16[128,768]{1,0:T(8,128)(2,1)S(1)}, bf16[128,768]{1,0:T(8,128)(2,1)S(1)}, u32[]{:S(2)}, u32[]{:S(2)}) %collective-permute-start.16) | collective-permute-done | bytes 196640 | tf_op jit(solution)/shard_map/ppermute | solution.py:579
  79.2 4.0 %collective-permute-start.19 = (bf16[128,768]{1,0:T(8,128)(2,1)S(1)}, bf16[128,768]{1,0:T(8,128)(2,1)S(1)}, u32[]{:S(2)}, u32[]{:S(2)}) collective-permute-start(bf16[128,768]{1,0:T(8,128)(2,1)S(1)} %get-tuple-element.119.refs_1_), channel_id=1, source_target_pairs={{0,2},{1,3},{2,0},{3,1},{4,6},{5,7},{6,4},{7,5},{8,10},{9,11},{10,... | collective-permute-start | bytes 589832 | tf_op jit(solution)/shard_map/ppermute | solution.py:579
  83.2 8.0 %collective-permute-done.19.refs_3_ = bf16[128,768]{1,0:T(8,128)(2,1)S(1)} collective-permute-done((bf16[128,768]{1,0:T(8,128)(2,1)S(1)}, bf16[128,768]{1,0:T(8,128)(2,1)S(1)}, u32[]{:S(2)}, u32[]{:S(2)}) %collective-permute-start.19) | collective-permute-done | bytes 196640 | tf_op jit(solution)/shard_map/ppermute | solution.py:579
  91.7 5.5 %collective-permute-done.20.refs_4_ = bf16[128,768]{1,0:T(8,128)(2,1)S(1)} collective-permute-done((bf16[128,768]{1,0:T(8,128)(2,1)S(1)}, bf16[128,768]{1,0:T(8,128)(2,1)S(1)}, u32[]{:S(2)}, u32[]{:S(2)}) %collective-permute-start.20) | collective-permute-done | bytes 196640 | tf_op jit(solution)/shard_map/ppermute | solution.py:579
  97.1 4.4 %feed_back.1 = (f32[128,768]{1,0:T(8,128)S(1)}, bf16[128,768]{1,0:T(8,128)(2,1)S(1)}, bf16[128,768]{1,0:T(8,128)(2,1)S(1)}, bf16[128,768]{1,0:T(8,128)(2,1)S(1)}...) custom-call(bf16[512,768]{1,0:T(8,128)(2,1)S(1)} %get-tuple-element., ...), custom_call_target="tpu_custom_call" | custom-call | flops 3019898880 | bytes 9240576 | tf_op jit(solution)/shard_map/feed_back/pallas_call | solution.py:83
  101.5 3.1 %feed_weights.1 = (f32[4,3,96,768]{3,2,1,0:T(8,128)S(1)}, bf16[4,3,96,768]{3,2,1,0:T(8,128)(2,1)S(1)}) custom-call(s32[12]{0:T(128)S(1)} %pad_add_fusion.ids, bf16[512,768]{1,0:T(8,128)(2,1)S(1)} %get-tuple-element.116.refs_4_.refs_0_, bf16[512,768]{1,0:T(8,128)(2,1)S(1)} %get-tuple-element.146.refs_1_, bf16[512,768]{1,0:T(8,128)(2,1)S(1)} %get-tuple-element.147.refs_2_, ...), custom_call_target="tpu_custom_call" | custom-call | flops 1811939328 | bytes 9240576 | tf_op jit(solution)/shard_map/feed_weights/pallas_call | solution.py:83
  106.2 2.9 %collective-permute-start.23 = (bf16[128,768]{1,0:T(8,128)(2,1)S(1)}, bf16[128,768]{1,0:T(8,128)(2,1)S(1)}, u32[]{:S(2)}, u32[]{:S(2)}) collective-permute-start(bf16[128,768]{1,0:T(8,128)(2,1)S(1)} %get-tuple-element.123), channel_id=1, source_target_pairs={{0,3},{1,2},{2,1},{3,0},{4,7},{5,6},{6,5},{7,4},{8,11},{9,10},{10,... | collective-permute-start | bytes 589832 | tf_op jit(solution)/shard_map/ppermute | solution.py:579
  109.1 6.0 %collective-permute-done.21.refs_1_ = bf16[128,768]{1,0:T(8,128)(2,1)S(1)} collective-permute-done((bf16[128,768]{1,0:T(8,128)(2,1)S(1)}, bf16[128,768]{1,0:T(8,128)(2,1)S(1)}, u32[]{:S(2)}, u32[]{:S(2)}) %collective-permute-start.21) | collective-permute-done | bytes 196640 | tf_op jit(solution)/shard_map/ppermute | solution.py:579
  115.2 7.0 %collective-permute-done.22.refs_2_ = bf16[128,768]{1,0:T(8,128)(2,1)S(1)} collective-permute-done((bf16[128,768]{1,0:T(8,128)(2,1)S(1)}, bf16[128,768]{1,0:T(8,128)(2,1)S(1)}, u32[]{:S(2)}, u32[]{:S(2)}) %collective-permute-start.22) | collective-permute-done | bytes 196640 | tf_op jit(solution)/shard_map/ppermute | solution.py:579
  127.5 3.9 %collective-permute-start.24 = (bf16[144,384]{1,0:T(8,128)(2,1)S(1)}, bf16[144,384]{1,0:T(8,128)(2,1)S(1)}, u32[]{:S(2)}, u32[]{:S(2)}) collective-permute-start(bf16[144,384]{1,0:T(8,128)(2,1)S(1)} %get-tuple-element.130), channel_id=1, source_target_pairs={{0,1},{1,0},{2,3},{3,2},{4,5},{5,4},{6,7},{7,6},{8,9},{9,8},{10,11... | collective-permute-start | bytes 331784 | tf_op jit(solution)/shard_map/ppermute | solution.py:579
  131.6 2.3 %collective-permute-start.26 = (bf16[144,384]{1,0:T(8,128)(2,1)S(1)}, bf16[144,384]{1,0:T(8,128)(2,1)S(1)}, u32[]{:S(2)}, u32[]{:S(2)}) collective-permute-start(bf16[144,384]{1,0:T(8,128)(2,1)S(1)} %get-tuple-element.132), channel_id=1, source_target_pairs={{0,3},{1,2},{2,1},{3,0},{4,7},{5,6},{6,5},{7,4},{8,11},{9,10},{10,... | collective-permute-start | bytes 331784 | tf_op jit(solution)/shard_map/ppermute | solution.py:579
  134.9 6.4 %collective-permute-done.25.refs_2_.refs_7_.refs_8_ = bf16[144,384]{1,0:T(8,128)(2,1)S(1)} collective-permute-done((bf16[144,384]{1,0:T(8,128)(2,1)S(1)}, bf16[144,384]{1,0:T(8,128)(2,1)S(1)}, u32[]{:S(2)}, u32[]{:S(2)}) %collective-permute-start.25) | collective-permute-done | bytes 110624 | tf_op jit(solution)/shard_map/ppermute | solution.py:579
  142.6 6.0 %attention_back.1 = (f32[128,768]{1,0:T(8,128)S(1)}, bf16[128,768]{1,0:T(8,128)(2,1)S(1)}, bf16[128,768]{1,0:T(8,128)(2,1)S(1)}, bf16[128,768]{1,0:T(8,128)(2,1)S(1)}, bf16[512,576]{1,0:T(8,128)(2,1)S(1)}) custom-call(bf16[144,384]{1,0:T(8,128)(2,1)S(1)} %get-tuple-element.129.refs_0_.refs_6_, ...), custom_call_target="tpu_custom_call" | custom-call | flops 956301312 | bytes 5062656 | tf_op jit(solution)/shard_map/attention_back/pallas_call | solution.py:83
  156.0 18.5 %collective-permute-done.40.refs_2_ = bf16[3,96,768]{2,1,0:T(8,128)(2,1)S(1)} collective-permute-done((bf16[3,96,768]{2,1,0:T(8,128)(2,1)S(1)}, bf16[3,96,768]{2,1,0:T(8,128)(2,1)S(1)}, u32[]{:S(2)}, u32[]{:S(2)}) %collective-permute-start.40) | collective-permute-done | bytes 442400 | tf_op jit(solution)/shard_map/ppermute | solution.py:579
  176.5 5.9 %collective-permute-done.27.refs_2_ = bf16[128,768]{1,0:T(8,128)(2,1)S(1)} collective-permute-done((bf16[128,768]{1,0:T(8,128)(2,1)S(1)}, bf16[128,768]{1,0:T(8,128)(2,1)S(1)}, u32[]{:S(2)}, u32[]{:S(2)}) %collective-permute-start.27) | collective-permute-done | bytes 196640 | tf_op jit(solution)/shard_map/ppermute | solution.py:579
  185.4 3.3 %collective-permute-done.29.refs_4_ = bf16[128,768]{1,0:T(8,128)(2,1)S(1)} collective-permute-done((bf16[128,768]{1,0:T(8,128)(2,1)S(1)}, bf16[128,768]{1,0:T(8,128)(2,1)S(1)}, u32[]{:S(2)}, u32[]{:S(2)}) %collective-permute-start.29) | collective-permute-done | bytes 196640 | tf_op jit(solution)/shard_map/ppermute | solution.py:579
  188.7 2.4 %collective-permute-start.38 = (bf16[112,768]{1,0:T(8,128)(2,1)S(1)}, bf16[112,768]{1,0:T(8,128)(2,1)S(1)}, u32[]{:S(2)}, u32[]{:S(2)}) collective-permute-start(bf16[112,768]{1,0:T(8,128)(2,1)S(1)} %get-tuple-element.173), channel_id=1, source_target_pairs={{0,24},{4,28},{8,16},{12,20},{16,8},{20,12},{24,0},{28,4},{1,25},{... | collective-permute-start | bytes 516104 | tf_op jit(solution)/shard_map/ppermute | solution.py:576
  191.1 3.9 %collective-permute-done.38.refs_3_ = bf16[112,768]{1,0:T(8,128)(2,1)S(1)} collective-permute-done((bf16[112,768]{1,0:T(8,128)(2,1)S(1)}, bf16[112,768]{1,0:T(8,128)(2,1)S(1)}, u32[]{:S(2)}, u32[]{:S(2)}) %collective-permute-start.38) | collective-permute-done | bytes 172064 | tf_op jit(solution)/shard_map/ppermute | solution.py:576
  195.1 3.6 %collective-permute-start.42 = (bf16[112,768]{1,0:T(8,128)(2,1)S(1)}, bf16[112,768]{1,0:T(8,128)(2,1)S(1)}, u32[]{:S(2)}, u32[]{:S(2)}) collective-permute-start(bf16[112,768]{1,0:T(8,128)(2,1)S(1)} %plane_sum.1.refs_0_), channel_id=1, source_target_pairs={{0,2},{1,3},{2,0},{3,1},{4,6},{5,7},{6,4},{7,5},{8,10},{9,11},{10,... | collective-permute-start | bytes 516104 | tf_op jit(solution)/shard_map/ppermute | solution.py:579
  199.4 4.5 %feed_final.1 = (f32[96,6144]{1,0:T(8,128)}, f32[384,768]{1,0:T(8,128)}) custom-call(s32[12]{0:T(128)S(1)} %pad_add_fusion.ids, bf16[3,96,768]{2,1,0:T(8,128)(2,1)S(1)} %step_three.1.refs_0_, bf16[3,96,768]{2,1,0:T(8,128)(2,1)S(1)} %collective-permute-done.39.refs_1_, bf16[3,96,768]{2,1,0:T(8,128)(2,1)S(1)} %collective-permute-done.40.refs_2_, ...), custom_call_target="tpu_custom_call" | custom-call | bytes 5308416 | tf_op jit(solution)/shard_map/feed_final/pallas_call | solution.py:83
  207.0 4.0 %collective-permute-done.44.refs_3_ = bf16[112,768]{1,0:T(8,128)(2,1)S(1)} collective-permute-done((bf16[112,768]{1,0:T(8,128)(2,1)S(1)}, bf16[112,768]{1,0:T(8,128)(2,1)S(1)}, u32[]{:S(2)}, u32[]{:S(2)}) %collective-permute-start.44) | collective-permute-done | bytes 172064 | tf_op jit(solution)/shard_map/ppermute | solution.py:579
  (102 shorter events, 54.7 us)
Async XLA Ops:
  1.9 14.4 %collective-permute-start.5 = (bf16[96,576]{1,0:T(8,128)(2,1)S(1)}, bf16[96,576]{1,0:T(8,128)(2,1)S(1)}, u32[]{:S(2)}, u32[]{:S(2)}) collective-permute-start(bf16[96,576]{1,0:T(8,128)(2,1)S(1)} %pad_maximum_fusion.3.refs_4_), channel_id=1, source_target_pairs={{0,24},{4,28},{8,16},{12,20},{16,8},{20,12},{24,0},{28,4},{1,25},{... | collective-permute-start | bytes 331784 | tf_op jit(solution)/shard_map/ppermute | solution.py:576
  5.9 10.5 %collective-permute-start.4 = (bf16[96,576]{1,0:T(8,128)(2,1)S(1)}, bf16[96,576]{1,0:T(8,128)(2,1)S(1)}, u32[]{:S(2)}, u32[]{:S(2)}) collective-permute-start(bf16[96,576]{1,0:T(8,128)(2,1)S(1)} %pad_maximum_fusion.3.refs_4_), channel_id=1, source_target_pairs={{0,16},{4,20},{8,24},{12,28},{16,0},{20,4},{24,8},{28,12},{1,17},{... | collective-permute-start | bytes 331784 | tf_op jit(solution)/shard_map/ppermute | solution.py:576
  6.4 10.0 %collective-permute-start.3 = (bf16[96,576]{1,0:T(8,128)(2,1)S(1)}, bf16[96,576]{1,0:T(8,128)(2,1)S(1)}, u32[]{:S(2)}, u32[]{:S(2)}) collective-permute-start(bf16[96,576]{1,0:T(8,128)(2,1)S(1)} %pad_maximum_fusion.3.refs_4_), channel_id=1, source_target_pairs={{0,8},{4,12},{8,0},{12,4},{16,24},{20,28},{24,16},{28,20},{1,9},{5... | collective-permute-start | bytes 331784 | tf_op jit(solution)/shard_map/ppermute | solution.py:576
  6.6 11.6 %collective-permute-start.1 = (bf16[128,768]{1,0:T(8,128)(2,1)}, bf16[128,768]{1,0:T(8,128)(2,1)S(1)}, u32[]{:S(2)}, u32[]{:S(2)}) collective-permute-start(bf16[128,768]{1,0:T(8,128)(2,1)} %bitcast.12), channel_id=1, source_target_pairs={{0,2},{1,3},{2,0},{3,1},{4,6},{5,7},{6,4},{7,5},{8,10},{9,11},{10,... | collective-permute-start | bytes 589832 | tf_op jit(solution)/shard_map/ppermute | solution.py:579
  9.6 8.8 %collective-permute-start = (bf16[128,768]{1,0:T(8,128)(2,1)}, bf16[128,768]{1,0:T(8,128)(2,1)S(1)}, u32[]{:S(2)}, u32[]{:S(2)}) collective-permute-start(bf16[128,768]{1,0:T(8,128)(2,1)} %bitcast.13), channel_id=1, source_target_pairs={{0,1},{1,0},{2,3},{3,2},{4,5},{5,4},{6,7},{7,6},{8,9},{9,8},{10,11... | collective-permute-start | bytes 589832 | tf_op jit(solution)/shard_map/ppermute | solution.py:579
  18.4 17.0 %collective-permute-start.11 = (bf16[400,768]{1,0:T(8,128)(2,1)S(1)}, bf16[400,768]{1,0:T(8,128)(2,1)S(1)}, u32[]{:S(2)}, u32[]{:S(2)}) collective-permute-start(bf16[400,768]{1,0:T(8,128)(2,1)S(1)} %select_units.1.refs_0_), channel_id=1, source_target_pairs={{0,16},{4,20},{8,24},{12,28},{16,0},{20,4},{24,8},{28,12},{1,17},{... | collective-permute-start | bytes 1843208 | tf_op jit(solution)/shard_map/ppermute | solution.py:576
  20.0 15.4 %collective-permute-start.10 = (bf16[400,768]{1,0:T(8,128)(2,1)S(1)}, bf16[400,768]{1,0:T(8,128)(2,1)S(1)}, u32[]{:S(2)}, u32[]{:S(2)}) collective-permute-start(bf16[400,768]{1,0:T(8,128)(2,1)S(1)} %select_units.1.refs_0_), channel_id=1, source_target_pairs={{0,8},{4,12},{8,0},{12,4},{16,24},{20,28},{24,16},{28,20},{1,9},{5... | collective-permute-start | bytes 1843208 | tf_op jit(solution)/shard_map/ppermute | solution.py:576
  35.4 8.8 %collective-permute-start.13 = (bf16[400,384]{1,0:T(8,128)(2,1)S(1)}, bf16[400,384]{1,0:T(8,128)(2,1)S(1)}, u32[]{:S(2)}, u32[]{:S(2)}) collective-permute-start(bf16[400,384]{1,0:T(8,128)(2,1)S(1)} %slice.10), channel_id=1, source_target_pairs={{0,8},{4,12},{8,0},{12,4},{16,24},{20,28},{24,16},{28,20},{1,9},{5... | collective-permute-start | bytes 921608 | tf_op jit(solution)/shard_map/ppermute | solution.py:576
  36.0 8.5 %collective-permute-start.12 = (bf16[400,384]{1,0:T(8,128)(2,1)S(1)}, bf16[400,384]{1,0:T(8,128)(2,1)S(1)}, u32[]{:S(2)}, u32[]{:S(2)}) collective-permute-start(bf16[400,384]{1,0:T(8,128)(2,1)S(1)} %slice.9), channel_id=1, source_target_pairs={{0,16},{4,20},{8,24},{12,28},{16,0},{20,4},{24,8},{28,12},{1,17},{... | collective-permute-start | bytes 921608 | tf_op jit(solution)/shard_map/ppermute | solution.py:576
  36.5 10.9 %collective-permute-start.8 = (bf16[768,128]{1,0:T(8,128)(2,1)S(1)}, bf16[768,128]{1,0:T(8,128)(2,1)S(1)}, u32[]{:S(2)}, u32[]{:S(2)}) collective-permute-start(bf16[768,128]{1,0:T(8,128)(2,1)S(1)} %get-tuple-element.100.refs_0_), channel_id=1, source_target_pairs={{0,2},{1,3},{2,0},{3,1},{4,6},{5,7},{6,4},{7,5},{8,10},{9,11},{10,... | collective-permute-start | bytes 589832 | tf_op jit(solution)/shard_map/ppermute | solution.py:579
  38.5 9.2 %collective-permute-start.7 = (bf16[768,128]{1,0:T(8,128)(2,1)S(1)}, bf16[768,128]{1,0:T(8,128)(2,1)S(1)}, u32[]{:S(2)}, u32[]{:S(2)}) collective-permute-start(bf16[768,128]{1,0:T(8,128)(2,1)S(1)} %get-tuple-element.100.refs_0_), channel_id=1, source_target_pairs={{0,1},{1,0},{2,3},{3,2},{4,5},{5,4},{6,7},{7,6},{8,9},{9,8},{10,11... | collective-permute-start | bytes 589832 | tf_op jit(solution)/shard_map/ppermute | solution.py:579
  59.8 9.7 %collective-permute-start.15 = (bf16[128,768]{1,0:T(8,128)(2,1)S(1)}, bf16[128,768]{1,0:T(8,128)(2,1)S(1)}, u32[]{:S(2)}, u32[]{:S(2)}) collective-permute-start(bf16[128,768]{1,0:T(8,128)(2,1)S(1)} %get-tuple-element.113), channel_id=1, source_target_pairs={{0,1},{1,0},{2,3},{3,2},{4,5},{5,4},{6,7},{7,6},{8,9},{9,8},{10,11... | collective-permute-start | bytes 589832 | tf_op jit(solution)/shard_map/ppermute | solution.py:579
  61.0 17.1 %collective-permute-start.16 = (bf16[128,768]{1,0:T(8,128)(2,1)S(1)}, bf16[128,768]{1,0:T(8,128)(2,1)S(1)}, u32[]{:S(2)}, u32[]{:S(2)}) collective-permute-start(bf16[128,768]{1,0:T(8,128)(2,1)S(1)} %get-tuple-element.114), channel_id=1, source_target_pairs={{0,2},{1,3},{2,0},{3,1},{4,6},{5,7},{6,4},{7,5},{8,10},{9,11},{10,... | collective-permute-start | bytes 589832 | tf_op jit(solution)/shard_map/ppermute | solution.py:579
  63.3 14.8 %collective-permute-start.17 = (bf16[128,768]{1,0:T(8,128)(2,1)S(1)}, bf16[128,768]{1,0:T(8,128)(2,1)S(1)}, u32[]{:S(2)}, u32[]{:S(2)}) collective-permute-start(bf16[128,768]{1,0:T(8,128)(2,1)S(1)} %get-tuple-element.115), channel_id=1, source_target_pairs={{0,3},{1,2},{2,1},{3,0},{4,7},{5,6},{6,5},{7,4},{8,11},{9,10},{10,... | collective-permute-start | bytes 589832 | tf_op jit(solution)/shard_map/ppermute | solution.py:579
  79.2 12.0 %collective-permute-start.19 = (bf16[128,768]{1,0:T(8,128)(2,1)S(1)}, bf16[128,768]{1,0:T(8,128)(2,1)S(1)}, u32[]{:S(2)}, u32[]{:S(2)}) collective-permute-start(bf16[128,768]{1,0:T(8,128)(2,1)S(1)} %get-tuple-element.119.refs_1_), channel_id=1, source_target_pairs={{0,2},{1,3},{2,0},{3,1},{4,6},{5,7},{6,4},{7,5},{8,10},{9,11},{10,... | collective-permute-start | bytes 589832 | tf_op jit(solution)/shard_map/ppermute | solution.py:579
  104.6 19.5 %collective-permute-start.30 = (bf16[4,3,96,768]{3,2,1,0:T(8,128)(2,1)S(1)}, bf16[4,3,96,768]{3,2,1,0:T(8,128)(2,1)S(1)}, u32[]{:S(2)}, u32[]{:S(2)}) collective-permute-start(bf16[4,3,96,768]{3,2,1,0:T(8,128)(2,1)S(1)} %get-tuple-element.152), channel_id=1, source_target_pairs={{0,4},{4,0},{8,12},{12,8},{16,20},{20,16},{24,28},{28,24},{1,5},{5... | collective-permute-start | bytes 5308424 | tf_op jit(solution)/shard_map/ppermute | solution.py:576
  104.7 10.5 %collective-permute-start.21 = (bf16[128,768]{1,0:T(8,128)(2,1)S(1)}, bf16[128,768]{1,0:T(8,128)(2,1)S(1)}, u32[]{:S(2)}, u32[]{:S(2)}) collective-permute-start(bf16[128,768]{1,0:T(8,128)(2,1)S(1)} %get-tuple-element.121), channel_id=1, source_target_pairs={{0,1},{1,0},{2,3},{3,2},{4,5},{5,4},{6,7},{7,6},{8,9},{9,8},{10,11... | collective-permute-start | bytes 589832 | tf_op jit(solution)/shard_map/ppermute | solution.py:579
  105.0 17.1 %collective-permute-start.22 = (bf16[128,768]{1,0:T(8,128)(2,1)S(1)}, bf16[128,768]{1,0:T(8,128)(2,1)S(1)}, u32[]{:S(2)}, u32[]{:S(2)}) collective-permute-start(bf16[128,768]{1,0:T(8,128)(2,1)S(1)} %get-tuple-element.122), channel_id=1, source_target_pairs={{0,2},{1,3},{2,0},{3,1},{4,6},{5,7},{6,4},{7,5},{8,10},{9,11},{10,... | collective-permute-start | bytes 589832 | tf_op jit(solution)/shard_map/ppermute | solution.py:579
  106.2 16.0 %collective-permute-start.23 = (bf16[128,768]{1,0:T(8,128)(2,1)S(1)}, bf16[128,768]{1,0:T(8,128)(2,1)S(1)}, u32[]{:S(2)}, u32[]{:S(2)}) collective-permute-start(bf16[128,768]{1,0:T(8,128)(2,1)S(1)} %get-tuple-element.123), channel_id=1, source_target_pairs={{0,3},{1,2},{2,1},{3,0},{4,7},{5,6},{6,5},{7,4},{8,11},{9,10},{10,... | collective-permute-start | bytes 589832 | tf_op jit(solution)/shard_map/ppermute | solution.py:579
  124.4 16.9 %collective-permute-start.31 = (bf16[2,3,96,384]{3,2,1,0:T(8,128)(2,1)S(1)}, bf16[2,3,96,384]{3,2,1,0:T(8,128)(2,1)S(1)}, u32[]{:S(2)}, u32[]{:S(2)}) collective-permute-start(bf16[2,3,96,384]{3,2,1,0:T(8,128)(2,1)S(1)} %get-tuple-element.161), channel_id=1, source_target_pairs={{0,8},{4,12},{8,0},{12,4},{16,24},{20,28},{24,16},{28,20},{1,9},{5... | collective-permute-start | bytes 1327112 | tf_op jit(solution)/shard_map/ppermute | solution.py:576
  126.0 15.3 %collective-permute-start.32 = (bf16[2,3,96,384]{3,2,1,0:T(8,128)(2,1)S(1)}, bf16[2,3,96,384]{3,2,1,0:T(8,128)(2,1)S(1)}, u32[]{:S(2)}, u32[]{:S(2)}) collective-permute-start(bf16[2,3,96,384]{3,2,1,0:T(8,128)(2,1)S(1)} %get-tuple-element.162), channel_id=1, source_target_pairs={{0,16},{4,20},{8,24},{12,28},{16,0},{20,4},{24,8},{28,12},{1,17},{... | collective-permute-start | bytes 1327112 | tf_op jit(solution)/shard_map/ppermute | solution.py:576
  131.5 9.9 %collective-permute-start.25 = (bf16[144,384]{1,0:T(8,128)(2,1)S(1)}, bf16[144,384]{1,0:T(8,128)(2,1)S(1)}, u32[]{:S(2)}, u32[]{:S(2)}) collective-permute-start(bf16[144,384]{1,0:T(8,128)(2,1)S(1)} %get-tuple-element.131), channel_id=1, source_target_pairs={{0,2},{1,3},{2,0},{3,1},{4,6},{5,7},{6,4},{7,5},{8,10},{9,11},{10,... | collective-permute-start | bytes 331784 | tf_op jit(solution)/shard_map/ppermute | solution.py:579
  131.6 9.8 %collective-permute-start.26 = (bf16[144,384]{1,0:T(8,128)(2,1)S(1)}, bf16[144,384]{1,0:T(8,128)(2,1)S(1)}, u32[]{:S(2)}, u32[]{:S(2)}) collective-permute-start(bf16[144,384]{1,0:T(8,128)(2,1)S(1)} %get-tuple-element.132), channel_id=1, source_target_pairs={{0,3},{1,2},{2,1},{3,0},{4,7},{5,6},{6,5},{7,4},{8,11},{9,10},{10,... | collective-permute-start | bytes 331784 | tf_op jit(solution)/shard_map/ppermute | solution.py:579
  150.8 25.6 %collective-permute-start.35 = (bf16[4,112,768]{2,1,0:T(8,128)(2,1)S(1)}, bf16[4,112,768]{2,1,0:T(8,128)(2,1)S(1)}, u32[]{:S(2)}, u32[]{:S(2)}) collective-permute-start(bf16[4,112,768]{2,1,0:T(8,128)(2,1)S(1)} %get-tuple-element.169), channel_id=1, source_target_pairs={{0,4},{4,0},{8,12},{12,8},{16,20},{20,16},{24,28},{28,24},{1,5},{5... | collective-permute-start | bytes 2064392 | tf_op jit(solution)/shard_map/ppermute | solution.py:576
  150.9 23.6 %collective-permute-start.40 = (bf16[3,96,768]{2,1,0:T(8,128)(2,1)S(1)}, bf16[3,96,768]{2,1,0:T(8,128)(2,1)S(1)}, u32[]{:S(2)}, u32[]{:S(2)}) collective-permute-start(bf16[3,96,768]{2,1,0:T(8,128)(2,1)S(1)} %step_three.1.refs_0_), channel_id=1, source_target_pairs={{0,2},{1,3},{2,0},{3,1},{4,6},{5,7},{6,4},{7,5},{8,10},{9,11},{10,... | collective-permute-start | bytes 1327112 | tf_op jit(solution)/shard_map/ppermute | solution.py:579
  153.1 38.0 %collective-permute-start.39 = (bf16[3,96,768]{2,1,0:T(8,128)(2,1)S(1)}, bf16[3,96,768]{2,1,0:T(8,128)(2,1)S(1)}, u32[]{:S(2)}, u32[]{:S(2)}) collective-permute-start(bf16[3,96,768]{2,1,0:T(8,128)(2,1)S(1)} %step_three.1.refs_0_), channel_id=1, source_target_pairs={{0,1},{1,0},{2,3},{3,2},{4,5},{5,4},{6,7},{7,6},{8,9},{9,8},{10,11... | collective-permute-start | bytes 1327112 | tf_op jit(solution)/shard_map/ppermute | solution.py:579
  153.4 29.0 %collective-permute-start.27 = (bf16[128,768]{1,0:T(8,128)(2,1)S(1)}, bf16[128,768]{1,0:T(8,128)(2,1)S(1)}, u32[]{:S(2)}, u32[]{:S(2)}) collective-permute-start(bf16[128,768]{1,0:T(8,128)(2,1)S(1)} %get-tuple-element.139), channel_id=1, source_target_pairs={{0,1},{1,0},{2,3},{3,2},{4,5},{5,4},{6,7},{7,6},{8,9},{9,8},{10,11... | collective-permute-start | bytes 589832 | tf_op jit(solution)/shard_map/ppermute | solution.py:579
  155.1 28.7 %collective-permute-start.28 = (bf16[128,768]{1,0:T(8,128)(2,1)S(1)}, bf16[128,768]{1,0:T(8,128)(2,1)S(1)}, u32[]{:S(2)}, u32[]{:S(2)}) collective-permute-start(bf16[128,768]{1,0:T(8,128)(2,1)S(1)} %get-tuple-element.140), channel_id=1, source_target_pairs={{0,2},{1,3},{2,0},{3,1},{4,6},{5,7},{6,4},{7,5},{8,10},{9,11},{10,... | collective-permute-start | bytes 589832 | tf_op jit(solution)/shard_map/ppermute | solution.py:579
  174.4 14.2 %collective-permute-start.29 = (bf16[128,768]{1,0:T(8,128)(2,1)S(1)}, bf16[128,768]{1,0:T(8,128)(2,1)S(1)}, u32[]{:S(2)}, u32[]{:S(2)}) collective-permute-start(bf16[128,768]{1,0:T(8,128)(2,1)S(1)} %get-tuple-element.141), channel_id=1, source_target_pairs={{0,3},{1,2},{2,1},{3,0},{4,7},{5,6},{6,5},{7,4},{8,11},{9,10},{10,... | collective-permute-start | bytes 589832 | tf_op jit(solution)/shard_map/ppermute | solution.py:579
  176.4 23.1 %collective-permute-start.43 = (bf16[3,96,768]{2,1,0:T(8,128)(2,1)S(1)}, bf16[3,96,768]{2,1,0:T(8,128)(2,1)S(1)}, u32[]{:S(2)}, u32[]{:S(2)}) collective-permute-start(bf16[3,96,768]{2,1,0:T(8,128)(2,1)S(1)} %collective-permute-done.40.refs_2_), channel_id=1, source_target_pairs={{0,1},{1,0},{2,3},{3,2},{4,5},{5,4},{6,7},{7,6},{8,9},{9,8},{10,11... | collective-permute-start | bytes 1327112 | tf_op jit(solution)/shard_map/ppermute | solution.py:579
  182.4 8.7 %collective-permute-start.36 = (bf16[112,768]{1,0:T(8,128)(2,1)S(1)}, bf16[112,768]{1,0:T(8,128)(2,1)S(1)}, u32[]{:S(2)}, u32[]{:S(2)}) collective-permute-start(bf16[112,768]{1,0:T(8,128)(2,1)S(1)} %get-tuple-element.171), channel_id=1, source_target_pairs={{0,8},{4,12},{8,0},{12,4},{16,24},{20,28},{24,16},{28,20},{1,9},{5... | collective-permute-start | bytes 516104 | tf_op jit(solution)/shard_map/ppermute | solution.py:576
  195.1 10.5 %collective-permute-start.42 = (bf16[112,768]{1,0:T(8,128)(2,1)S(1)}, bf16[112,768]{1,0:T(8,128)(2,1)S(1)}, u32[]{:S(2)}, u32[]{:S(2)}) collective-permute-start(bf16[112,768]{1,0:T(8,128)(2,1)S(1)} %plane_sum.1.refs_0_), channel_id=1, source_target_pairs={{0,2},{1,3},{2,0},{3,1},{4,6},{5,7},{6,4},{7,5},{8,10},{9,11},{10,... | collective-permute-start | bytes 516104 | tf_op jit(solution)/shard_map/ppermute | solution.py:579
  (20 other events, 199.4 us)
